TPU v7x, 32 devices: a whole 2x2x4 slice. The times are simulated.
32 devices in a mesh: ctx: 8 (over z, y), head: 4 (over x, core).
Axes of the slice: x: 2, y: 2, z: 4, core: 2. Of those that a mesh axis runs over, the one named last changes fastest.
Arguments:
- queries: bfloat16 [3072, 2048], P('ctx', 'head'), may hold values from -10 to 10, as said below
- key_rows: bfloat16 [3072, 2048], P('ctx', 'head'), may hold values from -10 to 10, as said below
- value_rows: bfloat16 [3072, 2048], P('ctx', 'head'), may hold values from -6 to 6
- out_weight: bfloat16 [2048, 2048], P('head'), may hold values from -0.125 to 0.125
- cotangent: bfloat16 [3072, 2048], P('ctx', 'head'), may hold values from -6 to 6
- offsets: int32 [136], replicated, may hold values from 0 to 25920, as said below
Outputs:
- mixed: bfloat16 [3072, 2048], P('ctx', 'head')
- grad_queries: bfloat16 [3072, 2048], P('ctx', 'head')
- grad_keys: bfloat16 [3072, 2048], P('ctx', 'head')
- grad_values: bfloat16 [3072, 2048], P('ctx', 'head')
Inputs may be any that keep to these rules, and one draw needn't show every extreme that they name: offsets start at 0 and increase; consecutive entries differ by 1 to 192 except before the last entry, which is (135) * 192 and lies beyond the history, as does the entry before it. `queries`: real values. `key_rows`: real values.
All inputs are finite; a program needn't handle non-finite values.
Results may differ from a plain program's by a relative error of at most 0.018.
Values may be sent and summed in bfloat16 or wider, within the bound.
No kernel may reach another device: no remote copies, remote signals or barrier semaphores. Data moves between devices by JAX's collectives and lax.ppermute only.
A program may use at most 64 MiB of HBM per device.

v0:
```python
import functools
import math

import jax
import jax.numpy as jnp
from jax import lax
from jax.experimental import pallas as pl
from jax.experimental.pallas import tpu as pltpu
from jax.sharding import PartitionSpec as P


HD = 128
REACH = 2
PREV = 3
ROWS = 128
NEG_FILL = -1e30
SCALE = 1.0 / math.sqrt(HD)
LOG2E = 1.4426950408889634
VMEM_BYTES = 32 << 20
F32 = jnp.float32
BF16 = jnp.bfloat16


NT = (((1,), (1,)), ((), ()))
NN = (((1,), (0,)), ((), ()))


def passed_along(shard, axis, by):
    length = lax.axis_size(axis)
    pairs = [(i, i + by) for i in range(length) if 0 <= i + by < length]
    return lax.ppermute(shard, axis, pairs)


def swapped(shard, axis, bit):
    length = lax.axis_size(axis)
    return lax.ppermute(shard, axis, [(i, i ^ bit) for i in range(length)])


def windows_kernel(base_ref, offsets_ref, col_ref, row_ref):
    tiles, rows = row_ref.shape
    lines = tiles * rows // HD
    place = HD * lax.broadcasted_iota(jnp.int32, (lines, HD), 0) + lax.broadcasted_iota(
        jnp.int32, (lines, HD), 1
    )
    position = base_ref[0] + place

    def step(m, first):
        return jnp.where(offsets_ref[m + PREV] <= position, offsets_ref[m], first)

    first = lax.fori_loop(
        0, offsets_ref.shape[0] - PREV, step, jnp.zeros_like(position), unroll=4
    )
    first = jnp.where(position < base_ref[1], first - base_ref[0], tiles * rows)
    for line in range(lines):
        tile, start = divmod(line * HD, rows)
        row_ref[tile : tile + 1, start : start + HD] = first[line : line + 1, :]
        if tile == 0:
            spread = jnp.broadcast_to(first[line : line + 1, :], (HD, HD))
            col_ref[start : start + HD, :] = spread.T


def windows_call(base, offsets, rows):
    return pl.pallas_call(
        windows_kernel,
        name="windows",
        out_shape=(
            jax.ShapeDtypeStruct((rows, HD), jnp.int32),
            jax.ShapeDtypeStruct((REACH + 1, rows), jnp.int32),
        ),
        in_specs=[pl.BlockSpec(memory_space=pltpu.SMEM)] * 2,
        compiler_params=pltpu.CompilerParams(vmem_limit_bytes=VMEM_BYTES),
        cost_estimate=pl.CostEstimate(flops=1 << 20, bytes_accessed=1 << 18, transcendentals=0),
    )(base, offsets)


def in_hbm(*arrays):
    return [pltpu.with_memory_space_constraint(x, pltpu.HBM) for x in arrays]


def in_vmem(*arrays):
    return [pltpu.with_memory_space_constraint(x, pltpu.VMEM) for x in arrays]


def mm(a, b, dims):
    return lax.dot_general(a, b, dims, preferred_element_type=F32)


def grad_out_kernel(me_ref, c0, c1, c2, c3, w_ref, out_ref):
    cols = c0.shape[1]
    total = None
    for s, c in enumerate((c0, c1, c2, c3)):
        start = pl.multiple_of((me_ref[0] ^ s) * cols, cols)
        part = mm(c[...], w_ref[:, pl.ds(start, cols)], NT)
        total = part if total is None else total + part
    out_ref[...] = total.astype(BF16)


def grad_out_call(me, shards, weight):
    rows, cols = shards[0].shape
    whole = pl.BlockSpec((rows, cols), lambda h, me: (0, 0))
    return pl.pallas_call(
        grad_out_kernel,
        name="grad_out",
        out_shape=jax.ShapeDtypeStruct((rows, cols), BF16),
        grid_spec=pltpu.PrefetchScalarGridSpec(
            num_scalar_prefetch=1,
            grid=(cols // (2 * HD),),
            in_specs=[whole] * 4
            + [pl.BlockSpec((2 * HD, weight.shape[1]), lambda h, me: (h, 0))],
            out_specs=pl.BlockSpec((rows, 2 * HD), lambda h, me: (0, h)),
        ),
        compiler_params=pltpu.CompilerParams(vmem_limit_bytes=VMEM_BYTES),
        cost_estimate=pl.CostEstimate(
            flops=2 * rows * cols * weight.shape[1], bytes_accessed=6 << 20, transcendentals=0
        ),
    )(me, *in_hbm(shards[0]), *in_vmem(*shards[1:]), *in_hbm(weight))


def key_pieces(block, rows):
    first, last = block * ROWS, (block + 1) * ROWS
    return ((2, first, rows, -2 * rows), (1, 0, rows, -rows), (0, 0, last, 0))


def pick(odd, even_ref, odd_ref, into):
    into[...] = jnp.where(odd == 0, even_ref[...], odd_ref[...])


def attend_kernel(
    odd_ref, me_ref, lo_ref, q, k0, k2, v0, v2, r1, r2, r3, g, w_ref,
    att_ref, prob_ref, stat_ref, sent_ref, mine_ref, far_ref, k1, v1,
):
    rows = q.shape[0]
    head = pl.program_id(0)
    pick(odd_ref[0], r2, r1, k1)
    pick(odd_ref[0], r3, r2, v1)
    keys, values = (k0, k1, k2), (v0, v1, v2)
    for b in range(rows // ROWS):
        mine = slice(b * ROWS, (b + 1) * ROWS)
        qb = q[mine, :]
        lo = lo_ref[mine, :]
        scores, places = [], []
        for tile, first, last, off in key_pieces(b, rows):
            raw = mm(qb, keys[tile][first:last, :], NT)
            for c in range(0, last - first, HD):
                part = raw[:, c : c + HD]
                pos = off + first + c + lax.broadcasted_iota(jnp.int32, part.shape, 1)
                ok = pos >= lo
                if tile == 0 and first + c == b * ROWS:
                    ok &= pos <= b * ROWS + lax.broadcasted_iota(jnp.int32, part.shape, 0)
                scores.append(jnp.where(ok, part, NEG_FILL))
                places.append(tile * rows + first + c)
        top = jnp.max(functools.reduce(jnp.maximum, scores), axis=1, keepdims=True)
        shift = jnp.broadcast_to(top * (SCALE * LOG2E), (ROWS, HD))
        exps = [jnp.exp2(s * (SCALE * LOG2E) - shift) for s in scores]
        total = jnp.sum(functools.reduce(jnp.add, exps), axis=1, keepdims=True)
        inverse = jnp.broadcast_to(1.0 / total, (ROWS, HD))
        mixed = None
        for e, place in zip(exps, places):
            prob_ref[0, mine, place : place + HD] = (e * inverse).astype(BF16)
        for tile, first, last, off in key_pieces(b, rows):
            prob = prob_ref[0, mine, tile * rows + first : tile * rows + last]
            part = mm(prob, values[tile][first:last, :], NN)
            mixed = part if mixed is None else mixed + part
        attended = mixed.astype(BF16)
        att_ref[mine, pl.ds(pl.multiple_of(head * HD, HD), HD)] = attended
        delta = jnp.sum(attended.astype(F32) * g[mine, :].astype(F32), axis=1, keepdims=True)
        log_total = shift + jnp.log2(total)
        lane = lax.broadcasted_iota(jnp.int32, (ROWS, ROWS), 1)
        stats = jnp.where(lane == 0, log_total, delta).T
        stat_ref[0, :, mine] = stats[0:2, :]

    @pl.when(head == pl.num_programs(0) - 1)
    def _():
        cols = att_ref.shape[1]

        def project(group):
            start = pl.multiple_of((me_ref[0] ^ group) * cols, cols)
            return mm(att_ref[...], w_ref[:, pl.ds(start, cols)], NN)

        sent_ref[:, 0:cols] = project(1).astype(BF16)
        sent_ref[:, cols : 2 * cols] = project(3).astype(BF16)
        far_ref[...] = project(2)
        mine_ref[...] = project(0)


def tile_specs(rows):
    tile = pl.BlockSpec((rows, HD), lambda h, odd, *_: (0, h))
    on_odd = pl.BlockSpec((rows, HD), lambda h, odd, *_: (0, h * odd[0]))
    on_even = pl.BlockSpec((rows, HD), lambda h, odd, *_: (0, h * (1 - odd[0])))
    return tile, on_odd, on_even


def attend_call(odd, me, lo, q, k0, k2, v0, v2, r1, r2, r3, g, weight):
    rows, cols = q.shape
    heads = cols // HD
    tile, on_odd, on_even = tile_specs(rows)
    span = REACH * rows + ROWS
    whole = pl.BlockSpec((rows, cols), lambda h, odd, me: (0, 0))
    return pl.pallas_call(
        attend_kernel,
        name="attend",
        out_shape=(
            jax.ShapeDtypeStruct((rows, cols), BF16),
            jax.ShapeDtypeStruct((heads, rows, (REACH + 1) * rows), BF16),
            jax.ShapeDtypeStruct((heads, 2, rows), F32),
            jax.ShapeDtypeStruct((rows, 2 * cols), BF16),
            jax.ShapeDtypeStruct((rows, cols), F32),
            jax.ShapeDtypeStruct((rows, cols), F32),
        ),
        grid_spec=pltpu.PrefetchScalarGridSpec(
            num_scalar_prefetch=2,
            grid=(heads,),
            in_specs=[pl.BlockSpec((rows, HD), lambda h, odd, me: (0, 0))]
            + [tile] * 5
            + [on_odd, tile, on_even, tile]
            + [pl.BlockSpec(weight.shape, lambda h, odd, me: (0, 0))],
            out_specs=(
                whole,
                pl.BlockSpec((1, rows, (REACH + 1) * rows), lambda h, odd, me: (h, 0, 0)),
                pl.BlockSpec((1, 2, rows), lambda h, odd, me: (h, 0, 0)),
                pl.BlockSpec((rows, 2 * cols), lambda h, odd, me: (0, 0)),
                whole,
                whole,
            ),
            scratch_shapes=[pltpu.VMEM((rows, HD), BF16)] * 2,
        ),
        compiler_params=pltpu.CompilerParams(vmem_limit_bytes=VMEM_BYTES),
        cost_estimate=pl.CostEstimate(
            flops=8 * heads * rows * span * HD, bytes_accessed=12 << 20,
            transcendentals=heads * rows * span,
        ),
    )(odd, me, lo, *in_hbm(q, k0), *in_vmem(k2), *in_hbm(v0), *in_vmem(v2, r1, r2, r3, g), *in_hbm(weight))


def grads_kernel(
    odd_ref, me_ref, lo_ref, prob_ref, att, k0, k2, v0, v2, q0, q2, r1, r2, r3, g0, g1, g2,
    s0, s10, s11, s20, s21, dq_ref, dk_ref, dv_ref,
    kc, qc, gc, v1, s1, s2, probs, grad_s, grad_q,
):
    rows = g0.shape[0]
    blocks = range(0, rows, ROWS)

    @pl.when(pl.program_id(0) == 0)
    def _():
        nothing = jnp.zeros((ROWS, ROWS), BF16)
        for early in blocks:
            for late in range(early + ROWS, rows, ROWS):
                far = 2 * rows
                for into in (probs, grad_s):
                    into[late : late + ROWS, early : early + ROWS] = nothing
                    into[early : early + ROWS, far + late : far + late + ROWS] = nothing
                grad_q[early : early + ROWS, late : late + ROWS] = nothing
                grad_q[late : late + ROWS, far + early : far + early + ROWS] = nothing

    odd, group = odd_ref[0], me_ref[0] & 1
    tiles = [slice(t * rows, (t + 1) * rows) for t in range(REACH + 1)]
    pick(odd, r2, r1, kc.at[tiles[1], :])
    pick(odd, r3, r2, v1)
    pick(odd, r1, r3, qc.at[tiles[1], :])
    pick(group, s10, s11, s1)
    pick(group, s20, s21, s2)
    for into, t, ref in (
        (kc, 0, k0), (kc, 2, k2), (qc, 0, q0), (qc, 2, q2), (gc, 0, g0), (gc, 1, g1), (gc, 2, g2)
    ):
        into[tiles[t], :] = ref[...]
    values, stats = (v0, v1, v2), (s0, s1, s2)

    for t in (0, 2, 1):
        for c in blocks:
            first, last = {0: (0, c + ROWS), 1: (0, rows), 2: (c, rows)}[t]
            at = t * rows + c
            asked = qc[at : at + ROWS, :]
            grad = gc[at : at + ROWS, :]
            raw = mm(k0[first:last, :], asked, NT)
            grad_prob = mm(values[0][first:last, :], grad, NT)
            lo = lo_ref[t : t + 1, c : c + ROWS]
            log_total = stats[t][0, 0:1, c : c + ROWS]
            delta = stats[t][0, 1:2, c : c + ROWS]
            for r in range(first, last, ROWS):
                here = slice(r - first, r - first + ROWS)
                part = raw[here, :]
                pos = r + lax.broadcasted_iota(jnp.int32, part.shape, 0)
                ok = pos >= lo
                if t == 0 and r == c:
                    ok &= pos <= c + lax.broadcasted_iota(jnp.int32, part.shape, 1)
                prob = jnp.where(ok, jnp.exp2(part * (SCALE * LOG2E) - log_total), 0.0)
                probs[r : r + ROWS, at : at + ROWS] = prob.astype(BF16)
                grad_s[r : r + ROWS, at : at + ROWS] = (
                    prob * (grad_prob[here, :] - delta)
                ).astype(BF16)
    dk_ref[...] = (mm(grad_s[...], qc[...], NN) * SCALE).astype(BF16)
    dv_ref[...] = mm(probs[...], gc[...], NN).astype(BF16)

    product = att[...].astype(F32) * g0[...].astype(F32)
    delta = jnp.broadcast_to(jnp.sum(product, axis=1, keepdims=True), (rows, HD))
    for t in (0, 2, 1):
        for c in blocks:
            first, last = {0: (c, rows), 1: (0, rows), 2: (0, c + ROWS)}[t]
            at = t * rows + c
            grad_prob = mm(g0[first:last, :], values[t][c : c + ROWS, :], NT)
            prob = prob_ref[0, first:last, at : at + ROWS].astype(F32)
            grad_q[first:last, at : at + ROWS] = (
                prob * (grad_prob - delta[first:last, :])
            ).astype(BF16)
    dq_ref[...] = (mm(grad_q[...], kc[...], NN) * SCALE).astype(BF16)


def grads_call(odd, me, lo, prob, att, k, v, q, received, grads, stats):
    rows, cols = q[0].shape
    heads = cols // HD
    tile, _, _ = tile_specs(rows)
    span = (REACH + 1) * rows
    stat = pl.BlockSpec((1, 2, rows), lambda h, odd, me: (h, 0, 0))
    hbm = in_hbm(k[0], v[0], q[0])
    vmem = in_vmem(k[1], v[1], q[1], *received, *grads)
    return pl.pallas_call(
        grads_kernel,
        name="grads",
        out_shape=(jax.ShapeDtypeStruct((rows, cols), BF16),) * 3,
        grid_spec=pltpu.PrefetchScalarGridSpec(
            num_scalar_prefetch=2,
            grid=(heads,),
            in_specs=[
                pl.BlockSpec((REACH + 1, rows), lambda h, odd, me: (0, 0)),
                pl.BlockSpec((1, rows, span), lambda h, odd, me: (h, 0, 0)),
            ]
            + [tile] * 13
            + [stat] * 5,
            out_specs=(tile,) * 3,
            scratch_shapes=[pltpu.VMEM((span, HD), BF16)] * 3
            + [pltpu.VMEM((rows, HD), BF16)]
            + [pltpu.VMEM((1, 2, rows), F32)] * 2
            + [pltpu.VMEM((rows, span), BF16)] * 3,
        ),
        compiler_params=pltpu.CompilerParams(vmem_limit_bytes=VMEM_BYTES),
        cost_estimate=pl.CostEstimate(
            flops=12 * heads * rows * span * HD, bytes_accessed=10 << 20,
            transcendentals=heads * rows * span,
        ),
    )(
        odd, me, lo, prob, att, hbm[0], vmem[0], hbm[1], vmem[1], hbm[2], vmem[2], *vmem[3:], *stats
    )


def layer(queries, key_rows, value_rows, out_weight, cotangent, offsets):
    rows, cols = queries.shape
    count = lax.axis_size("ctx")
    index = lax.axis_index("ctx")
    base = index * rows
    odd = (index % 2).astype(jnp.int32).reshape(1)
    me = lax.axis_index("head").astype(jnp.int32).reshape(1)

    def along(shard, by):
        return passed_along(shard, "ctx", by)

    def across(shard, bit):
        return swapped(shard, "head", bit)

    def pair(from_even, from_odd):
        return swapped(jnp.where(index % 2 == 0, from_even, from_odd), "ctx", 1)

    def ringed(shard, by, bit):
        groups = lax.axis_size("head")
        pairs = []
        for i in range(count):
            for h in range(groups):
                to = i - by if (h & 1) == bit else i + by
                here = i * groups + h
                pairs.append((here, to * groups + h if 0 <= to < count else here ^ 1))
        return lax.ppermute(shard, ("ctx", "head"), pairs)

    cot_far = across(cotangent, 2)
    cot_near = across(cotangent, 1)
    k2 = along(key_rows, 2)
    r1 = pair(key_rows, queries)
    v2 = along(value_rows, 2)
    cot_both = across(cot_far, 1)
    q2 = along(queries, -2)
    r2 = pair(value_rows, k2)

    g = grad_out_call(me, (cotangent, cot_near, cot_far, cot_both), out_weight)
    g2 = along(g, -2)
    bounds = jnp.stack([base, count * rows]).astype(jnp.int32)
    lo_col, lo_row = windows_call(bounds, offsets, rows)
    r3 = pair(q2, v2)
    g1 = pair(g2, g)

    attended, prob, stat, sent, kept, kept_far = attend_call(
        odd, me, lo_col, queries, key_rows, k2, value_rows, v2, r1, r2, r3, g, out_weight
    )
    stats = [stat] + [ringed(stat, n, bit) for n in (1, 2) for bit in (0, 1)]
    came = across(sent, 1)
    far = across((kept_far + came[:, cols:].astype(F32)).astype(BF16), 2)

    grad_queries, grad_keys, grad_values = grads_call(
        odd, me, lo_row, prob, attended, (key_rows, k2), (value_rows, v2), (queries, q2),
        (r1, r2, r3), (g, g1, g2), stats,
    )
    mixed = (kept + came[:, :cols].astype(F32) + far.astype(F32)).astype(BF16)
    return (mixed, grad_queries, grad_keys, grad_values)


def solution(mesh):
    in_specs = (
        P("ctx", "head"),
        P("ctx", "head"),
        P("ctx", "head"),
        P("head", None),
        P("ctx", "head"),
        P(),
    )
    out_specs = (P("ctx", "head"), P("ctx", "head"), P("ctx", "head"), P("ctx", "head"))
    return jax.shard_map(layer, mesh=mesh, in_specs=in_specs, out_specs=out_specs, check_vma=False)
```

profile of v0, /device:TPU:0, one launch (start us, length us, event | category | flops | bytes accessed | tf_op | source)
XLA Modules:
  0.0 91.4 jit_solution(4788812622738842689)
XLA Ops:
  0.6 5.0 %collective-permute-start = (bf16[384,512]{1,0:T(8,128)(2,1)}, bf16[384,512]{1,0:T(8,128)(2,1)S(1)}, u32[]{:S(2)}, u32[]{:S(2)}) collective-permute-start(bf16[384,512]{1,0:T(8,128)(2,1)} %k0.3), channel_id=1, source_target_pairs={{0,8},{4,12},{8,16},{12,20},{16,24},{20,28},{1,9},{5,13},{9,17},{1... | collective-permute-start | bytes 1179656 | tf_op jit(solution)/shard_map/ppermute | solution.py:31
  5.6 0.1 collective-permute-start.6
  5.7 1.6 %collective-permute-start.7 = (bf16[384,512]{1,0:T(8,128)(2,1)}, bf16[384,512]{1,0:T(8,128)(2,1)S(1)}, u32[]{:S(2)}, u32[]{:S(2)}) collective-permute-start(bf16[384,512]{1,0:T(8,128)(2,1)} %c0.1), channel_id=1, source_target_pairs={{0,2},{1,3},{2,0},{3,1},{4,6},{5,7},{6,4},{7,5},{8,10},{9,11},{10,... | collective-permute-start | bytes 1179656 | tf_op jit(solution)/shard_map/ppermute | solution.py:36
  7.3 3.5 %collective-permute-start.1 = (bf16[384,512]{1,0:T(8,128)(2,1)}, bf16[384,512]{1,0:T(8,128)(2,1)S(1)}, u32[]{:S(2)}, u32[]{:S(2)}) collective-permute-start(bf16[384,512]{1,0:T(8,128)(2,1)} %v0.3), channel_id=1, source_target_pairs={{0,8},{4,12},{8,16},{12,20},{16,24},{20,28},{1,9},{5,13},{9,17},{1... | collective-permute-start | bytes 1179656 | tf_op jit(solution)/shard_map/ppermute | solution.py:31
  10.8 1.3 %collective-permute-start.4 = (bf16[384,512]{1,0:T(8,128)(2,1)}, bf16[384,512]{1,0:T(8,128)(2,1)S(1)}, u32[]{:S(2)}, u32[]{:S(2)}) collective-permute-start(bf16[384,512]{1,0:T(8,128)(2,1)} %q0.1), channel_id=1, source_target_pairs={{8,0},{12,4},{16,8},{20,12},{24,16},{28,20},{9,1},{13,5},{17,9},{2... | collective-permute-start | bytes 1179656 | tf_op jit(solution)/shard_map/ppermute | solution.py:31
  12.1 1.8 %broadcast_select_fusion.3 = bf16[384,512]{1,0:T(8,128)(2,1)} fusion(bf16[384,512]{1,0:T(8,128)(2,1)} %k0.3, bf16[384,512]{1,0:T(8,128)(2,1)} %q0.1, pred[]{:T(512)S(6)} %eq.12), kind=kLoop, calls=%fused_computation.5 | loop fusion | flops 196608 | bytes 1179649 | tf_op jit(solution)/shard_map/jit(_where)/select_n | solution.py:360
  13.9 1.5 %collective-permute-done.k2 = bf16[384,512]{1,0:T(8,128)(2,1)S(1)} collective-permute-done((bf16[384,512]{1,0:T(8,128)(2,1)}, bf16[384,512]{1,0:T(8,128)(2,1)S(1)}, u32[]{:S(2)}, u32[]{:S(2)}) %collective-permute-start) | collective-permute-done | bytes 393248 | tf_op jit(solution)/shard_map/ppermute | solution.py:31
  15.4 1.5 %collective-permute-start.2 = (bf16[384,512]{1,0:T(8,128)(2,1)}, bf16[384,512]{1,0:T(8,128)(2,1)S(1)}, u32[]{:S(2)}, u32[]{:S(2)}) collective-permute-start(bf16[384,512]{1,0:T(8,128)(2,1)} %broadcast_select_fusion.3), channel_id=1, source_target_pairs={{0,4},{4,0},{8,12},{12,8},{16,20},{20,16},{24,28},{28,24},{1,5},{5... | collective-permute-start | bytes 1179656 | tf_op jit(solution)/shard_map/ppermute | solution.py:36
  16.9 1.8 %broadcast_select_fusion.2 = bf16[384,512]{1,0:T(8,128)(2,1)} fusion(bf16[384,512]{1,0:T(8,128)(2,1)} %v0.3, bf16[384,512]{1,0:T(8,128)(2,1)S(1)} %collective-permute-done.k2, pred[]{:T(512)S(6)} %eq.12), kind=kLoop, calls=%fused_computation.4 | loop fusion | flops 196608 | bytes 1179649 | tf_op jit(solution)/shard_map/jit(_where)/select_n | solution.py:360
  18.7 4.0 %collective-permute-done.1.v2 = bf16[384,512]{1,0:T(8,128)(2,1)S(1)} collective-permute-done((bf16[384,512]{1,0:T(8,128)(2,1)}, bf16[384,512]{1,0:T(8,128)(2,1)S(1)}, u32[]{:S(2)}, u32[]{:S(2)}) %collective-permute-start.1) | collective-permute-done | bytes 393248 | tf_op jit(solution)/shard_map/ppermute | solution.py:31
  22.7 1.5 %collective-permute-start.3 = (bf16[384,512]{1,0:T(8,128)(2,1)}, bf16[384,512]{1,0:T(8,128)(2,1)S(1)}, u32[]{:S(2)}, u32[]{:S(2)}) collective-permute-start(bf16[384,512]{1,0:T(8,128)(2,1)} %broadcast_select_fusion.2), channel_id=1, source_target_pairs={{0,4},{4,0},{8,12},{12,8},{16,20},{20,16},{24,28},{28,24},{1,5},{5... | collective-permute-start | bytes 1179656 | tf_op jit(solution)/shard_map/ppermute | solution.py:36
  24.2 0.8 broadcast_select_fusion.1
  25.0 1.0 %collective-permute-start.5 = (bf16[384,512]{1,0:T(8,128)(2,1)}, bf16[384,512]{1,0:T(8,128)(2,1)S(1)}, u32[]{:S(2)}, u32[]{:S(2)}) collective-permute-start(bf16[384,512]{1,0:T(8,128)(2,1)} %broadcast_select_fusion.1), channel_id=1, source_target_pairs={{0,4},{4,0},{8,12},{12,8},{16,20},{20,16},{24,28},{28,24},{1,5},{5... | collective-permute-start | bytes 1179656 | tf_op jit(solution)/shard_map/ppermute | solution.py:36
  26.1 0.1 pad_add_fusion.base_ref
  26.1 1.0 %windows.1 = (s32[384,128]{1,0:T(8,128)S(1)}, s32[3,384]{1,0:T(4,128)S(1)}) custom-call(s32[2]{0:T(128)S(1)} %pad_add_fusion.base_ref, s32[136]{0:T(256)S(1)} %copy-done), custom_call_target="tpu_custom_call" | custom-call | flops 1048576 | bytes 262144 | tf_op jit(solution)/shard_map/windows/pallas_call | solution.py:63
  27.2 2.6 %grad_out.1.g.g0 = bf16[384,512]{1,0:T(8,128)(2,1)S(1)} custom-call(s32[1]{0:T(128)} %bitcast.1.me_ref, bf16[384,512]{1,0:T(8,128)(2,1)} %c0.1, bf16[384,512]{1,0:T(8,128)(2,1)S(1)} %collective-permute-done.6.c1, bf16[384,512]{1,0:T(8,128)(2,1)S(1)} %collective-permute-done.7.c2, bf16[384,512]{1,0:T(8,128)(2,1)S(1)} %collective-permute-done.8.c3, ...), custom_call_target="tpu_custom_call" | custom-call | flops 805306368 | bytes 6291456 | tf_op jit(solution)/shard_map/grad_out/pallas_call | solution.py:101
  29.8 5.1 %collective-permute-done.3.r2 = bf16[384,512]{1,0:T(8,128)(2,1)S(1)} collective-permute-done((bf16[384,512]{1,0:T(8,128)(2,1)}, bf16[384,512]{1,0:T(8,128)(2,1)S(1)}, u32[]{:S(2)}, u32[]{:S(2)}) %collective-permute-start.3) | collective-permute-done | bytes 393248 | tf_op jit(solution)/shard_map/ppermute | solution.py:36
  34.9 6.9 %collective-permute-done.5.r3 = bf16[384,512]{1,0:T(8,128)(2,1)S(1)} collective-permute-done((bf16[384,512]{1,0:T(8,128)(2,1)}, bf16[384,512]{1,0:T(8,128)(2,1)S(1)}, u32[]{:S(2)}, u32[]{:S(2)}) %collective-permute-start.5) | collective-permute-done | bytes 393248 | tf_op jit(solution)/shard_map/ppermute | solution.py:36
  41.8 10.1 %attend.1 = (bf16[384,512]{1,0:T(8,128)(2,1)S(1)}, bf16[4,384,1152]{2,1,0:T(8,128)(2,1)S(1)}, f32[4,2,384]{2,1,0:T(2,128)S(1)}, bf16[384,1024]{1,0:T(8,128)(2,1)...) custom-call(s32[1]{0:T(128)} %bitcast.odd_ref, s32[1]{0:T(128)} %bitcast.1.me_ref, ...), custom_call_target="tpu_custom_call" | custom-call | flops 1409286144 | bytes 12582912 | tf_op jit(solution)/shard_map/attend/pallas_call | solution.py:199
  52.0 0.1 collective-permute-start.9
  52.0 1.3 %collective-permute-start.11 = (bf16[384,512]{1,0:T(8,128)(2,1)S(1)}, bf16[384,512]{1,0:T(8,128)(2,1)S(1)}, u32[]{:S(2)}, u32[]{:S(2)}) collective-permute-start(bf16[384,512]{1,0:T(8,128)(2,1)S(1)} %grad_out.1.g.g0), channel_id=1, source_target_pairs={{8,0},{12,4},{16,8},{20,12},{24,16},{28,20},{9,1},{13,5},{17,9},{2... | collective-permute-start | bytes 1179656 | tf_op jit(solution)/shard_map/ppermute | solution.py:31
  53.3 12.7 %collective-permute-done.11.g2 = bf16[384,512]{1,0:T(8,128)(2,1)S(1)} collective-permute-done((bf16[384,512]{1,0:T(8,128)(2,1)S(1)}, bf16[384,512]{1,0:T(8,128)(2,1)S(1)}, u32[]{:S(2)}, u32[]{:S(2)}) %collective-permute-start.11) | collective-permute-done | bytes 393248 | tf_op jit(solution)/shard_map/ppermute | solution.py:31
  66.1 0.1 broadcast_select_fusion
  66.1 1.6 %collective-permute-start.12 = (bf16[384,512]{1,0:T(8,128)(2,1)S(1)}, bf16[384,512]{1,0:T(8,128)(2,1)S(1)}, u32[]{:S(2)}, u32[]{:S(2)}) collective-permute-start(bf16[384,512]{1,0:T(8,128)(2,1)S(1)} %broadcast_select_fusion), channel_id=1, source_target_pairs={{0,4},{4,0},{8,12},{12,8},{16,20},{20,16},{24,28},{28,24},{1,5},{5... | collective-permute-start | bytes 1179656 | tf_op jit(solution)/shard_map/ppermute | solution.py:36
  67.7 0.2 add_convert_fusion.1
  67.9 1.1 %collective-permute-start.10 = (bf16[384,512]{1,0:T(8,128)(2,1)S(1)}, bf16[384,512]{1,0:T(8,128)(2,1)S(1)}, u32[]{:S(2)}, u32[]{:S(2)}) collective-permute-start(bf16[384,512]{1,0:T(8,128)(2,1)S(1)} %add_convert_fusion.1), channel_id=1, source_target_pairs={{0,2},{1,3},{2,0},{3,1},{4,6},{5,7},{6,4},{7,5},{8,10},{9,11},{10,... | collective-permute-start | bytes 1179656 | tf_op jit(solution)/shard_map/ppermute | solution.py:36
  69.0 2.0 %collective-permute-start.14 = (f32[4,2,384]{2,1,0:T(2,128)S(1)}, f32[4,2,384]{2,1,0:T(2,128)S(1)}, u32[]{:S(2)}, u32[]{:S(2)}) collective-permute-start(f32[4,2,384]{2,1,0:T(2,128)S(1)} %get-tuple-element.22.s0), channel_id=1, source_target_pairs={{0,4},{1,0},{2,6},{3,2},{4,8},{5,1},{6,10},{7,3},{8,12},{9,5},{10,... | collective-permute-start | bytes 36872 | tf_op jit(solution)/shard_map/ppermute | solution.py:370
  71.0 6.4 %collective-permute-done.13.s10 = f32[4,2,384]{2,1,0:T(2,128)S(1)} collective-permute-done((f32[4,2,384]{2,1,0:T(2,128)S(1)}, f32[4,2,384]{2,1,0:T(2,128)S(1)}, u32[]{:S(2)}, u32[]{:S(2)}) %collective-permute-start.13) | collective-permute-done | bytes 12320 | tf_op jit(solution)/shard_map/ppermute | solution.py:370
  77.4 1.7 %collective-permute-start.16 = (f32[4,2,384]{2,1,0:T(2,128)S(1)}, f32[4,2,384]{2,1,0:T(2,128)S(1)}, u32[]{:S(2)}, u32[]{:S(2)}) collective-permute-start(f32[4,2,384]{2,1,0:T(2,128)S(1)} %get-tuple-element.22.s0), channel_id=1, source_target_pairs={{0,8},{1,0},{2,10},{3,2},{4,12},{5,4},{6,14},{7,6},{8,16},{9,1},{1... | collective-permute-start | bytes 36872 | tf_op jit(solution)/shard_map/ppermute | solution.py:370
  79.1 1.4 %collective-permute-done.16.s21 = f32[4,2,384]{2,1,0:T(2,128)S(1)} collective-permute-done((f32[4,2,384]{2,1,0:T(2,128)S(1)}, f32[4,2,384]{2,1,0:T(2,128)S(1)}, u32[]{:S(2)}, u32[]{:S(2)}) %collective-permute-start.16) | collective-permute-done | bytes 12320 | tf_op jit(solution)/shard_map/ppermute | solution.py:370
  80.5 9.9 %grads.1 = (bf16[384,512]{1,0:T(8,128)(2,1)}, bf16[384,512]{1,0:T(8,128)(2,1)}, bf16[384,512]{1,0:T(8,128)(2,1)}) custom-call(s32[1]{0:T(128)} %bitcast.odd_ref, s32[1]{0:T(128)} %bitcast.1.me_ref, s32[3,384]{1,0:T(4,128)S(1)} %get-tuple-element.19.lo_ref, bf16[4,384,1152]{2,1,0:T(8,128)(2,1)S(1)} %get-tuple-element.20.prob_ref, ...), custom_call_target="tpu_custom_call" | custom-call | flops 2717908992 | bytes 10485760 | tf_op jit(solution)/shard_map/grads/pallas_call | solution.py:316
  90.4 1.0 %add_convert_fusion = bf16[384,512]{1,0:T(8,128)(2,1)} fusion(bf16[384,512]{1,0:T(8,128)(2,1)S(1)} %collective-permute-done.10, f32[384,512]{1,0:T(8,128)S(1)} %get-tuple-element.16, bf16[384,1024]{1,0:T(8,128)(2,1)S(1)} %collective-permute-done.9), kind=kLoop, calls=%fused_computation | loop fusion | flops 983040 | bytes 1966080 | tf_op jit(solution)/shard_map/convert_element_type | solution.py:399
  (15 shorter events, 0.0 us)
Async XLA Ops:
  0.6 25.5 %copy-start = (s32[136]{0:T(256)S(1)}, s32[136]{0:T(256)}, u32[]{:S(2)}) copy-start(s32[136]{0:T(256)} %offsets_ref.1) | copy-start | bytes 1636
  0.6 14.8 %collective-permute-start = (bf16[384,512]{1,0:T(8,128)(2,1)}, bf16[384,512]{1,0:T(8,128)(2,1)S(1)}, u32[]{:S(2)}, u32[]{:S(2)}) collective-permute-start(bf16[384,512]{1,0:T(8,128)(2,1)} %k0.3), channel_id=1, source_target_pairs={{0,8},{4,12},{8,16},{12,20},{16,24},{20,28},{1,9},{5,13},{9,17},{1... | collective-permute-start | bytes 1179656 | tf_op jit(solution)/shard_map/ppermute | solution.py:31
  5.6 21.5 %collective-permute-start.6 = (bf16[384,512]{1,0:T(8,128)(2,1)}, bf16[384,512]{1,0:T(8,128)(2,1)S(1)}, u32[]{:S(2)}, u32[]{:S(2)}) collective-permute-start(bf16[384,512]{1,0:T(8,128)(2,1)} %c0.1), channel_id=1, source_target_pairs={{0,1},{1,0},{2,3},{3,2},{4,5},{5,4},{6,7},{7,6},{8,9},{9,8},{10,11... | collective-permute-start | bytes 1179656 | tf_op jit(solution)/shard_map/ppermute | solution.py:36
  5.7 18.5 %collective-permute-start.7 = (bf16[384,512]{1,0:T(8,128)(2,1)}, bf16[384,512]{1,0:T(8,128)(2,1)S(1)}, u32[]{:S(2)}, u32[]{:S(2)}) collective-permute-start(bf16[384,512]{1,0:T(8,128)(2,1)} %c0.1), channel_id=1, source_target_pairs={{0,2},{1,3},{2,0},{3,1},{4,6},{5,7},{6,4},{7,5},{8,10},{9,11},{10,... | collective-permute-start | bytes 1179656 | tf_op jit(solution)/shard_map/ppermute | solution.py:36
  7.3 15.4 %collective-permute-start.1 = (bf16[384,512]{1,0:T(8,128)(2,1)}, bf16[384,512]{1,0:T(8,128)(2,1)S(1)}, u32[]{:S(2)}, u32[]{:S(2)}) collective-permute-start(bf16[384,512]{1,0:T(8,128)(2,1)} %v0.3), channel_id=1, source_target_pairs={{0,8},{4,12},{8,16},{12,20},{16,24},{20,28},{1,9},{5,13},{9,17},{1... | collective-permute-start | bytes 1179656 | tf_op jit(solution)/shard_map/ppermute | solution.py:31
  10.8 13.5 %collective-permute-start.4 = (bf16[384,512]{1,0:T(8,128)(2,1)}, bf16[384,512]{1,0:T(8,128)(2,1)S(1)}, u32[]{:S(2)}, u32[]{:S(2)}) collective-permute-start(bf16[384,512]{1,0:T(8,128)(2,1)} %q0.1), channel_id=1, source_target_pairs={{8,0},{12,4},{16,8},{20,12},{24,16},{28,20},{9,1},{13,5},{17,9},{2... | collective-permute-start | bytes 1179656 | tf_op jit(solution)/shard_map/ppermute | solution.py:31
  15.4 14.3 %collective-permute-start.2 = (bf16[384,512]{1,0:T(8,128)(2,1)}, bf16[384,512]{1,0:T(8,128)(2,1)S(1)}, u32[]{:S(2)}, u32[]{:S(2)}) collective-permute-start(bf16[384,512]{1,0:T(8,128)(2,1)} %broadcast_select_fusion.3), channel_id=1, source_target_pairs={{0,4},{4,0},{8,12},{12,8},{16,20},{20,16},{24,28},{28,24},{1,5},{5... | collective-permute-start | bytes 1179656 | tf_op jit(solution)/shard_map/ppermute | solution.py:36
  22.7 12.2 %collective-permute-start.3 = (bf16[384,512]{1,0:T(8,128)(2,1)}, bf16[384,512]{1,0:T(8,128)(2,1)S(1)}, u32[]{:S(2)}, u32[]{:S(2)}) collective-permute-start(bf16[384,512]{1,0:T(8,128)(2,1)} %broadcast_select_fusion.2), channel_id=1, source_target_pairs={{0,4},{4,0},{8,12},{12,8},{16,20},{20,16},{24,28},{28,24},{1,5},{5... | collective-permute-start | bytes 1179656 | tf_op jit(solution)/shard_map/ppermute | solution.py:36
  24.2 2.9 %collective-permute-start.8 = (bf16[384,512]{1,0:T(8,128)(2,1)S(1)}, bf16[384,512]{1,0:T(8,128)(2,1)S(1)}, u32[]{:S(2)}, u32[]{:S(2)}) collective-permute-start(bf16[384,512]{1,0:T(8,128)(2,1)S(1)} %collective-permute-done.7.c2), channel_id=1, source_target_pairs={{0,1},{1,0},{2,3},{3,2},{4,5},{5,4},{6,7},{7,6},{8,9},{9,8},{10,11... | collective-permute-start | bytes 1179656 | tf_op jit(solution)/shard_map/ppermute | solution.py:36
  25.0 16.8 %collective-permute-start.5 = (bf16[384,512]{1,0:T(8,128)(2,1)}, bf16[384,512]{1,0:T(8,128)(2,1)S(1)}, u32[]{:S(2)}, u32[]{:S(2)}) collective-permute-start(bf16[384,512]{1,0:T(8,128)(2,1)} %broadcast_select_fusion.1), channel_id=1, source_target_pairs={{0,4},{4,0},{8,12},{12,8},{16,20},{20,16},{24,28},{28,24},{1,5},{5... | collective-permute-start | bytes 1179656 | tf_op jit(solution)/shard_map/ppermute | solution.py:36
  52.0 15.8 %collective-permute-start.9 = (bf16[384,1024]{1,0:T(8,128)(2,1)S(1)}, bf16[384,1024]{1,0:T(8,128)(2,1)S(1)}, u32[]{:S(2)}, u32[]{:S(2)}) collective-permute-start(bf16[384,1024]{1,0:T(8,128)(2,1)S(1)} %get-tuple-element.17), channel_id=1, source_target_pairs={{0,1},{1,0},{2,3},{3,2},{4,5},{5,4},{6,7},{7,6},{8,9},{9,8},{10,11... | collective-permute-start | bytes 2359304 | tf_op jit(solution)/shard_map/ppermute | solution.py:36
  52.0 14.0 %collective-permute-start.11 = (bf16[384,512]{1,0:T(8,128)(2,1)S(1)}, bf16[384,512]{1,0:T(8,128)(2,1)S(1)}, u32[]{:S(2)}, u32[]{:S(2)}) collective-permute-start(bf16[384,512]{1,0:T(8,128)(2,1)S(1)} %grad_out.1.g.g0), channel_id=1, source_target_pairs={{8,0},{12,4},{16,8},{20,12},{24,16},{28,20},{9,1},{13,5},{17,9},{2... | collective-permute-start | bytes 1179656 | tf_op jit(solution)/shard_map/ppermute | solution.py:31
  66.1 14.4 %collective-permute-start.12 = (bf16[384,512]{1,0:T(8,128)(2,1)S(1)}, bf16[384,512]{1,0:T(8,128)(2,1)S(1)}, u32[]{:S(2)}, u32[]{:S(2)}) collective-permute-start(bf16[384,512]{1,0:T(8,128)(2,1)S(1)} %broadcast_select_fusion), channel_id=1, source_target_pairs={{0,4},{4,0},{8,12},{12,8},{16,20},{20,16},{24,28},{28,24},{1,5},{5... | collective-permute-start | bytes 1179656 | tf_op jit(solution)/shard_map/ppermute | solution.py:36
  67.9 22.5 %collective-permute-start.10 = (bf16[384,512]{1,0:T(8,128)(2,1)S(1)}, bf16[384,512]{1,0:T(8,128)(2,1)S(1)}, u32[]{:S(2)}, u32[]{:S(2)}) collective-permute-start(bf16[384,512]{1,0:T(8,128)(2,1)S(1)} %add_convert_fusion.1), channel_id=1, source_target_pairs={{0,2},{1,3},{2,0},{3,1},{4,6},{5,7},{6,4},{7,5},{8,10},{9,11},{10,... | collective-permute-start | bytes 1179656 | tf_op jit(solution)/shard_map/ppermute | solution.py:36
  69.0 8.4 %collective-permute-start.13 = (f32[4,2,384]{2,1,0:T(2,128)S(1)}, f32[4,2,384]{2,1,0:T(2,128)S(1)}, u32[]{:S(2)}, u32[]{:S(2)}) collective-permute-start(f32[4,2,384]{2,1,0:T(2,128)S(1)} %get-tuple-element.22.s0), channel_id=1, source_target_pairs={{0,1},{1,5},{2,3},{3,7},{4,0},{5,9},{6,2},{7,11},{8,4},{9,13},{10,... | collective-permute-start | bytes 36872 | tf_op jit(solution)/shard_map/ppermute | solution.py:370
  69.0 10.1 %collective-permute-start.14 = (f32[4,2,384]{2,1,0:T(2,128)S(1)}, f32[4,2,384]{2,1,0:T(2,128)S(1)}, u32[]{:S(2)}, u32[]{:S(2)}) collective-permute-start(f32[4,2,384]{2,1,0:T(2,128)S(1)} %get-tuple-element.22.s0), channel_id=1, source_target_pairs={{0,4},{1,0},{2,6},{3,2},{4,8},{5,1},{6,10},{7,3},{8,12},{9,5},{10,... | collective-permute-start | bytes 36872 | tf_op jit(solution)/shard_map/ppermute | solution.py:370
  71.0 8.1 %collective-permute-start.15 = (f32[4,2,384]{2,1,0:T(2,128)S(1)}, f32[4,2,384]{2,1,0:T(2,128)S(1)}, u32[]{:S(2)}, u32[]{:S(2)}) collective-permute-start(f32[4,2,384]{2,1,0:T(2,128)S(1)} %get-tuple-element.22.s0), channel_id=1, source_target_pairs={{0,1},{1,9},{2,3},{3,11},{4,5},{5,13},{6,7},{7,15},{8,0},{9,17},{1... | collective-permute-start | bytes 36872 | tf_op jit(solution)/shard_map/ppermute | solution.py:370
  77.4 3.1 %collective-permute-start.16 = (f32[4,2,384]{2,1,0:T(2,128)S(1)}, f32[4,2,384]{2,1,0:T(2,128)S(1)}, u32[]{:S(2)}, u32[]{:S(2)}) collective-permute-start(f32[4,2,384]{2,1,0:T(2,128)S(1)} %get-tuple-element.22.s0), channel_id=1, source_target_pairs={{0,8},{1,0},{2,10},{3,2},{4,12},{5,4},{6,14},{7,6},{8,16},{9,1},{1... | collective-permute-start | bytes 36872 | tf_op jit(solution)/shard_map/ppermute | solution.py:370
where the time goes:
time: 91.8 us; the launch traced here: 91.4 us
  waiting for transfers between devices  38.1 us (42%)
  Pallas kernels  23.6 us (26%)
  starting transfers between devices  23.2 us (25%)
  other arithmetic  5.6 us (6%)
    ppermute x4, waiting for transfers between devices, passed_along(): return lax.ppermute(shard, axis, pairs)  18.3 us
    ppermute x9, waiting for transfers between devices, swapped(): return lax.ppermute(shard, axis, [(i, i ^ bit) for i in range(length)])  12.1 us
    ppermute x4, starting transfers between devices, passed_along(): return lax.ppermute(shard, axis, pairs)  11 us
    pallas_call x1, Pallas kernels, attend_call(): pl.pallas_call(attend_kernel, name='attend', out_shape=(jax.ShapeDtypeStr...  10.1 us
    pallas_call x1, Pallas kernels, grads_call(): pl.pallas_call(grads_kernel, name='grads', out_shape=(jax.ShapeDtypeStruc...  9.91 us
    ppermute x9, starting transfers between devices, swapped(): return lax.ppermute(shard, axis, [(i, i ^ bit) for i in range(length)])  8.45 us
    ppermute x4, waiting for transfers between devices, ringed(): return lax.ppermute(shard, ('ctx', 'head'), pairs)  7.78 us
    select_n x4, other arithmetic, pair(): return swapped(jnp.where(index % 2 == 0, from_even, from_odd), 'ctx', 1)  4.42 us
  transfers between devices with their start and end apart: 17, of which 7 were waited for; matrix products, arithmetic and copies ran while one was open for 5% of the time, Pallas kernels for 15%

commit v1 on v0

--- a/solution.py
+++ b/solution.py
@@ -83,6 +83,55 @@
 
 def mm(a, b, dims):
     return lax.dot_general(a, b, dims, preferred_element_type=F32)
+
+
+def payload_kernel(table, kinds, staged, odd_ref, me_ref, *refs):
+    sources, outs, sems = refs[:kinds], refs[kinds : kinds + len(table)], refs[-1]
+    seat = 2 * odd_ref[0] + (me_ref[0] & 1)
+    if staged:
+        stage, stage_sems = refs[-3], refs[-2]
+        loads = [
+            pltpu.make_async_copy(ref, stage.at[kind], stage_sems.at[kind])
+            for kind, ref in enumerate(sources)
+        ]
+        for load in loads:
+            load.start()
+        for load in loads:
+            load.wait()
+        sources = [stage.at[kind] for kind in range(kinds)]
+    for n, into in enumerate(outs):
+        for kind in range(kinds):
+            hits = [seat == place for place in range(4) if table[n][place] == kind]
+            if hits:
+
+                @pl.when(functools.reduce(jnp.logical_or, hits))
+                def _():
+                    pltpu.make_async_copy(sources[kind], into, sems.at[n]).start()
+
+    for n, into in enumerate(outs):
+        pltpu.make_async_copy(sources[0], into, sems.at[n]).wait()
+
+
+def payload_call(odd, me, table, *arrays, staged=False):
+    smem, anywhere = pl.BlockSpec(memory_space=pltpu.SMEM), pl.BlockSpec(memory_space=pl.ANY)
+    shape = arrays[0].shape
+    staging = []
+    if staged:
+        staging = [
+            pltpu.VMEM((len(arrays),) + shape, BF16), pltpu.SemaphoreType.DMA((len(arrays),))
+        ]
+    return pl.pallas_call(
+        functools.partial(payload_kernel, table, len(arrays), staged),
+        name="payload",
+        out_shape=(jax.ShapeDtypeStruct(shape, BF16),) * len(table),
+        in_specs=[smem, smem] + [anywhere] * len(arrays),
+        out_specs=(anywhere,) * len(table),
+        scratch_shapes=staging + [pltpu.SemaphoreType.DMA((len(table),))],
+        compiler_params=pltpu.CompilerParams(vmem_limit_bytes=2 << 20),
+        cost_estimate=pl.CostEstimate(
+            flops=0, bytes_accessed=4 * len(table) * shape[0] * shape[1], transcendentals=0
+        ),
+    )(odd, me, *arrays)
 
 
 def grad_out_kernel(me_ref, c0, c1, c2, c3, w_ref, out_ref):
@@ -126,11 +175,12 @@
 
 
 def attend_kernel(
-    odd_ref, me_ref, lo_ref, q, k0, k2, v0, v2, r1, r2, r3, g, w_ref,
-    att_ref, prob_ref, stat_ref, sent_ref, mine_ref, far_ref, k1, v1,
+    odd_ref, me_ref, lo_ref, q, k0, up, down, v0, v2, r1, r2, r3, g, w_ref,
+    att_ref, prob_ref, stat_ref, sent_ref, mine_ref, far_ref, k1, v1, k2,
 ):
     rows = q.shape[0]
     head = pl.program_id(0)
+    pick(me_ref[0] & 1, up, down, k2)
     pick(odd_ref[0], r2, r1, k1)
     pick(odd_ref[0], r3, r2, v1)
     keys, values = (k0, k1, k2), (v0, v1, v2)
@@ -190,7 +240,7 @@
     return tile, on_odd, on_even
 
 
-def attend_call(odd, me, lo, q, k0, k2, v0, v2, r1, r2, r3, g, weight):
+def attend_call(odd, me, lo, q, k0, up, down, v0, v2, r1, r2, r3, g, weight):
     rows, cols = q.shape
     heads = cols // HD
     tile, on_odd, on_even = tile_specs(rows)
@@ -211,7 +261,7 @@
             num_scalar_prefetch=2,
             grid=(heads,),
             in_specs=[pl.BlockSpec((rows, HD), lambda h, odd, me: (0, 0))]
-            + [tile] * 5
+            + [tile] * 6
             + [on_odd, tile, on_even, tile]
             + [pl.BlockSpec(weight.shape, lambda h, odd, me: (0, 0))],
             out_specs=(
@@ -222,18 +272,18 @@
                 whole,
                 whole,
             ),
-            scratch_shapes=[pltpu.VMEM((rows, HD), BF16)] * 2,
+            scratch_shapes=[pltpu.VMEM((rows, HD), BF16)] * 3,
         ),
         compiler_params=pltpu.CompilerParams(vmem_limit_bytes=VMEM_BYTES),
         cost_estimate=pl.CostEstimate(
             flops=8 * heads * rows * span * HD, bytes_accessed=12 << 20,
             transcendentals=heads * rows * span,
         ),
-    )(odd, me, lo, *in_hbm(q, k0), *in_vmem(k2), *in_hbm(v0), *in_vmem(v2, r1, r2, r3, g), *in_hbm(weight))
+    )(odd, me, lo, *in_hbm(q, k0), *in_vmem(up, down), *in_hbm(v0), *in_vmem(v2, r1, r2, r3, g), *in_hbm(weight))
 
 
 def grads_kernel(
-    odd_ref, me_ref, lo_ref, prob_ref, att, k0, k2, v0, v2, q0, q2, r1, r2, r3, g0, g1, g2,
+    odd_ref, me_ref, lo_ref, prob_ref, att, k0, up, v0, v2, q0, down, r1, r2, r3, g0, g1, g2,
     s0, s10, s11, s20, s21, dq_ref, dk_ref, dv_ref,
     kc, qc, gc, v1, s1, s2, probs, grad_s, grad_q,
 ):
@@ -259,8 +309,10 @@
     pick(odd, r1, r3, qc.at[tiles[1], :])
     pick(group, s10, s11, s1)
     pick(group, s20, s21, s2)
+    pick(group, up, down, kc.at[tiles[2], :])
+    pick(group, down, up, qc.at[tiles[2], :])
     for into, t, ref in (
-        (kc, 0, k0), (kc, 2, k2), (qc, 0, q0), (qc, 2, q2), (gc, 0, g0), (gc, 1, g1), (gc, 2, g2)
+        (kc, 0, k0), (qc, 0, q0), (gc, 0, g0), (gc, 1, g1), (gc, 2, g2)
     ):
         into[tiles[t], :] = ref[...]
     values, stats = (v0, v1, v2), (s0, s1, s2)
@@ -356,8 +408,8 @@
     def across(shard, bit):
         return swapped(shard, "head", bit)
 
-    def pair(from_even, from_odd):
-        return swapped(jnp.where(index % 2 == 0, from_even, from_odd), "ctx", 1)
+    def exchanged(shard):
+        return swapped(shard, "ctx", 1)
 
     def ringed(shard, by, bit):
         groups = lax.axis_size("head")
@@ -371,29 +423,34 @@
 
     cot_far = across(cotangent, 2)
     cot_near = across(cotangent, 1)
-    k2 = along(key_rows, 2)
-    r1 = pair(key_rows, queries)
+    side, up, down = payload_call(
+        odd, me, ((0, 0, 1, 1), (0, 1, 0, 1), (1, 0, 1, 0)), *in_hbm(key_rows, queries),
+        staged=True,
+    )
+    up = ringed(up, 2, 1)
+    down = ringed(down, 2, 0)
+    r1 = exchanged(side)
     v2 = along(value_rows, 2)
     cot_both = across(cot_far, 1)
-    q2 = along(queries, -2)
-    r2 = pair(value_rows, k2)
+    values = in_hbm(value_rows)
+    r2 = exchanged(*payload_call(odd, me, ((0, 0, 1, 2),), *values, *in_vmem(up, down)))
 
     g = grad_out_call(me, (cotangent, cot_near, cot_far, cot_both), out_weight)
     g2 = along(g, -2)
     bounds = jnp.stack([base, count * rows]).astype(jnp.int32)
     lo_col, lo_row = windows_call(bounds, offsets, rows)
-    r3 = pair(q2, v2)
-    g1 = pair(g2, g)
+    r3 = exchanged(*payload_call(odd, me, ((1, 0, 2, 2),), *in_vmem(up, down, v2)))
+    g1 = exchanged(*payload_call(odd, me, ((0, 0, 1, 1),), *in_vmem(g2, g)))
 
     attended, prob, stat, sent, kept, kept_far = attend_call(
-        odd, me, lo_col, queries, key_rows, k2, value_rows, v2, r1, r2, r3, g, out_weight
+        odd, me, lo_col, queries, key_rows, up, down, value_rows, v2, r1, r2, r3, g, out_weight
     )
     stats = [stat] + [ringed(stat, n, bit) for n in (1, 2) for bit in (0, 1)]
     came = across(sent, 1)
     far = across((kept_far + came[:, cols:].astype(F32)).astype(BF16), 2)
 
     grad_queries, grad_keys, grad_values = grads_call(
-        odd, me, lo_row, prob, attended, (key_rows, k2), (value_rows, v2), (queries, q2),
+        odd, me, lo_row, prob, attended, (key_rows, up), (value_rows, v2), (queries, down),
         (r1, r2, r3), (g, g1, g2), stats,
     )
     mixed = (kept + came[:, :cols].astype(F32) + far.astype(F32)).astype(BF16)

time: 91.8 us -> 97.3 us (1.060)
  Pallas kernels: 23.6 us -> 39.6 us
  other arithmetic: 5.6 us -> 1.15 us
  starting transfers between devices: 23.2 us -> 19.5 us
  waiting for transfers between devices: 38.1 us -> 35.9 us
    pallas_call x0 -> x4, Pallas kernels: none -> 15.9 us  [payload_call(): pl.pallas_call(functools.partial(payload_kernel, table, len(arrays), stag...]
    ppermute x4 -> x2, waiting for transfers between devices: 18.3 us -> 12.2 us  [passed_along(): return lax.ppermute(shard, axis, pairs)]
    ppermute x4 -> x2, starting transfers between devices: 11 us -> 5.23 us  [passed_along(): return lax.ppermute(shard, axis, pairs)]
    select_n x4 -> x0, other arithmetic: 4.42 us -> none  [pair(): return swapped(jnp.where(index % 2 == 0, from_even, from_odd), 'ctx', 1)]
    ppermute x4 -> x6, waiting for transfers between devices: 7.78 us -> 12.1 us  [ringed(): return lax.ppermute(shard, ('ctx', 'head'), pairs)]
    ppermute x4 -> x6, starting transfers between devices: 3.75 us -> 5.57 us  [ringed(): return lax.ppermute(shard, ('ctx', 'head'), pairs)]
  transfers between devices with their start and end apart: 17 -> 17, of which waited for: 7 -> 7; matrix products, arithmetic and copies ran while one was open for 5% -> 0% of each run, Pallas kernels for 15% -> 30%
where the time goes in v1:
time: 97.3 us; the launch traced here: 97 us
  Pallas kernels  39.6 us (41%)
  waiting for transfers between devices  35.9 us (37%)
  starting transfers between devices  19.5 us (20%)
  other arithmetic  1.15 us (1%)
    pallas_call x4, Pallas kernels, payload_call(): pl.pallas_call(functools.partial(payload_kernel, table, len(arrays), stag...  15.9 us
    ppermute x2, waiting for transfers between devices, passed_along(): return lax.ppermute(shard, axis, pairs)  12.2 us
    ppermute x6, waiting for transfers between devices, ringed(): return lax.ppermute(shard, ('ctx', 'head'), pairs)  12.1 us
    ppermute x9, waiting for transfers between devices, swapped(): return lax.ppermute(shard, axis, [(i, i ^ bit) for i in range(length)])  11.7 us
    pallas_call x1, Pallas kernels, attend_call(): pl.pallas_call(attend_kernel, name='attend', out_shape=(jax.ShapeDtypeStr...  10.2 us
    pallas_call x1, Pallas kernels, grads_call(): pl.pallas_call(grads_kernel, name='grads', out_shape=(jax.ShapeDtypeStruc...  9.94 us
    ppermute x9, starting transfers between devices, swapped(): return lax.ppermute(shard, axis, [(i, i ^ bit) for i in range(length)])  8.68 us
    ppermute x6, starting transfers between devices, ringed(): return lax.ppermute(shard, ('ctx', 'head'), pairs)  5.57 us
  transfers between devices with their start and end apart: 17, of which 7 were waited for; matrix products, arithmetic and copies ran while one was open for 0% of the time, Pallas kernels for 30%

profile of v1, /device:TPU:0, one launch (start us, length us, event | category | flops | bytes accessed | tf_op | source)
XLA Modules:
  0.0 97.0 jit_solution(636007352279789252)
XLA Ops:
  0.6 3.0 %collective-permute-start.7 = (bf16[384,512]{1,0:T(8,128)(2,1)}, bf16[384,512]{1,0:T(8,128)(2,1)S(1)}, u32[]{:S(2)}, u32[]{:S(2)}) collective-permute-start(bf16[384,512]{1,0:T(8,128)(2,1)} %c0.1), channel_id=1, source_target_pairs={{0,2},{1,3},{2,0},{3,1},{4,6},{5,7},{6,4},{7,5},{8,10},{9,11},{10,... | collective-permute-start | bytes 1179656 | tf_op jit(solution)/shard_map/ppermute | solution.py:36
  3.7 1.9 %payload.4 = (bf16[384,512]{1,0:T(8,128)(2,1)}, bf16[384,512]{1,0:T(8,128)(2,1)S(1)}, bf16[384,512]{1,0:T(8,128)(2,1)S(1)}) custom-call(s32[1]{0:T(128)} %bitcast.odd_ref, s32[1]{0:T(128)} %bitcast.1.me_ref, bf16[384,512]{1,0:T(8,128)(2,1)} %k0.3, bf16[384,512]{1,0:T(8,128)(2,1)} %q0.1), custom_call_target="tpu_custom_call" | custom-call | bytes 2359296 | tf_op jit(solution)/shard_map/payload/pallas_call | solution.py:123
  5.6 1.6 %collective-permute-start = (bf16[384,512]{1,0:T(8,128)(2,1)S(1)}, bf16[384,512]{1,0:T(8,128)(2,1)S(1)}, u32[]{:S(2)}, u32[]{:S(2)}) collective-permute-start(bf16[384,512]{1,0:T(8,128)(2,1)S(1)} %get-tuple-element.19), channel_id=1, source_target_pairs={{0,8},{1,0},{2,10},{3,2},{4,12},{5,4},{6,14},{7,6},{8,16},{9,1},{1... | collective-permute-start | bytes 1179656 | tf_op jit(solution)/shard_map/ppermute | solution.py:422
  7.2 3.9 %collective-permute-start.2 = (bf16[384,512]{1,0:T(8,128)(2,1)}, bf16[384,512]{1,0:T(8,128)(2,1)S(1)}, u32[]{:S(2)}, u32[]{:S(2)}) collective-permute-start(bf16[384,512]{1,0:T(8,128)(2,1)} %v0.3), channel_id=1, source_target_pairs={{0,8},{4,12},{8,16},{12,20},{16,24},{20,28},{1,9},{5,13},{9,17},{1... | collective-permute-start | bytes 1179656 | tf_op jit(solution)/shard_map/ppermute | solution.py:31
  11.1 0.1 collective-permute-start.6
  11.2 1.8 %collective-permute-done.7.c2 = bf16[384,512]{1,0:T(8,128)(2,1)S(1)} collective-permute-done((bf16[384,512]{1,0:T(8,128)(2,1)}, bf16[384,512]{1,0:T(8,128)(2,1)S(1)}, u32[]{:S(2)}, u32[]{:S(2)}) %collective-permute-start.7) | collective-permute-done | bytes 393248 | tf_op jit(solution)/shard_map/ppermute | solution.py:36
  13.0 0.0 collective-permute-start.8
  13.0 3.7 %collective-permute-done.refs_1_.refs_0_.up = bf16[384,512]{1,0:T(8,128)(2,1)S(1)} collective-permute-done((bf16[384,512]{1,0:T(8,128)(2,1)S(1)}, bf16[384,512]{1,0:T(8,128)(2,1)S(1)}, u32[]{:S(2)}, u32[]{:S(2)}) %collective-permute-start) | collective-permute-done | bytes 393248 | tf_op jit(solution)/shard_map/ppermute | solution.py:422
  16.7 1.5 %collective-permute-start.3 = (bf16[384,512]{1,0:T(8,128)(2,1)}, bf16[384,512]{1,0:T(8,128)(2,1)S(1)}, u32[]{:S(2)}, u32[]{:S(2)}) collective-permute-start(bf16[384,512]{1,0:T(8,128)(2,1)} %get-tuple-element.21), channel_id=1, source_target_pairs={{0,4},{4,0},{8,12},{12,8},{16,20},{20,16},{24,28},{28,24},{1,5},{5... | collective-permute-start | bytes 1179656 | tf_op jit(solution)/shard_map/ppermute | solution.py:36
  18.2 13.0 %payload.5 = bf16[384,512]{1,0:T(8,128)(2,1)} custom-call(s32[1]{0:T(128)} %bitcast.odd_ref, s32[1]{0:T(128)} %bitcast.1.me_ref, bf16[384,512]{1,0:T(8,128)(2,1)} %v0.3, bf16[384,512]{1,0:T(8,128)(2,1)S(1)} %collective-permute-done.refs_1_.refs_0_.up, bf16[384,512]{1,0:T(8,128)(2,1)S(1)} %collective-permute-done.1.refs_2_.refs_1_.down), custom_call_target="tpu_custom_call" | custom-call | bytes 786432 | tf_op jit(solution)/shard_map/payload/pallas_call | solution.py:123
  31.2 0.1 collective-permute-start.4
  31.3 0.8 payload.6
  32.1 2.1 %collective-permute-start.5 = (bf16[384,512]{1,0:T(8,128)(2,1)}, bf16[384,512]{1,0:T(8,128)(2,1)S(1)}, u32[]{:S(2)}, u32[]{:S(2)}) collective-permute-start(bf16[384,512]{1,0:T(8,128)(2,1)} %payload.6), channel_id=1, source_target_pairs={{0,4},{4,0},{8,12},{12,8},{16,20},{20,16},{24,28},{28,24},{1,5},{5... | collective-permute-start | bytes 1179656 | tf_op jit(solution)/shard_map/ppermute | solution.py:36
  34.2 0.1 pad_add_fusion.base_ref
  34.2 1.0 %windows.1 = (s32[384,128]{1,0:T(8,128)S(1)}, s32[3,384]{1,0:T(4,128)S(1)}) custom-call(s32[2]{0:T(128)S(1)} %pad_add_fusion.base_ref, s32[136]{0:T(256)S(1)} %copy-done), custom_call_target="tpu_custom_call" | custom-call | flops 1048576 | bytes 262144 | tf_op jit(solution)/shard_map/windows/pallas_call | solution.py:63
  35.3 2.6 %grad_out.1.g.refs_1_.g0 = bf16[384,512]{1,0:T(8,128)(2,1)S(1)} custom-call(s32[1]{0:T(128)} %bitcast.1.me_ref, bf16[384,512]{1,0:T(8,128)(2,1)} %c0.1, bf16[384,512]{1,0:T(8,128)(2,1)S(1)} %collective-permute-done.6.c1, bf16[384,512]{1,0:T(8,128)(2,1)S(1)} %collective-permute-done.7.c2, bf16[384,512]{1,0:T(8,128)(2,1)S(1)} %collective-permute-done.8.c3, ...), custom_call_target="tpu_custom_call" | custom-call | flops 805306368 | bytes 6291456 | tf_op jit(solution)/shard_map/grad_out/pallas_call | solution.py:150
  37.9 5.6 %collective-permute-done.4.r2 = bf16[384,512]{1,0:T(8,128)(2,1)S(1)} collective-permute-done((bf16[384,512]{1,0:T(8,128)(2,1)}, bf16[384,512]{1,0:T(8,128)(2,1)S(1)}, u32[]{:S(2)}, u32[]{:S(2)}) %collective-permute-start.4) | collective-permute-done | bytes 393248 | tf_op jit(solution)/shard_map/ppermute | solution.py:36
  43.5 4.3 %collective-permute-done.5.r3 = bf16[384,512]{1,0:T(8,128)(2,1)S(1)} collective-permute-done((bf16[384,512]{1,0:T(8,128)(2,1)}, bf16[384,512]{1,0:T(8,128)(2,1)S(1)}, u32[]{:S(2)}, u32[]{:S(2)}) %collective-permute-start.5) | collective-permute-done | bytes 393248 | tf_op jit(solution)/shard_map/ppermute | solution.py:36
  47.8 10.2 %attend.1 = (bf16[384,512]{1,0:T(8,128)(2,1)S(1)}, bf16[4,384,1152]{2,1,0:T(8,128)(2,1)S(1)}, f32[4,2,384]{2,1,0:T(2,128)S(1)}, bf16[384,1024]{1,0:T(8,128)(2,1)...) custom-call(s32[1]{0:T(128)} %bitcast.odd_ref, s32[1]{0:T(128)} %bitcast.1.me_ref, ...), custom_call_target="tpu_custom_call" | custom-call | flops 1409286144 | bytes 12582912 | tf_op jit(solution)/shard_map/attend/pallas_call | solution.py:249
  58.0 0.1 collective-permute-start.9
  58.1 1.3 %collective-permute-start.11 = (bf16[384,512]{1,0:T(8,128)(2,1)S(1)}, bf16[384,512]{1,0:T(8,128)(2,1)S(1)}, u32[]{:S(2)}, u32[]{:S(2)}) collective-permute-start(bf16[384,512]{1,0:T(8,128)(2,1)S(1)} %grad_out.1.g.refs_1_.g0), channel_id=1, source_target_pairs={{8,0},{12,4},{16,8},{20,12},{24,16},{28,20},{9,1},{13,5},{17,9},{2... | collective-permute-start | bytes 1179656 | tf_op jit(solution)/shard_map/ppermute | solution.py:31
  59.4 12.2 %collective-permute-done.11.refs_0_.g2 = bf16[384,512]{1,0:T(8,128)(2,1)S(1)} collective-permute-done((bf16[384,512]{1,0:T(8,128)(2,1)S(1)}, bf16[384,512]{1,0:T(8,128)(2,1)S(1)}, u32[]{:S(2)}, u32[]{:S(2)}) %collective-permute-start.11) | collective-permute-done | bytes 393248 | tf_op jit(solution)/shard_map/ppermute | solution.py:31
  71.5 0.2 payload.7
  71.7 0.3 collective-permute-start.12
  72.1 0.1 add_convert_fusion.1
  72.2 1.5 %collective-permute-start.10 = (bf16[384,512]{1,0:T(8,128)(2,1)S(1)}, bf16[384,512]{1,0:T(8,128)(2,1)S(1)}, u32[]{:S(2)}, u32[]{:S(2)}) collective-permute-start(bf16[384,512]{1,0:T(8,128)(2,1)S(1)} %add_convert_fusion.1), channel_id=1, source_target_pairs={{0,2},{1,3},{2,0},{3,1},{4,6},{5,7},{6,4},{7,5},{8,10},{9,11},{10,... | collective-permute-start | bytes 1179656 | tf_op jit(solution)/shard_map/ppermute | solution.py:36
  73.7 2.0 %collective-permute-start.14 = (f32[4,2,384]{2,1,0:T(2,128)S(1)}, f32[4,2,384]{2,1,0:T(2,128)S(1)}, u32[]{:S(2)}, u32[]{:S(2)}) collective-permute-start(f32[4,2,384]{2,1,0:T(2,128)S(1)} %get-tuple-element.28.s0), channel_id=1, source_target_pairs={{0,4},{1,0},{2,6},{3,2},{4,8},{5,1},{6,10},{7,3},{8,12},{9,5},{10,... | collective-permute-start | bytes 36872 | tf_op jit(solution)/shard_map/ppermute | solution.py:422
  75.8 7.0 %collective-permute-done.13.s10 = f32[4,2,384]{2,1,0:T(2,128)S(1)} collective-permute-done((f32[4,2,384]{2,1,0:T(2,128)S(1)}, f32[4,2,384]{2,1,0:T(2,128)S(1)}, u32[]{:S(2)}, u32[]{:S(2)}) %collective-permute-start.13) | collective-permute-done | bytes 12320 | tf_op jit(solution)/shard_map/ppermute | solution.py:422
  82.8 1.9 %collective-permute-start.16 = (f32[4,2,384]{2,1,0:T(2,128)S(1)}, f32[4,2,384]{2,1,0:T(2,128)S(1)}, u32[]{:S(2)}, u32[]{:S(2)}) collective-permute-start(f32[4,2,384]{2,1,0:T(2,128)S(1)} %get-tuple-element.28.s0), channel_id=1, source_target_pairs={{0,8},{1,0},{2,10},{3,2},{4,12},{5,4},{6,14},{7,6},{8,16},{9,1},{1... | collective-permute-start | bytes 36872 | tf_op jit(solution)/shard_map/ppermute | solution.py:422
  84.7 1.4 %collective-permute-done.16.s21 = f32[4,2,384]{2,1,0:T(2,128)S(1)} collective-permute-done((f32[4,2,384]{2,1,0:T(2,128)S(1)}, f32[4,2,384]{2,1,0:T(2,128)S(1)}, u32[]{:S(2)}, u32[]{:S(2)}) %collective-permute-start.16) | collective-permute-done | bytes 12320 | tf_op jit(solution)/shard_map/ppermute | solution.py:422
  86.1 9.9 %grads.1 = (bf16[384,512]{1,0:T(8,128)(2,1)}, bf16[384,512]{1,0:T(8,128)(2,1)}, bf16[384,512]{1,0:T(8,128)(2,1)}) custom-call(s32[1]{0:T(128)} %bitcast.odd_ref, s32[1]{0:T(128)} %bitcast.1.me_ref, s32[3,384]{1,0:T(4,128)S(1)} %get-tuple-element.25.lo_ref, bf16[4,384,1152]{2,1,0:T(8,128)(2,1)S(1)} %get-tuple-element.26.prob_ref, ...), custom_call_target="tpu_custom_call" | custom-call | flops 2717908992 | bytes 10485760 | tf_op jit(solution)/shard_map/grads/pallas_call | solution.py:368
  96.1 0.9 add_convert_fusion
  (15 shorter events, 0.0 us)
Async XLA Ops:
  0.6 33.6 %copy-start = (s32[136]{0:T(256)S(1)}, s32[136]{0:T(256)}, u32[]{:S(2)}) copy-start(s32[136]{0:T(256)} %offsets_ref.1) | copy-start | bytes 1636
  0.6 12.4 %collective-permute-start.7 = (bf16[384,512]{1,0:T(8,128)(2,1)}, bf16[384,512]{1,0:T(8,128)(2,1)S(1)}, u32[]{:S(2)}, u32[]{:S(2)}) collective-permute-start(bf16[384,512]{1,0:T(8,128)(2,1)} %c0.1), channel_id=1, source_target_pairs={{0,2},{1,3},{2,0},{3,1},{4,6},{5,7},{6,4},{7,5},{8,10},{9,11},{10,... | collective-permute-start | bytes 1179656 | tf_op jit(solution)/shard_map/ppermute | solution.py:36
  5.6 11.1 %collective-permute-start = (bf16[384,512]{1,0:T(8,128)(2,1)S(1)}, bf16[384,512]{1,0:T(8,128)(2,1)S(1)}, u32[]{:S(2)}, u32[]{:S(2)}) collective-permute-start(bf16[384,512]{1,0:T(8,128)(2,1)S(1)} %get-tuple-element.19), channel_id=1, source_target_pairs={{0,8},{1,0},{2,10},{3,2},{4,12},{5,4},{6,14},{7,6},{8,16},{9,1},{1... | collective-permute-start | bytes 1179656 | tf_op jit(solution)/shard_map/ppermute | solution.py:422
  7.2 11.0 %collective-permute-start.1 = (bf16[384,512]{1,0:T(8,128)(2,1)S(1)}, bf16[384,512]{1,0:T(8,128)(2,1)S(1)}, u32[]{:S(2)}, u32[]{:S(2)}) collective-permute-start(bf16[384,512]{1,0:T(8,128)(2,1)S(1)} %get-tuple-element.20), channel_id=1, source_target_pairs={{0,1},{1,9},{2,3},{3,11},{4,5},{5,13},{6,7},{7,15},{8,0},{9,17},{1... | collective-permute-start | bytes 1179656 | tf_op jit(solution)/shard_map/ppermute | solution.py:422
  7.2 24.1 %collective-permute-start.2 = (bf16[384,512]{1,0:T(8,128)(2,1)}, bf16[384,512]{1,0:T(8,128)(2,1)S(1)}, u32[]{:S(2)}, u32[]{:S(2)}) collective-permute-start(bf16[384,512]{1,0:T(8,128)(2,1)} %v0.3), channel_id=1, source_target_pairs={{0,8},{4,12},{8,16},{12,20},{16,24},{20,28},{1,9},{5,13},{9,17},{1... | collective-permute-start | bytes 1179656 | tf_op jit(solution)/shard_map/ppermute | solution.py:31
  11.1 24.1 %collective-permute-start.6 = (bf16[384,512]{1,0:T(8,128)(2,1)}, bf16[384,512]{1,0:T(8,128)(2,1)S(1)}, u32[]{:S(2)}, u32[]{:S(2)}) collective-permute-start(bf16[384,512]{1,0:T(8,128)(2,1)} %c0.1), channel_id=1, source_target_pairs={{0,1},{1,0},{2,3},{3,2},{4,5},{5,4},{6,7},{7,6},{8,9},{9,8},{10,11... | collective-permute-start | bytes 1179656 | tf_op jit(solution)/shard_map/ppermute | solution.py:36
  13.0 22.2 %collective-permute-start.8 = (bf16[384,512]{1,0:T(8,128)(2,1)S(1)}, bf16[384,512]{1,0:T(8,128)(2,1)S(1)}, u32[]{:S(2)}, u32[]{:S(2)}) collective-permute-start(bf16[384,512]{1,0:T(8,128)(2,1)S(1)} %collective-permute-done.7.c2), channel_id=1, source_target_pairs={{0,1},{1,0},{2,3},{3,2},{4,5},{5,4},{6,7},{7,6},{8,9},{9,8},{10,11... | collective-permute-start | bytes 1179656 | tf_op jit(solution)/shard_map/ppermute | solution.py:36
  16.7 21.2 %collective-permute-start.3 = (bf16[384,512]{1,0:T(8,128)(2,1)}, bf16[384,512]{1,0:T(8,128)(2,1)S(1)}, u32[]{:S(2)}, u32[]{:S(2)}) collective-permute-start(bf16[384,512]{1,0:T(8,128)(2,1)} %get-tuple-element.21), channel_id=1, source_target_pairs={{0,4},{4,0},{8,12},{12,8},{16,20},{20,16},{24,28},{28,24},{1,5},{5... | collective-permute-start | bytes 1179656 | tf_op jit(solution)/shard_map/ppermute | solution.py:36
  31.2 12.3 %collective-permute-start.4 = (bf16[384,512]{1,0:T(8,128)(2,1)}, bf16[384,512]{1,0:T(8,128)(2,1)S(1)}, u32[]{:S(2)}, u32[]{:S(2)}) collective-permute-start(bf16[384,512]{1,0:T(8,128)(2,1)} %payload.5), channel_id=1, source_target_pairs={{0,4},{4,0},{8,12},{12,8},{16,20},{20,16},{24,28},{28,24},{1,5},{5... | collective-permute-start | bytes 1179656 | tf_op jit(solution)/shard_map/ppermute | solution.py:36
  32.1 15.7 %collective-permute-start.5 = (bf16[384,512]{1,0:T(8,128)(2,1)}, bf16[384,512]{1,0:T(8,128)(2,1)S(1)}, u32[]{:S(2)}, u32[]{:S(2)}) collective-permute-start(bf16[384,512]{1,0:T(8,128)(2,1)} %payload.6), channel_id=1, source_target_pairs={{0,4},{4,0},{8,12},{12,8},{16,20},{20,16},{24,28},{28,24},{1,5},{5... | collective-permute-start | bytes 1179656 | tf_op jit(solution)/shard_map/ppermute | solution.py:36
  58.0 14.1 %collective-permute-start.9 = (bf16[384,1024]{1,0:T(8,128)(2,1)S(1)}, bf16[384,1024]{1,0:T(8,128)(2,1)S(1)}, u32[]{:S(2)}, u32[]{:S(2)}) collective-permute-start(bf16[384,1024]{1,0:T(8,128)(2,1)S(1)} %get-tuple-element.23), channel_id=1, source_target_pairs={{0,1},{1,0},{2,3},{3,2},{4,5},{5,4},{6,7},{7,6},{8,9},{9,8},{10,11... | collective-permute-start | bytes 2359304 | tf_op jit(solution)/shard_map/ppermute | solution.py:36
  58.1 13.5 %collective-permute-start.11 = (bf16[384,512]{1,0:T(8,128)(2,1)S(1)}, bf16[384,512]{1,0:T(8,128)(2,1)S(1)}, u32[]{:S(2)}, u32[]{:S(2)}) collective-permute-start(bf16[384,512]{1,0:T(8,128)(2,1)S(1)} %grad_out.1.g.refs_1_.g0), channel_id=1, source_target_pairs={{8,0},{12,4},{16,8},{20,12},{24,16},{28,20},{9,1},{13,5},{17,9},{2... | collective-permute-start | bytes 1179656 | tf_op jit(solution)/shard_map/ppermute | solution.py:31
  71.7 14.4 %collective-permute-start.12 = (bf16[384,512]{1,0:T(8,128)(2,1)S(1)}, bf16[384,512]{1,0:T(8,128)(2,1)S(1)}, u32[]{:S(2)}, u32[]{:S(2)}) collective-permute-start(bf16[384,512]{1,0:T(8,128)(2,1)S(1)} %payload.7), channel_id=1, source_target_pairs={{0,4},{4,0},{8,12},{12,8},{16,20},{20,16},{24,28},{28,24},{1,5},{5... | collective-permute-start | bytes 1179656 | tf_op jit(solution)/shard_map/ppermute | solution.py:36
  72.2 23.8 %collective-permute-start.10 = (bf16[384,512]{1,0:T(8,128)(2,1)S(1)}, bf16[384,512]{1,0:T(8,128)(2,1)S(1)}, u32[]{:S(2)}, u32[]{:S(2)}) collective-permute-start(bf16[384,512]{1,0:T(8,128)(2,1)S(1)} %add_convert_fusion.1), channel_id=1, source_target_pairs={{0,2},{1,3},{2,0},{3,1},{4,6},{5,7},{6,4},{7,5},{8,10},{9,11},{10,... | collective-permute-start | bytes 1179656 | tf_op jit(solution)/shard_map/ppermute | solution.py:36
  73.7 9.0 %collective-permute-start.13 = (f32[4,2,384]{2,1,0:T(2,128)S(1)}, f32[4,2,384]{2,1,0:T(2,128)S(1)}, u32[]{:S(2)}, u32[]{:S(2)}) collective-permute-start(f32[4,2,384]{2,1,0:T(2,128)S(1)} %get-tuple-element.28.s0), channel_id=1, source_target_pairs={{0,1},{1,5},{2,3},{3,7},{4,0},{5,9},{6,2},{7,11},{8,4},{9,13},{10,... | collective-permute-start | bytes 36872 | tf_op jit(solution)/shard_map/ppermute | solution.py:422
  73.7 11.0 %collective-permute-start.14 = (f32[4,2,384]{2,1,0:T(2,128)S(1)}, f32[4,2,384]{2,1,0:T(2,128)S(1)}, u32[]{:S(2)}, u32[]{:S(2)}) collective-permute-start(f32[4,2,384]{2,1,0:T(2,128)S(1)} %get-tuple-element.28.s0), channel_id=1, source_target_pairs={{0,4},{1,0},{2,6},{3,2},{4,8},{5,1},{6,10},{7,3},{8,12},{9,5},{10,... | collective-permute-start | bytes 36872 | tf_op jit(solution)/shard_map/ppermute | solution.py:422
  75.8 9.0 %collective-permute-start.15 = (f32[4,2,384]{2,1,0:T(2,128)S(1)}, f32[4,2,384]{2,1,0:T(2,128)S(1)}, u32[]{:S(2)}, u32[]{:S(2)}) collective-permute-start(f32[4,2,384]{2,1,0:T(2,128)S(1)} %get-tuple-element.28.s0), channel_id=1, source_target_pairs={{0,1},{1,9},{2,3},{3,11},{4,5},{5,13},{6,7},{7,15},{8,0},{9,17},{1... | collective-permute-start | bytes 36872 | tf_op jit(solution)/shard_map/ppermute | solution.py:422
  82.8 3.3 %collective-permute-start.16 = (f32[4,2,384]{2,1,0:T(2,128)S(1)}, f32[4,2,384]{2,1,0:T(2,128)S(1)}, u32[]{:S(2)}, u32[]{:S(2)}) collective-permute-start(f32[4,2,384]{2,1,0:T(2,128)S(1)} %get-tuple-element.28.s0), channel_id=1, source_target_pairs={{0,8},{1,0},{2,10},{3,2},{4,12},{5,4},{6,14},{7,6},{8,16},{9,1},{1... | collective-permute-start | bytes 36872 | tf_op jit(solution)/shard_map/ppermute | solution.py:422

commit v2 on v1

--- a/solution.py
+++ b/solution.py
@@ -165,54 +165,105 @@
     )(me, *in_hbm(shards[0]), *in_vmem(*shards[1:]), *in_hbm(weight))
 
 
-def key_pieces(block, rows):
-    first, last = block * ROWS, (block + 1) * ROWS
-    return ((2, first, rows, -2 * rows), (1, 0, rows, -rows), (0, 0, last, 0))
-
-
 def pick(odd, even_ref, odd_ref, into):
     into[...] = jnp.where(odd == 0, even_ref[...], odd_ref[...])
 
 
+def spread(column):
+    return jnp.broadcast_to(column, (column.shape[0], HD))
+
+
+def near_kernel(
+    me_ref, lo_ref, q, k0, up, down, v0, v2, prob_ref, top_ref, total_ref, sum_ref, k2
+):
+    rows = q.shape[0]
+    blocks = range(0, rows, ROWS)
+    pick(me_ref[0] & 1, up, down, k2)
+    own = [mm(q[c:rows, :], k0[c : c + ROWS, :], NT) for c in blocks]
+    far = [mm(q[0 : c + ROWS, :], k2[c : c + ROWS, :], NT) for c in blocks]
+    for b in blocks:
+        mine = slice(b, b + ROWS)
+        lo = lo_ref[mine, :]
+        scores = []
+        for c in blocks:
+            lane = lax.broadcasted_iota(jnp.int32, (ROWS, HD), 1)
+            if c <= b:
+                ok = lane + c >= lo
+                if c == b:
+                    ok &= lane <= lax.broadcasted_iota(jnp.int32, (ROWS, HD), 0)
+                part = own[c // ROWS][b - c : b - c + ROWS, :]
+                scores.append((c, jnp.where(ok, part, NEG_FILL)))
+            if c >= b:
+                ok = lane + (c - REACH * rows) >= lo
+                part = far[c // ROWS][mine, :]
+                scores.append((rows + c, jnp.where(ok, part, NEG_FILL)))
+        top = jnp.max(functools.reduce(jnp.maximum, [x for _, x in scores]), axis=1, keepdims=True)
+        shift = spread(top * (SCALE * LOG2E))
+        exps = [jnp.exp2(x * (SCALE * LOG2E) - shift) for _, x in scores]
+        total = jnp.sum(functools.reduce(jnp.add, exps), axis=1, keepdims=True)
+        for (place, _), e in zip(scores, exps):
+            prob_ref[0, mine, place : place + HD] = e.astype(BF16)
+        sum_ref[mine, :] = mm(prob_ref[0, mine, 0 : b + ROWS], v0[0 : b + ROWS, :], NN) + mm(
+            prob_ref[0, mine, rows + b : 2 * rows], v2[b:rows, :], NN
+        )
+        top_ref[mine, :] = shift
+        total_ref[mine, :] = spread(total)
+
+
+def near_call(me, lo, q, k0, up, down, v0, v2):
+    rows, cols = q.shape
+    heads = cols // HD
+    tile = pl.BlockSpec((rows, HD), lambda h, me: (0, h))
+    return pl.pallas_call(
+        near_kernel,
+        name="near",
+        out_shape=(jax.ShapeDtypeStruct((heads, rows, 2 * rows), BF16),)
+        + (jax.ShapeDtypeStruct((rows, cols), F32),) * 3,
+        grid_spec=pltpu.PrefetchScalarGridSpec(
+            num_scalar_prefetch=1,
+            grid=(heads,),
+            in_specs=[pl.BlockSpec((rows, HD), lambda h, me: (0, 0))] + [tile] * 6,
+            out_specs=(pl.BlockSpec((1, rows, 2 * rows), lambda h, me: (h, 0, 0)),) + (tile,) * 3,
+            scratch_shapes=[pltpu.VMEM((rows, HD), BF16)],
+        ),
+        compiler_params=pltpu.CompilerParams(vmem_limit_bytes=VMEM_BYTES),
+        cost_estimate=pl.CostEstimate(
+            flops=16 * heads * rows * rows * HD, bytes_accessed=10 << 20,
+            transcendentals=2 * heads * rows * rows,
+        ),
+    )(me, lo, *in_hbm(q, k0), *in_vmem(up, down), *in_hbm(v0), *in_vmem(v2))
+
+
 def attend_kernel(
-    odd_ref, me_ref, lo_ref, q, k0, up, down, v0, v2, r1, r2, r3, g, w_ref,
-    att_ref, prob_ref, stat_ref, sent_ref, mine_ref, far_ref, k1, v1, k2,
+    odd_ref, me_ref, lo_ref, q, r1, r2, r3, g, near_top, near_total, near_sum, w_ref,
+    att_ref, prob_ref, factor_ref, stat_ref, sent_ref, mine_ref, far_ref, k1, v1,
 ):
     rows = q.shape[0]
     head = pl.program_id(0)
-    pick(me_ref[0] & 1, up, down, k2)
     pick(odd_ref[0], r2, r1, k1)
     pick(odd_ref[0], r3, r2, v1)
-    keys, values = (k0, k1, k2), (v0, v1, v2)
-    for b in range(rows // ROWS):
-        mine = slice(b * ROWS, (b + 1) * ROWS)
-        qb = q[mine, :]
+    raw = mm(q[...], k1[...], NT)
+    for b in range(0, rows, ROWS):
+        mine = slice(b, b + ROWS)
         lo = lo_ref[mine, :]
-        scores, places = [], []
-        for tile, first, last, off in key_pieces(b, rows):
-            raw = mm(qb, keys[tile][first:last, :], NT)
-            for c in range(0, last - first, HD):
-                part = raw[:, c : c + HD]
-                pos = off + first + c + lax.broadcasted_iota(jnp.int32, part.shape, 1)
-                ok = pos >= lo
-                if tile == 0 and first + c == b * ROWS:
-                    ok &= pos <= b * ROWS + lax.broadcasted_iota(jnp.int32, part.shape, 0)
-                scores.append(jnp.where(ok, part, NEG_FILL))
-                places.append(tile * rows + first + c)
+        scores = []
+        for c in range(0, rows, ROWS):
+            lane = lax.broadcasted_iota(jnp.int32, (ROWS, HD), 1)
+            scores.append(jnp.where(lane + (c - rows) >= lo, raw[mine, c : c + HD], NEG_FILL))
         top = jnp.max(functools.reduce(jnp.maximum, scores), axis=1, keepdims=True)
-        shift = jnp.broadcast_to(top * (SCALE * LOG2E), (ROWS, HD))
+        shift = jnp.maximum(spread(top * (SCALE * LOG2E)), near_top[mine, :])
         exps = [jnp.exp2(s * (SCALE * LOG2E) - shift) for s in scores]
-        total = jnp.sum(functools.reduce(jnp.add, exps), axis=1, keepdims=True)
-        inverse = jnp.broadcast_to(1.0 / total, (ROWS, HD))
-        mixed = None
-        for e, place in zip(exps, places):
-            prob_ref[0, mine, place : place + HD] = (e * inverse).astype(BF16)
-        for tile, first, last, off in key_pieces(b, rows):
-            prob = prob_ref[0, mine, tile * rows + first : tile * rows + last]
-            part = mm(prob, values[tile][first:last, :], NN)
-            mixed = part if mixed is None else mixed + part
-        attended = mixed.astype(BF16)
+        rescale = jnp.exp2(near_top[mine, :] - shift)
+        total = rescale * near_total[mine, :] + spread(
+            jnp.sum(functools.reduce(jnp.add, exps), axis=1, keepdims=True)
+        )
+        inverse = 1.0 / total
+        factor = rescale * inverse
+        for n, e in enumerate(exps):
+            prob_ref[0, mine, n * HD : (n + 1) * HD] = (e * inverse).astype(BF16)
+        attended = (near_sum[mine, :] * factor + mm(prob_ref[0, mine, :], v1[...], NN)).astype(BF16)
         att_ref[mine, pl.ds(pl.multiple_of(head * HD, HD), HD)] = attended
+        factor_ref[mine, :] = factor
         delta = jnp.sum(attended.astype(F32) * g[mine, :].astype(F32), axis=1, keepdims=True)
         log_total = shift + jnp.log2(total)
         lane = lax.broadcasted_iota(jnp.int32, (ROWS, ROWS), 1)
@@ -240,18 +291,18 @@
     return tile, on_odd, on_even
 
 
-def attend_call(odd, me, lo, q, k0, up, down, v0, v2, r1, r2, r3, g, weight):
+def attend_call(odd, me, lo, q, r1, r2, r3, g, near, weight):
     rows, cols = q.shape
     heads = cols // HD
     tile, on_odd, on_even = tile_specs(rows)
-    span = REACH * rows + ROWS
     whole = pl.BlockSpec((rows, cols), lambda h, odd, me: (0, 0))
     return pl.pallas_call(
         attend_kernel,
         name="attend",
         out_shape=(
             jax.ShapeDtypeStruct((rows, cols), BF16),
-            jax.ShapeDtypeStruct((heads, rows, (REACH + 1) * rows), BF16),
+            jax.ShapeDtypeStruct((heads, rows, rows), BF16),
+            jax.ShapeDtypeStruct((rows, cols), F32),
             jax.ShapeDtypeStruct((heads, 2, rows), F32),
             jax.ShapeDtypeStruct((rows, 2 * cols), BF16),
             jax.ShapeDtypeStruct((rows, cols), F32),
@@ -261,29 +312,29 @@
             num_scalar_prefetch=2,
             grid=(heads,),
             in_specs=[pl.BlockSpec((rows, HD), lambda h, odd, me: (0, 0))]
-            + [tile] * 6
-            + [on_odd, tile, on_even, tile]
+            + [tile, on_odd, tile, on_even, tile, tile, tile, tile]
             + [pl.BlockSpec(weight.shape, lambda h, odd, me: (0, 0))],
             out_specs=(
                 whole,
-                pl.BlockSpec((1, rows, (REACH + 1) * rows), lambda h, odd, me: (h, 0, 0)),
+                pl.BlockSpec((1, rows, rows), lambda h, odd, me: (h, 0, 0)),
+                tile,
                 pl.BlockSpec((1, 2, rows), lambda h, odd, me: (h, 0, 0)),
                 pl.BlockSpec((rows, 2 * cols), lambda h, odd, me: (0, 0)),
                 whole,
                 whole,
             ),
-            scratch_shapes=[pltpu.VMEM((rows, HD), BF16)] * 3,
+            scratch_shapes=[pltpu.VMEM((rows, HD), BF16)] * 2,
         ),
         compiler_params=pltpu.CompilerParams(vmem_limit_bytes=VMEM_BYTES),
         cost_estimate=pl.CostEstimate(
-            flops=8 * heads * rows * span * HD, bytes_accessed=12 << 20,
-            transcendentals=heads * rows * span,
-        ),
-    )(odd, me, lo, *in_hbm(q, k0), *in_vmem(up, down), *in_hbm(v0), *in_vmem(v2, r1, r2, r3, g), *in_hbm(weight))
+            flops=8 * heads * rows * rows * HD, bytes_accessed=12 << 20,
+            transcendentals=heads * rows * rows,
+        ),
+    )(odd, me, lo, *in_hbm(q), *in_vmem(r1, r2, r3, g), *near, *in_vmem(weight))
 
 
 def grads_kernel(
-    odd_ref, me_ref, lo_ref, prob_ref, att, k0, up, v0, v2, q0, down, r1, r2, r3, g0, g1, g2,
+    odd_ref, me_ref, lo_ref, near_ref, prob_ref, factor_ref, att, k0, up, v0, v2, q0, down, r1, r2, r3, g0, g1, g2,
     s0, s10, s11, s20, s21, dq_ref, dk_ref, dv_ref,
     kc, qc, gc, v1, s1, s2, probs, grad_s, grad_q,
 ):
@@ -300,16 +351,16 @@
                     into[late : late + ROWS, early : early + ROWS] = nothing
                     into[early : early + ROWS, far + late : far + late + ROWS] = nothing
                 grad_q[early : early + ROWS, late : late + ROWS] = nothing
-                grad_q[late : late + ROWS, far + early : far + early + ROWS] = nothing
+                grad_q[late : late + ROWS, rows + early : rows + early + ROWS] = nothing
 
     odd, group = odd_ref[0], me_ref[0] & 1
     tiles = [slice(t * rows, (t + 1) * rows) for t in range(REACH + 1)]
-    pick(odd, r2, r1, kc.at[tiles[1], :])
+    pick(odd, r2, r1, kc.at[tiles[2], :])
     pick(odd, r3, r2, v1)
     pick(odd, r1, r3, qc.at[tiles[1], :])
     pick(group, s10, s11, s1)
     pick(group, s20, s21, s2)
-    pick(group, up, down, kc.at[tiles[2], :])
+    pick(group, up, down, kc.at[tiles[1], :])
     pick(group, down, up, qc.at[tiles[2], :])
     for into, t, ref in (
         (kc, 0, k0), (qc, 0, q0), (gc, 0, g0), (gc, 1, g1), (gc, 2, g2)
@@ -348,16 +399,21 @@
     for t in (0, 2, 1):
         for c in blocks:
             first, last = {0: (c, rows), 1: (0, rows), 2: (0, c + ROWS)}[t]
-            at = t * rows + c
             grad_prob = mm(g0[first:last, :], values[t][c : c + ROWS, :], NT)
-            prob = prob_ref[0, first:last, at : at + ROWS].astype(F32)
-            grad_q[first:last, at : at + ROWS] = (
+            into = {0: 0, 2: rows, 1: 2 * rows}[t] + c
+            if t == 1:
+                prob = prob_ref[0, first:last, c : c + ROWS].astype(F32)
+            else:
+                prob = near_ref[0, first:last, into : into + ROWS].astype(F32)
+            grad_q[first:last, into : into + ROWS] = (
                 prob * (grad_prob - delta[first:last, :])
             ).astype(BF16)
-    dq_ref[...] = (mm(grad_q[...], kc[...], NN) * SCALE).astype(BF16)
-
-
-def grads_call(odd, me, lo, prob, att, k, v, q, received, grads, stats):
+    near = mm(grad_q[:, 0 : 2 * rows], kc[0 : 2 * rows, :], NN)
+    last = mm(grad_q[:, 2 * rows :], kc[2 * rows :, :], NN)
+    dq_ref[...] = ((near * factor_ref[...] + last) * SCALE).astype(BF16)
+
+
+def grads_call(odd, me, lo, near, prob, factor, att, k, v, q, received, grads, stats):
     rows, cols = q[0].shape
     heads = cols // HD
     tile, _, _ = tile_specs(rows)
@@ -374,7 +430,9 @@
             grid=(heads,),
             in_specs=[
                 pl.BlockSpec((REACH + 1, rows), lambda h, odd, me: (0, 0)),
-                pl.BlockSpec((1, rows, span), lambda h, odd, me: (h, 0, 0)),
+                pl.BlockSpec((1, rows, 2 * rows), lambda h, odd, me: (h, 0, 0)),
+                pl.BlockSpec((1, rows, rows), lambda h, odd, me: (h, 0, 0)),
+                tile,
             ]
             + [tile] * 13
             + [stat] * 5,
@@ -390,7 +448,7 @@
             transcendentals=heads * rows * span,
         ),
     )(
-        odd, me, lo, prob, att, hbm[0], vmem[0], hbm[1], vmem[1], hbm[2], vmem[2], *vmem[3:], *stats
+        odd, me, lo, near, prob, factor, att, hbm[0], vmem[0], hbm[1], vmem[1], hbm[2], vmem[2], *vmem[3:], *stats
     )
 
 
@@ -442,15 +500,18 @@
     r3 = exchanged(*payload_call(odd, me, ((1, 0, 2, 2),), *in_vmem(up, down, v2)))
     g1 = exchanged(*payload_call(odd, me, ((0, 0, 1, 1),), *in_vmem(g2, g)))
 
-    attended, prob, stat, sent, kept, kept_far = attend_call(
-        odd, me, lo_col, queries, key_rows, up, down, value_rows, v2, r1, r2, r3, g, out_weight
+    near, *near_rows = near_call(
+        me, lo_col, queries, key_rows, up, down, value_rows, v2
+    )
+    attended, prob, factor, stat, sent, kept, kept_far = attend_call(
+        odd, me, lo_col, queries, r1, r2, r3, g, near_rows, out_weight
     )
     stats = [stat] + [ringed(stat, n, bit) for n in (1, 2) for bit in (0, 1)]
     came = across(sent, 1)
     far = across((kept_far + came[:, cols:].astype(F32)).astype(BF16), 2)
 
     grad_queries, grad_keys, grad_values = grads_call(
-        odd, me, lo_row, prob, attended, (key_rows, up), (value_rows, v2), (queries, down),
+        odd, me, lo_row, near, prob, factor, attended, (key_rows, up), (value_rows, v2), (queries, down),
         (r1, r2, r3), (g, g1, g2), stats,
     )
     mixed = (kept + came[:, :cols].astype(F32) + far.astype(F32)).astype(BF16)

time: 97.3 us -> 87.7 us (0.901)
  Pallas kernels: 39.6 us -> 26.4 us
  waiting for transfers between devices: 35.9 us -> 39.8 us
    pallas_call x4, Pallas kernels: 15.9 us -> 3.3 us  [payload_call(): pl.pallas_call(functools.partial(payload_kernel, table, len(arrays), stag...]
    ppermute x2, waiting for transfers between devices: 12.2 us -> 18.5 us  [passed_along(): return lax.ppermute(shard, axis, pairs)]
    pallas_call x1, Pallas kernels: 10.2 us -> 5.76 us  [attend_call(): pl.pallas_call(attend_kernel, name='attend', out_shape=(jax.ShapeDtypeStr...]
    pallas_call x0 -> x1, Pallas kernels: none -> 4.45 us  [near_call(): pl.pallas_call(near_kernel, name='near', out_shape=(jax.ShapeDtypeStruct(...]
    ppermute x9, waiting for transfers between devices: 11.7 us -> 9.3 us  [swapped(): return lax.ppermute(shard, axis, [(i, i ^ bit) for i in range(length)])]
  transfers between devices with their start and end apart: 17 -> 17, of which waited for: 7 -> 8; matrix products, arithmetic and copies ran while one was open for 0% -> 0% of each run, Pallas kernels for 30% -> 24%
where the time goes in v2:
time: 87.7 us; the launch traced here: 87.3 us
  waiting for transfers between devices  39.8 us (45%)
  Pallas kernels  26.4 us (30%)
  starting transfers between devices  19.1 us (22%)
  other arithmetic  1.14 us (1%)
    ppermute x2, waiting for transfers between devices, passed_along(): return lax.ppermute(shard, axis, pairs)  18.5 us
    ppermute x6, waiting for transfers between devices, ringed(): return lax.ppermute(shard, ('ctx', 'head'), pairs)  12 us
    ppermute x9, waiting for transfers between devices, swapped(): return lax.ppermute(shard, axis, [(i, i ^ bit) for i in range(length)])  9.3 us
    pallas_call x1, Pallas kernels, grads_call(): pl.pallas_call(grads_kernel, name='grads', out_shape=(jax.ShapeDtypeStruc...  9.16 us
    ppermute x9, starting transfers between devices, swapped(): return lax.ppermute(shard, axis, [(i, i ^ bit) for i in range(length)])  8.56 us
    pallas_call x1, Pallas kernels, attend_call(): pl.pallas_call(attend_kernel, name='attend', out_shape=(jax.ShapeDtypeStr...  5.76 us
    ppermute x6, starting transfers between devices, ringed(): return lax.ppermute(shard, ('ctx', 'head'), pairs)  5.34 us
    ppermute x2, starting transfers between devices, passed_along(): return lax.ppermute(shard, axis, pairs)  5.23 us
  transfers between devices with their start and end apart: 17, of which 8 were waited for; matrix products, arithmetic and copies ran while one was open for 0% of the time, Pallas kernels for 24%

profile of v2, /device:TPU:0, one launch (start us, length us, event | category | flops | bytes accessed | tf_op | source)
XLA Modules:
  0.0 87.3 jit_solution(9987690744721101941)
XLA Ops:
  0.6 3.0 %collective-permute-start.7 = (bf16[384,512]{1,0:T(8,128)(2,1)}, bf16[384,512]{1,0:T(8,128)(2,1)S(1)}, u32[]{:S(2)}, u32[]{:S(2)}) collective-permute-start(bf16[384,512]{1,0:T(8,128)(2,1)} %c0.1), channel_id=1, source_target_pairs={{0,2},{1,3},{2,0},{3,1},{4,6},{5,7},{6,4},{7,5},{8,10},{9,11},{10,... | collective-permute-start | bytes 1179656 | tf_op jit(solution)/shard_map/ppermute | solution.py:36
  3.7 1.9 %payload.4 = (bf16[384,512]{1,0:T(8,128)(2,1)}, bf16[384,512]{1,0:T(8,128)(2,1)S(1)}, bf16[384,512]{1,0:T(8,128)(2,1)S(1)}) custom-call(s32[1]{0:T(128)} %bitcast.odd_ref, s32[1]{0:T(128)} %bitcast.1.me_ref, bf16[384,512]{1,0:T(8,128)(2,1)} %k0.3, bf16[384,512]{1,0:T(8,128)(2,1)} %q0.1), custom_call_target="tpu_custom_call" | custom-call | bytes 2359296 | tf_op jit(solution)/shard_map/payload/pallas_call | solution.py:123
  5.6 1.6 %collective-permute-start.1 = (bf16[384,512]{1,0:T(8,128)(2,1)S(1)}, bf16[384,512]{1,0:T(8,128)(2,1)S(1)}, u32[]{:S(2)}, u32[]{:S(2)}) collective-permute-start(bf16[384,512]{1,0:T(8,128)(2,1)S(1)} %get-tuple-element.25), channel_id=1, source_target_pairs={{0,8},{1,0},{2,10},{3,2},{4,12},{5,4},{6,14},{7,6},{8,16},{9,1},{1... | collective-permute-start | bytes 1179656 | tf_op jit(solution)/shard_map/ppermute | solution.py:480
  7.2 3.9 %collective-permute-start.4 = (bf16[384,512]{1,0:T(8,128)(2,1)}, bf16[384,512]{1,0:T(8,128)(2,1)S(1)}, u32[]{:S(2)}, u32[]{:S(2)}) collective-permute-start(bf16[384,512]{1,0:T(8,128)(2,1)} %v0.3), channel_id=1, source_target_pairs={{0,8},{4,12},{8,16},{12,20},{16,24},{20,28},{1,9},{5,13},{9,17},{1... | collective-permute-start | bytes 1179656 | tf_op jit(solution)/shard_map/ppermute | solution.py:31
  11.1 0.1 collective-permute-start.6
  11.2 1.8 %collective-permute-done.7.c2 = bf16[384,512]{1,0:T(8,128)(2,1)S(1)} collective-permute-done((bf16[384,512]{1,0:T(8,128)(2,1)}, bf16[384,512]{1,0:T(8,128)(2,1)S(1)}, u32[]{:S(2)}, u32[]{:S(2)}) %collective-permute-start.7) | collective-permute-done | bytes 393248 | tf_op jit(solution)/shard_map/ppermute | solution.py:36
  13.0 3.7 %collective-permute-done.1.refs_1_.refs_0_.up = bf16[384,512]{1,0:T(8,128)(2,1)S(1)} collective-permute-done((bf16[384,512]{1,0:T(8,128)(2,1)S(1)}, bf16[384,512]{1,0:T(8,128)(2,1)S(1)}, u32[]{:S(2)}, u32[]{:S(2)}) %collective-permute-start.1) | collective-permute-done | bytes 393248 | tf_op jit(solution)/shard_map/ppermute | solution.py:480
  16.7 1.5 %collective-permute-start = (bf16[384,512]{1,0:T(8,128)(2,1)}, bf16[384,512]{1,0:T(8,128)(2,1)S(1)}, u32[]{:S(2)}, u32[]{:S(2)}) collective-permute-start(bf16[384,512]{1,0:T(8,128)(2,1)} %get-tuple-element.24), channel_id=1, source_target_pairs={{0,4},{4,0},{8,12},{12,8},{16,20},{20,16},{24,28},{28,24},{1,5},{5... | collective-permute-start | bytes 1179656 | tf_op jit(solution)/shard_map/ppermute | solution.py:36
  18.2 5.8 %collective-permute-done.4.refs_2_.v2 = bf16[384,512]{1,0:T(8,128)(2,1)S(1)} collective-permute-done((bf16[384,512]{1,0:T(8,128)(2,1)}, bf16[384,512]{1,0:T(8,128)(2,1)S(1)}, u32[]{:S(2)}, u32[]{:S(2)}) %collective-permute-start.4) | collective-permute-done | bytes 393248 | tf_op jit(solution)/shard_map/ppermute | solution.py:31
  24.0 0.2 payload.6
  24.2 1.6 %collective-permute-start.5 = (bf16[384,512]{1,0:T(8,128)(2,1)S(1)}, bf16[384,512]{1,0:T(8,128)(2,1)}, u32[]{:S(2)}, u32[]{:S(2)}) collective-permute-start(bf16[384,512]{1,0:T(8,128)(2,1)S(1)} %payload.6), channel_id=1, source_target_pairs={{0,4},{4,0},{8,12},{12,8},{16,20},{20,16},{24,28},{28,24},{1,5},{5... | collective-permute-start | bytes 1179656 | tf_op jit(solution)/shard_map/ppermute | solution.py:36
  25.8 1.0 %payload.5 = bf16[384,512]{1,0:T(8,128)(2,1)S(1)} custom-call(s32[1]{0:T(128)} %bitcast.odd_ref, s32[1]{0:T(128)} %bitcast.1.me_ref, bf16[384,512]{1,0:T(8,128)(2,1)} %v0.3, bf16[384,512]{1,0:T(8,128)(2,1)S(1)} %collective-permute-done.1.refs_1_.refs_0_.up, bf16[384,512]{1,0:T(8,128)(2,1)S(1)} %collective-permute-done.2.refs_2_.refs_1_.down), custom_call_target="tpu_custom_call" | custom-call | bytes 786432 | tf_op jit(solution)/shard_map/payload/pallas_call | solution.py:123
  26.8 0.1 collective-permute-start.3
  26.9 0.1 pad_add_fusion.base_ref
  26.9 1.0 %windows.1 = (s32[384,128]{1,0:T(8,128)S(1)}, s32[3,384]{1,0:T(4,128)S(1)}) custom-call(s32[2]{0:T(128)S(1)} %pad_add_fusion.base_ref, s32[136]{0:T(256)S(1)} %copy-done.1), custom_call_target="tpu_custom_call" | custom-call | flops 1048576 | bytes 262144 | tf_op jit(solution)/shard_map/windows/pallas_call | solution.py:63
  27.9 4.5 %near.1 = (bf16[4,384,768]{2,1,0:T(8,128)(2,1)S(1)}, f32[384,512]{1,0:T(8,128)S(1)}, f32[384,512]{1,0:T(8,128)S(1)}, f32[384,512]{1,0:T(8,128)S(1)}) custom-call(s32[1]{0:T(128)} %bitcast.1.me_ref, s32[384,128]{1,0:T(8,128)S(1)} %get-tuple-element.23.lo_ref, bf16[384,512]{1,0:T(8,128)(2,1)} %q0.1, bf16[384,512]{1,0:T(8,128)(2,1)} %k0.3, ...), custom_call_target="tpu_custom_call" | custom-call | flops 1207959552 | bytes 10485760 | tf_op jit(solution)/shard_map/near/pallas_call | solution.py:217
  32.4 2.7 %grad_out.1.g.refs_1_.g0 = bf16[384,512]{1,0:T(8,128)(2,1)S(1)} custom-call(s32[1]{0:T(128)} %bitcast.1.me_ref, bf16[384,512]{1,0:T(8,128)(2,1)} %c0.1, bf16[384,512]{1,0:T(8,128)(2,1)S(1)} %collective-permute-done.6.c1, bf16[384,512]{1,0:T(8,128)(2,1)S(1)} %collective-permute-done.7.c2, bf16[384,512]{1,0:T(8,128)(2,1)S(1)} %collective-permute-done.8.c3, ...), custom_call_target="tpu_custom_call" | custom-call | flops 805306368 | bytes 6291456 | tf_op jit(solution)/shard_map/grad_out/pallas_call | solution.py:150
  35.2 1.2 %collective-permute-done.5.r3 = bf16[384,512]{1,0:T(8,128)(2,1)} collective-permute-done((bf16[384,512]{1,0:T(8,128)(2,1)S(1)}, bf16[384,512]{1,0:T(8,128)(2,1)}, u32[]{:S(2)}, u32[]{:S(2)}) %collective-permute-start.5) | collective-permute-done | bytes 393248 | tf_op jit(solution)/shard_map/ppermute | solution.py:36
  36.3 6.3 %collective-permute-done.3.r2 = bf16[384,512]{1,0:T(8,128)(2,1)} collective-permute-done((bf16[384,512]{1,0:T(8,128)(2,1)S(1)}, bf16[384,512]{1,0:T(8,128)(2,1)}, u32[]{:S(2)}, u32[]{:S(2)}) %collective-permute-start.3) | collective-permute-done | bytes 393248 | tf_op jit(solution)/shard_map/ppermute | solution.py:36
  42.7 5.8 %attend.1 = (bf16[384,512]{1,0:T(8,128)(2,1)S(1)}, bf16[4,384,384]{2,1,0:T(8,128)(2,1)S(1)}, f32[384,512]{1,0:T(8,128)S(1)}, f32[4,2,384]{2,1,0:T(2,128)S(1)}, b...) custom-call(s32[1]{0:T(128)} %bitcast.odd_ref, s32[1]{0:T(128)} %bitcast.1.me_ref, ...), custom_call_target="tpu_custom_call" | custom-call | flops 603979776 | bytes 12582912 | tf_op jit(solution)/shard_map/attend/pallas_call | solution.py:299
  48.5 1.3 %collective-permute-start.11 = (bf16[384,512]{1,0:T(8,128)(2,1)S(1)}, bf16[384,512]{1,0:T(8,128)(2,1)S(1)}, u32[]{:S(2)}, u32[]{:S(2)}) collective-permute-start(bf16[384,512]{1,0:T(8,128)(2,1)S(1)} %grad_out.1.g.refs_1_.g0), channel_id=1, source_target_pairs={{8,0},{12,4},{16,8},{20,12},{24,16},{28,20},{9,1},{13,5},{17,9},{2... | collective-permute-start | bytes 1179656 | tf_op jit(solution)/shard_map/ppermute | solution.py:31
  49.8 12.7 %collective-permute-done.11.refs_0_.g2 = bf16[384,512]{1,0:T(8,128)(2,1)S(1)} collective-permute-done((bf16[384,512]{1,0:T(8,128)(2,1)S(1)}, bf16[384,512]{1,0:T(8,128)(2,1)S(1)}, u32[]{:S(2)}, u32[]{:S(2)}) %collective-permute-start.11) | collective-permute-done | bytes 393248 | tf_op jit(solution)/shard_map/ppermute | solution.py:31
  62.6 0.2 payload.7
  62.8 1.6 %collective-permute-start.12 = (bf16[384,512]{1,0:T(8,128)(2,1)S(1)}, bf16[384,512]{1,0:T(8,128)(2,1)S(1)}, u32[]{:S(2)}, u32[]{:S(2)}) collective-permute-start(bf16[384,512]{1,0:T(8,128)(2,1)S(1)} %payload.7), channel_id=1, source_target_pairs={{0,4},{4,0},{8,12},{12,8},{16,20},{20,16},{24,28},{28,24},{1,5},{5... | collective-permute-start | bytes 1179656 | tf_op jit(solution)/shard_map/ppermute | solution.py:36
  64.4 0.1 add_convert_fusion.1
  64.5 0.6 collective-permute-start.10
  65.1 2.0 %collective-permute-start.14 = (f32[4,2,384]{2,1,0:T(2,128)S(1)}, f32[4,2,384]{2,1,0:T(2,128)S(1)}, u32[]{:S(2)}, u32[]{:S(2)}) collective-permute-start(f32[4,2,384]{2,1,0:T(2,128)S(1)} %get-tuple-element.38.s0), channel_id=1, source_target_pairs={{0,4},{1,0},{2,6},{3,2},{4,8},{5,1},{6,10},{7,3},{8,12},{9,5},{10,... | collective-permute-start | bytes 36872 | tf_op jit(solution)/shard_map/ppermute | solution.py:480
  67.1 6.9 %collective-permute-done.13.s10 = f32[4,2,384]{2,1,0:T(2,128)S(1)} collective-permute-done((f32[4,2,384]{2,1,0:T(2,128)S(1)}, f32[4,2,384]{2,1,0:T(2,128)S(1)}, u32[]{:S(2)}, u32[]{:S(2)}) %collective-permute-start.13) | collective-permute-done | bytes 12320 | tf_op jit(solution)/shard_map/ppermute | solution.py:480
  74.0 1.7 %collective-permute-start.16 = (f32[4,2,384]{2,1,0:T(2,128)S(1)}, f32[4,2,384]{2,1,0:T(2,128)S(1)}, u32[]{:S(2)}, u32[]{:S(2)}) collective-permute-start(f32[4,2,384]{2,1,0:T(2,128)S(1)} %get-tuple-element.38.s0), channel_id=1, source_target_pairs={{0,8},{1,0},{2,10},{3,2},{4,12},{5,4},{6,14},{7,6},{8,16},{9,1},{1... | collective-permute-start | bytes 36872 | tf_op jit(solution)/shard_map/ppermute | solution.py:480
  75.8 1.4 %collective-permute-done.16.s21 = f32[4,2,384]{2,1,0:T(2,128)S(1)} collective-permute-done((f32[4,2,384]{2,1,0:T(2,128)S(1)}, f32[4,2,384]{2,1,0:T(2,128)S(1)}, u32[]{:S(2)}, u32[]{:S(2)}) %collective-permute-start.16) | collective-permute-done | bytes 12320 | tf_op jit(solution)/shard_map/ppermute | solution.py:480
  77.2 9.2 %grads.1 = (bf16[384,512]{1,0:T(8,128)(2,1)}, bf16[384,512]{1,0:T(8,128)(2,1)}, bf16[384,512]{1,0:T(8,128)(2,1)}) custom-call(s32[1]{0:T(128)} %bitcast.odd_ref, s32[1]{0:T(128)} %bitcast.1.me_ref, s32[3,384]{1,0:T(4,128)S(1)} %get-tuple-element.33.lo_ref, bf16[4,384,768]{2,1,0:T(8,128)(2,1)S(1)} %get-tuple-element.34.near_ref, ...), custom_call_target="tpu_custom_call" | custom-call | flops 2717908992 | bytes 10485760 | tf_op jit(solution)/shard_map/grads/pallas_call | solution.py:424
  86.3 0.9 %add_convert_fusion = bf16[384,512]{1,0:T(8,128)(2,1)} fusion(bf16[384,512]{1,0:T(8,128)(2,1)S(1)} %collective-permute-done.10, f32[384,512]{1,0:T(8,128)S(1)} %get-tuple-element.30, bf16[384,1024]{1,0:T(8,128)(2,1)S(1)} %collective-permute-done.9), kind=kLoop, calls=%fused_computation | loop fusion | flops 983040 | bytes 1966080 | tf_op jit(solution)/shard_map/convert_element_type | solution.py:517
  (18 shorter events, 0.1 us)
Async XLA Ops:
  0.6 26.3 %copy-start.1 = (s32[136]{0:T(256)S(1)}, s32[136]{0:T(256)}, u32[]{:S(2)}) copy-start(s32[136]{0:T(256)} %offsets_ref.1) | copy-start | bytes 1636
  0.6 12.4 %collective-permute-start.7 = (bf16[384,512]{1,0:T(8,128)(2,1)}, bf16[384,512]{1,0:T(8,128)(2,1)S(1)}, u32[]{:S(2)}, u32[]{:S(2)}) collective-permute-start(bf16[384,512]{1,0:T(8,128)(2,1)} %c0.1), channel_id=1, source_target_pairs={{0,2},{1,3},{2,0},{3,1},{4,6},{5,7},{6,4},{7,5},{8,10},{9,11},{10,... | collective-permute-start | bytes 1179656 | tf_op jit(solution)/shard_map/ppermute | solution.py:36
  5.6 11.1 %collective-permute-start.1 = (bf16[384,512]{1,0:T(8,128)(2,1)S(1)}, bf16[384,512]{1,0:T(8,128)(2,1)S(1)}, u32[]{:S(2)}, u32[]{:S(2)}) collective-permute-start(bf16[384,512]{1,0:T(8,128)(2,1)S(1)} %get-tuple-element.25), channel_id=1, source_target_pairs={{0,8},{1,0},{2,10},{3,2},{4,12},{5,4},{6,14},{7,6},{8,16},{9,1},{1... | collective-permute-start | bytes 1179656 | tf_op jit(solution)/shard_map/ppermute | solution.py:480
  7.2 11.0 %collective-permute-start.2 = (bf16[384,512]{1,0:T(8,128)(2,1)S(1)}, bf16[384,512]{1,0:T(8,128)(2,1)S(1)}, u32[]{:S(2)}, u32[]{:S(2)}) collective-permute-start(bf16[384,512]{1,0:T(8,128)(2,1)S(1)} %get-tuple-element.26), channel_id=1, source_target_pairs={{0,1},{1,9},{2,3},{3,11},{4,5},{5,13},{6,7},{7,15},{8,0},{9,17},{1... | collective-permute-start | bytes 1179656 | tf_op jit(solution)/shard_map/ppermute | solution.py:480
  7.2 16.8 %collective-permute-start.4 = (bf16[384,512]{1,0:T(8,128)(2,1)}, bf16[384,512]{1,0:T(8,128)(2,1)S(1)}, u32[]{:S(2)}, u32[]{:S(2)}) collective-permute-start(bf16[384,512]{1,0:T(8,128)(2,1)} %v0.3), channel_id=1, source_target_pairs={{0,8},{4,12},{8,16},{12,20},{16,24},{20,28},{1,9},{5,13},{9,17},{1... | collective-permute-start | bytes 1179656 | tf_op jit(solution)/shard_map/ppermute | solution.py:31
  11.1 21.3 %collective-permute-start.6 = (bf16[384,512]{1,0:T(8,128)(2,1)}, bf16[384,512]{1,0:T(8,128)(2,1)S(1)}, u32[]{:S(2)}, u32[]{:S(2)}) collective-permute-start(bf16[384,512]{1,0:T(8,128)(2,1)} %c0.1), channel_id=1, source_target_pairs={{0,1},{1,0},{2,3},{3,2},{4,5},{5,4},{6,7},{7,6},{8,9},{9,8},{10,11... | collective-permute-start | bytes 1179656 | tf_op jit(solution)/shard_map/ppermute | solution.py:36
  13.0 19.4 %collective-permute-start.8 = (bf16[384,512]{1,0:T(8,128)(2,1)S(1)}, bf16[384,512]{1,0:T(8,128)(2,1)S(1)}, u32[]{:S(2)}, u32[]{:S(2)}) collective-permute-start(bf16[384,512]{1,0:T(8,128)(2,1)S(1)} %collective-permute-done.7.c2), channel_id=1, source_target_pairs={{0,1},{1,0},{2,3},{3,2},{4,5},{5,4},{6,7},{7,6},{8,9},{9,8},{10,11... | collective-permute-start | bytes 1179656 | tf_op jit(solution)/shard_map/ppermute | solution.py:36
  16.7 18.5 %collective-permute-start = (bf16[384,512]{1,0:T(8,128)(2,1)}, bf16[384,512]{1,0:T(8,128)(2,1)S(1)}, u32[]{:S(2)}, u32[]{:S(2)}) collective-permute-start(bf16[384,512]{1,0:T(8,128)(2,1)} %get-tuple-element.24), channel_id=1, source_target_pairs={{0,4},{4,0},{8,12},{12,8},{16,20},{20,16},{24,28},{28,24},{1,5},{5... | collective-permute-start | bytes 1179656 | tf_op jit(solution)/shard_map/ppermute | solution.py:36
  24.2 12.2 %collective-permute-start.5 = (bf16[384,512]{1,0:T(8,128)(2,1)S(1)}, bf16[384,512]{1,0:T(8,128)(2,1)}, u32[]{:S(2)}, u32[]{:S(2)}) collective-permute-start(bf16[384,512]{1,0:T(8,128)(2,1)S(1)} %payload.6), channel_id=1, source_target_pairs={{0,4},{4,0},{8,12},{12,8},{16,20},{20,16},{24,28},{28,24},{1,5},{5... | collective-permute-start | bytes 1179656 | tf_op jit(solution)/shard_map/ppermute | solution.py:36
  26.8 15.9 %collective-permute-start.3 = (bf16[384,512]{1,0:T(8,128)(2,1)S(1)}, bf16[384,512]{1,0:T(8,128)(2,1)}, u32[]{:S(2)}, u32[]{:S(2)}) collective-permute-start(bf16[384,512]{1,0:T(8,128)(2,1)S(1)} %payload.5), channel_id=1, source_target_pairs={{0,4},{4,0},{8,12},{12,8},{16,20},{20,16},{24,28},{28,24},{1,5},{5... | collective-permute-start | bytes 1179656 | tf_op jit(solution)/shard_map/ppermute | solution.py:36
  32.4 10.3 %copy-start = (bf16[512,2048]{1,0:T(8,128)(2,1)S(1)}, bf16[512,2048]{1,0:T(8,128)(2,1)}, u32[]{:S(2)}) copy-start(bf16[512,2048]{1,0:T(8,128)(2,1)} %w_ref.3) | copy-start | bytes 6291460
  48.4 15.9 %collective-permute-start.9 = (bf16[384,1024]{1,0:T(8,128)(2,1)S(1)}, bf16[384,1024]{1,0:T(8,128)(2,1)S(1)}, u32[]{:S(2)}, u32[]{:S(2)}) collective-permute-start(bf16[384,1024]{1,0:T(8,128)(2,1)S(1)} %get-tuple-element.31), channel_id=1, source_target_pairs={{0,1},{1,0},{2,3},{3,2},{4,5},{5,4},{6,7},{7,6},{8,9},{9,8},{10,11... | collective-permute-start | bytes 2359304 | tf_op jit(solution)/shard_map/ppermute | solution.py:36
  48.5 14.0 %collective-permute-start.11 = (bf16[384,512]{1,0:T(8,128)(2,1)S(1)}, bf16[384,512]{1,0:T(8,128)(2,1)S(1)}, u32[]{:S(2)}, u32[]{:S(2)}) collective-permute-start(bf16[384,512]{1,0:T(8,128)(2,1)S(1)} %grad_out.1.g.refs_1_.g0), channel_id=1, source_target_pairs={{8,0},{12,4},{16,8},{20,12},{24,16},{28,20},{9,1},{13,5},{17,9},{2... | collective-permute-start | bytes 1179656 | tf_op jit(solution)/shard_map/ppermute | solution.py:31
  62.8 14.4 %collective-permute-start.12 = (bf16[384,512]{1,0:T(8,128)(2,1)S(1)}, bf16[384,512]{1,0:T(8,128)(2,1)S(1)}, u32[]{:S(2)}, u32[]{:S(2)}) collective-permute-start(bf16[384,512]{1,0:T(8,128)(2,1)S(1)} %payload.7), channel_id=1, source_target_pairs={{0,4},{4,0},{8,12},{12,8},{16,20},{20,16},{24,28},{28,24},{1,5},{5... | collective-permute-start | bytes 1179656 | tf_op jit(solution)/shard_map/ppermute | solution.py:36
  64.5 21.8 %collective-permute-start.10 = (bf16[384,512]{1,0:T(8,128)(2,1)S(1)}, bf16[384,512]{1,0:T(8,128)(2,1)S(1)}, u32[]{:S(2)}, u32[]{:S(2)}) collective-permute-start(bf16[384,512]{1,0:T(8,128)(2,1)S(1)} %add_convert_fusion.1), channel_id=1, source_target_pairs={{0,2},{1,3},{2,0},{3,1},{4,6},{5,7},{6,4},{7,5},{8,10},{9,11},{10,... | collective-permute-start | bytes 1179656 | tf_op jit(solution)/shard_map/ppermute | solution.py:36
  65.1 8.9 %collective-permute-start.13 = (f32[4,2,384]{2,1,0:T(2,128)S(1)}, f32[4,2,384]{2,1,0:T(2,128)S(1)}, u32[]{:S(2)}, u32[]{:S(2)}) collective-permute-start(f32[4,2,384]{2,1,0:T(2,128)S(1)} %get-tuple-element.38.s0), channel_id=1, source_target_pairs={{0,1},{1,5},{2,3},{3,7},{4,0},{5,9},{6,2},{7,11},{8,4},{9,13},{10,... | collective-permute-start | bytes 36872 | tf_op jit(solution)/shard_map/ppermute | solution.py:480
  65.1 10.6 %collective-permute-start.14 = (f32[4,2,384]{2,1,0:T(2,128)S(1)}, f32[4,2,384]{2,1,0:T(2,128)S(1)}, u32[]{:S(2)}, u32[]{:S(2)}) collective-permute-start(f32[4,2,384]{2,1,0:T(2,128)S(1)} %get-tuple-element.38.s0), channel_id=1, source_target_pairs={{0,4},{1,0},{2,6},{3,2},{4,8},{5,1},{6,10},{7,3},{8,12},{9,5},{10,... | collective-permute-start | bytes 36872 | tf_op jit(solution)/shard_map/ppermute | solution.py:480
  67.1 8.6 %collective-permute-start.15 = (f32[4,2,384]{2,1,0:T(2,128)S(1)}, f32[4,2,384]{2,1,0:T(2,128)S(1)}, u32[]{:S(2)}, u32[]{:S(2)}) collective-permute-start(f32[4,2,384]{2,1,0:T(2,128)S(1)} %get-tuple-element.38.s0), channel_id=1, source_target_pairs={{0,1},{1,9},{2,3},{3,11},{4,5},{5,13},{6,7},{7,15},{8,0},{9,17},{1... | collective-permute-start | bytes 36872 | tf_op jit(solution)/shard_map/ppermute | solution.py:480
  74.0 3.1 %collective-permute-start.16 = (f32[4,2,384]{2,1,0:T(2,128)S(1)}, f32[4,2,384]{2,1,0:T(2,128)S(1)}, u32[]{:S(2)}, u32[]{:S(2)}) collective-permute-start(f32[4,2,384]{2,1,0:T(2,128)S(1)} %get-tuple-element.38.s0), channel_id=1, source_target_pairs={{0,8},{1,0},{2,10},{3,2},{4,12},{5,4},{6,14},{7,6},{8,16},{9,1},{1... | collective-permute-start | bytes 36872 | tf_op jit(solution)/shard_map/ppermute | solution.py:480

commit v3 on v2

--- a/solution.py
+++ b/solution.py
@@ -36,6 +36,9 @@
     return lax.ppermute(shard, axis, [(i, i ^ bit) for i in range(length)])
 
 
+RESIDENT = pl.BlockSpec(memory_space=pltpu.VMEM)
+
+
 def windows_kernel(base_ref, offsets_ref, col_ref, row_ref):
     tiles, rows = row_ref.shape
     lines = tiles * rows // HD
@@ -85,20 +88,9 @@
     return lax.dot_general(a, b, dims, preferred_element_type=F32)
 
 
-def payload_kernel(table, kinds, staged, odd_ref, me_ref, *refs):
+def payload_kernel(table, kinds, odd_ref, me_ref, *refs):
     sources, outs, sems = refs[:kinds], refs[kinds : kinds + len(table)], refs[-1]
     seat = 2 * odd_ref[0] + (me_ref[0] & 1)
-    if staged:
-        stage, stage_sems = refs[-3], refs[-2]
-        loads = [
-            pltpu.make_async_copy(ref, stage.at[kind], stage_sems.at[kind])
-            for kind, ref in enumerate(sources)
-        ]
-        for load in loads:
-            load.start()
-        for load in loads:
-            load.wait()
-        sources = [stage.at[kind] for kind in range(kinds)]
     for n, into in enumerate(outs):
         for kind in range(kinds):
             hits = [seat == place for place in range(4) if table[n][place] == kind]
@@ -112,22 +104,17 @@
         pltpu.make_async_copy(sources[0], into, sems.at[n]).wait()
 
 
-def payload_call(odd, me, table, *arrays, staged=False):
+def payload_call(odd, me, table, *arrays):
     smem, anywhere = pl.BlockSpec(memory_space=pltpu.SMEM), pl.BlockSpec(memory_space=pl.ANY)
     shape = arrays[0].shape
-    staging = []
-    if staged:
-        staging = [
-            pltpu.VMEM((len(arrays),) + shape, BF16), pltpu.SemaphoreType.DMA((len(arrays),))
-        ]
     return pl.pallas_call(
-        functools.partial(payload_kernel, table, len(arrays), staged),
+        functools.partial(payload_kernel, table, len(arrays)),
         name="payload",
         out_shape=(jax.ShapeDtypeStruct(shape, BF16),) * len(table),
         in_specs=[smem, smem] + [anywhere] * len(arrays),
         out_specs=(anywhere,) * len(table),
-        scratch_shapes=staging + [pltpu.SemaphoreType.DMA((len(table),))],
-        compiler_params=pltpu.CompilerParams(vmem_limit_bytes=2 << 20),
+        scratch_shapes=[pltpu.SemaphoreType.DMA((len(table),))],
+        compiler_params=pltpu.CompilerParams(vmem_limit_bytes=1 << 20),
         cost_estimate=pl.CostEstimate(
             flops=0, bytes_accessed=4 * len(table) * shape[0] * shape[1], transcendentals=0
         ),
@@ -154,7 +141,7 @@
         grid_spec=pltpu.PrefetchScalarGridSpec(
             num_scalar_prefetch=1,
             grid=(cols // (2 * HD),),
-            in_specs=[whole] * 4
+            in_specs=[whole] + [RESIDENT] * 3
             + [pl.BlockSpec((2 * HD, weight.shape[1]), lambda h, me: (h, 0))],
             out_specs=pl.BlockSpec((rows, 2 * HD), lambda h, me: (0, h)),
         ),
@@ -167,6 +154,10 @@
 
 def pick(odd, even_ref, odd_ref, into):
     into[...] = jnp.where(odd == 0, even_ref[...], odd_ref[...])
+
+
+def head_cols():
+    return pl.ds(pl.multiple_of(pl.program_id(0) * HD, HD), HD)
 
 
 def spread(column):
@@ -178,6 +169,11 @@
 ):
     rows = q.shape[0]
     blocks = range(0, rows, ROWS)
+    cols = head_cols()
+    head = pl.program_id(0)
+    up, down, v2 = up.at[:, cols], down.at[:, cols], v2.at[:, cols]
+    top_ref, total_ref, sum_ref = (x.at[:, cols] for x in (top_ref, total_ref, sum_ref))
+    prob_ref = prob_ref.at[head]
     pick(me_ref[0] & 1, up, down, k2)
     own = [mm(q[c:rows, :], k0[c : c + ROWS, :], NT) for c in blocks]
     far = [mm(q[0 : c + ROWS, :], k2[c : c + ROWS, :], NT) for c in blocks]
@@ -202,9 +198,9 @@
         exps = [jnp.exp2(x * (SCALE * LOG2E) - shift) for _, x in scores]
         total = jnp.sum(functools.reduce(jnp.add, exps), axis=1, keepdims=True)
         for (place, _), e in zip(scores, exps):
-            prob_ref[0, mine, place : place + HD] = e.astype(BF16)
-        sum_ref[mine, :] = mm(prob_ref[0, mine, 0 : b + ROWS], v0[0 : b + ROWS, :], NN) + mm(
-            prob_ref[0, mine, rows + b : 2 * rows], v2[b:rows, :], NN
+            prob_ref[mine, place : place + HD] = e.astype(BF16)
+        sum_ref[mine, :] = mm(prob_ref[mine, 0 : b + ROWS], v0[0 : b + ROWS, :], NN) + mm(
+            prob_ref[mine, rows + b : 2 * rows], v2[b:rows, :], NN
         )
         top_ref[mine, :] = shift
         total_ref[mine, :] = spread(total)
@@ -222,8 +218,8 @@
         grid_spec=pltpu.PrefetchScalarGridSpec(
             num_scalar_prefetch=1,
             grid=(heads,),
-            in_specs=[pl.BlockSpec((rows, HD), lambda h, me: (0, 0))] + [tile] * 6,
-            out_specs=(pl.BlockSpec((1, rows, 2 * rows), lambda h, me: (h, 0, 0)),) + (tile,) * 3,
+            in_specs=[RESIDENT, tile, tile, RESIDENT, RESIDENT, tile, RESIDENT],
+            out_specs=(RESIDENT,) * 4,
             scratch_shapes=[pltpu.VMEM((rows, HD), BF16)],
         ),
         compiler_params=pltpu.CompilerParams(vmem_limit_bytes=VMEM_BYTES),
@@ -231,7 +227,7 @@
             flops=16 * heads * rows * rows * HD, bytes_accessed=10 << 20,
             transcendentals=2 * heads * rows * rows,
         ),
-    )(me, lo, *in_hbm(q, k0), *in_vmem(up, down), *in_hbm(v0), *in_vmem(v2))
+    )(me, *in_vmem(lo), *in_hbm(q, k0), *in_vmem(up, down), *in_hbm(v0), *in_vmem(v2))
 
 
 def attend_kernel(
@@ -240,6 +236,11 @@
 ):
     rows = q.shape[0]
     head = pl.program_id(0)
+    cols = head_cols()
+    r1, r2, r3, g, near_top, near_total, near_sum, factor_ref = (
+        x.at[:, cols] for x in (r1, r2, r3, g, near_top, near_total, near_sum, factor_ref)
+    )
+    prob_ref, stat_ref = prob_ref.at[head], stat_ref.at[head]
     pick(odd_ref[0], r2, r1, k1)
     pick(odd_ref[0], r3, r2, v1)
     raw = mm(q[...], k1[...], NT)
@@ -260,15 +261,15 @@
         inverse = 1.0 / total
         factor = rescale * inverse
         for n, e in enumerate(exps):
-            prob_ref[0, mine, n * HD : (n + 1) * HD] = (e * inverse).astype(BF16)
-        attended = (near_sum[mine, :] * factor + mm(prob_ref[0, mine, :], v1[...], NN)).astype(BF16)
-        att_ref[mine, pl.ds(pl.multiple_of(head * HD, HD), HD)] = attended
+            prob_ref[mine, n * HD : (n + 1) * HD] = (e * inverse).astype(BF16)
+        attended = (near_sum[mine, :] * factor + mm(prob_ref[mine, :], v1[...], NN)).astype(BF16)
+        att_ref[mine, cols] = attended
         factor_ref[mine, :] = factor
         delta = jnp.sum(attended.astype(F32) * g[mine, :].astype(F32), axis=1, keepdims=True)
         log_total = shift + jnp.log2(total)
         lane = lax.broadcasted_iota(jnp.int32, (ROWS, ROWS), 1)
         stats = jnp.where(lane == 0, log_total, delta).T
-        stat_ref[0, :, mine] = stats[0:2, :]
+        stat_ref[:, mine] = stats[0:2, :]
 
     @pl.when(head == pl.num_programs(0) - 1)
     def _():
@@ -284,18 +285,10 @@
         mine_ref[...] = project(0)
 
 
-def tile_specs(rows):
-    tile = pl.BlockSpec((rows, HD), lambda h, odd, *_: (0, h))
-    on_odd = pl.BlockSpec((rows, HD), lambda h, odd, *_: (0, h * odd[0]))
-    on_even = pl.BlockSpec((rows, HD), lambda h, odd, *_: (0, h * (1 - odd[0])))
-    return tile, on_odd, on_even
-
-
 def attend_call(odd, me, lo, q, r1, r2, r3, g, near, weight):
     rows, cols = q.shape
     heads = cols // HD
-    tile, on_odd, on_even = tile_specs(rows)
-    whole = pl.BlockSpec((rows, cols), lambda h, odd, me: (0, 0))
+    tile = pl.BlockSpec((rows, HD), lambda h, odd, me: (0, h))
     return pl.pallas_call(
         attend_kernel,
         name="attend",
@@ -311,18 +304,8 @@
         grid_spec=pltpu.PrefetchScalarGridSpec(
             num_scalar_prefetch=2,
             grid=(heads,),
-            in_specs=[pl.BlockSpec((rows, HD), lambda h, odd, me: (0, 0))]
-            + [tile, on_odd, tile, on_even, tile, tile, tile, tile]
-            + [pl.BlockSpec(weight.shape, lambda h, odd, me: (0, 0))],
-            out_specs=(
-                whole,
-                pl.BlockSpec((1, rows, rows), lambda h, odd, me: (h, 0, 0)),
-                tile,
-                pl.BlockSpec((1, 2, rows), lambda h, odd, me: (h, 0, 0)),
-                pl.BlockSpec((rows, 2 * cols), lambda h, odd, me: (0, 0)),
-                whole,
-                whole,
-            ),
+            in_specs=[RESIDENT, tile] + [RESIDENT] * 8,
+            out_specs=(RESIDENT,) * 7,
             scratch_shapes=[pltpu.VMEM((rows, HD), BF16)] * 2,
         ),
         compiler_params=pltpu.CompilerParams(vmem_limit_bytes=VMEM_BYTES),
@@ -330,7 +313,7 @@
             flops=8 * heads * rows * rows * HD, bytes_accessed=12 << 20,
             transcendentals=heads * rows * rows,
         ),
-    )(odd, me, lo, *in_hbm(q), *in_vmem(r1, r2, r3, g), *near, *in_vmem(weight))
+    )(odd, me, *in_vmem(lo), *in_hbm(q), *in_vmem(r1, r2, r3, g, *near, weight))
 
 
 def grads_kernel(
@@ -340,6 +323,14 @@
 ):
     rows = g0.shape[0]
     blocks = range(0, rows, ROWS)
+    cols = head_cols()
+    head = pl.program_id(0)
+    factor_ref, att, up, v2, down, r1, r2, r3, g0, g1, g2 = (
+        x.at[:, cols] for x in (factor_ref, att, up, v2, down, r1, r2, r3, g0, g1, g2)
+    )
+    near_ref, prob_ref, s0, s10, s11, s20, s21 = (
+        x.at[head] for x in (near_ref, prob_ref, s0, s10, s11, s20, s21)
+    )
 
     @pl.when(pl.program_id(0) == 0)
     def _():
@@ -377,8 +368,8 @@
             raw = mm(k0[first:last, :], asked, NT)
             grad_prob = mm(values[0][first:last, :], grad, NT)
             lo = lo_ref[t : t + 1, c : c + ROWS]
-            log_total = stats[t][0, 0:1, c : c + ROWS]
-            delta = stats[t][0, 1:2, c : c + ROWS]
+            log_total = stats[t][0:1, c : c + ROWS]
+            delta = stats[t][1:2, c : c + ROWS]
             for r in range(first, last, ROWS):
                 here = slice(r - first, r - first + ROWS)
                 part = raw[here, :]
@@ -402,9 +393,9 @@
             grad_prob = mm(g0[first:last, :], values[t][c : c + ROWS, :], NT)
             into = {0: 0, 2: rows, 1: 2 * rows}[t] + c
             if t == 1:
-                prob = prob_ref[0, first:last, c : c + ROWS].astype(F32)
+                prob = prob_ref[first:last, c : c + ROWS].astype(F32)
             else:
-                prob = near_ref[0, first:last, into : into + ROWS].astype(F32)
+                prob = near_ref[first:last, into : into + ROWS].astype(F32)
             grad_q[first:last, into : into + ROWS] = (
                 prob * (grad_prob - delta[first:last, :])
             ).astype(BF16)
@@ -416,9 +407,8 @@
 def grads_call(odd, me, lo, near, prob, factor, att, k, v, q, received, grads, stats):
     rows, cols = q[0].shape
     heads = cols // HD
-    tile, _, _ = tile_specs(rows)
+    tile = pl.BlockSpec((rows, HD), lambda h, odd, me: (0, h))
     span = (REACH + 1) * rows
-    stat = pl.BlockSpec((1, 2, rows), lambda h, odd, me: (h, 0, 0))
     hbm = in_hbm(k[0], v[0], q[0])
     vmem = in_vmem(k[1], v[1], q[1], *received, *grads)
     return pl.pallas_call(
@@ -428,18 +418,13 @@
         grid_spec=pltpu.PrefetchScalarGridSpec(
             num_scalar_prefetch=2,
             grid=(heads,),
-            in_specs=[
-                pl.BlockSpec((REACH + 1, rows), lambda h, odd, me: (0, 0)),
-                pl.BlockSpec((1, rows, 2 * rows), lambda h, odd, me: (h, 0, 0)),
-                pl.BlockSpec((1, rows, rows), lambda h, odd, me: (h, 0, 0)),
-                tile,
-            ]
-            + [tile] * 13
-            + [stat] * 5,
+            in_specs=[RESIDENT] * 5
+            + [tile, RESIDENT, tile, RESIDENT, tile, RESIDENT]
+            + [RESIDENT] * 11,
             out_specs=(tile,) * 3,
             scratch_shapes=[pltpu.VMEM((span, HD), BF16)] * 3
             + [pltpu.VMEM((rows, HD), BF16)]
-            + [pltpu.VMEM((1, 2, rows), F32)] * 2
+            + [pltpu.VMEM((2, rows), F32)] * 2
             + [pltpu.VMEM((rows, span), BF16)] * 3,
         ),
         compiler_params=pltpu.CompilerParams(vmem_limit_bytes=VMEM_BYTES),
@@ -448,7 +433,8 @@
             transcendentals=heads * rows * span,
         ),
     )(
-        odd, me, lo, near, prob, factor, att, hbm[0], vmem[0], hbm[1], vmem[1], hbm[2], vmem[2], *vmem[3:], *stats
+        odd, me, *in_vmem(lo, near, prob, factor, att),
+        hbm[0], vmem[0], hbm[1], vmem[1], hbm[2], vmem[2], *vmem[3:], *in_vmem(*stats),
     )
 
 
@@ -481,10 +467,10 @@
 
     cot_far = across(cotangent, 2)
     cot_near = across(cotangent, 1)
-    side, up, down = payload_call(
-        odd, me, ((0, 0, 1, 1), (0, 1, 0, 1), (1, 0, 1, 0)), *in_hbm(key_rows, queries),
-        staged=True,
-    )
+    up, down = payload_call(
+        odd, me, ((0, 1, 0, 1), (1, 0, 1, 0)), *in_hbm(key_rows, queries)
+    )
+    (side,) = payload_call(odd, me, ((0, 1, 1, 0),), *in_vmem(up, down))
     up = ringed(up, 2, 1)
     down = ringed(down, 2, 0)
     r1 = exchanged(side)

time: 87.7 us -> 87.1 us (level)
    ppermute x6, waiting for transfers between devices: 12 us -> 10.7 us  [ringed(): return lax.ppermute(shard, ('ctx', 'head'), pairs)]
    ppermute x9, waiting for transfers between devices: 9.3 us -> 10.3 us  [swapped(): return lax.ppermute(shard, axis, [(i, i ^ bit) for i in range(length)])]
    pallas_call x4 -> x5, Pallas kernels: 3.3 us -> 2.73 us  [payload_call(): pl.pallas_call(functools.partial(payload_kernel, table, len(arrays)), nam...]
  transfers between devices with their start and end apart: 17 -> 17, of which waited for: 8 -> 8; matrix products, arithmetic and copies ran while one was open for 0% -> 0% of each run, Pallas kernels for 24% -> 23%
where the time goes in v3:
time: 87.1 us; the launch traced here: 86.6 us
  waiting for transfers between devices  39.6 us (45%)
  Pallas kernels  25.6 us (29%)
  starting transfers between devices  19.4 us (22%)
  other arithmetic  1.15 us (1%)
    ppermute x2, waiting for transfers between devices, passed_along(): return lax.ppermute(shard, axis, pairs)  18.6 us
    ppermute x6, waiting for transfers between devices, ringed(): return lax.ppermute(shard, ('ctx', 'head'), pairs)  10.7 us
    ppermute x9, waiting for transfers between devices, swapped(): return lax.ppermute(shard, axis, [(i, i ^ bit) for i in range(length)])  10.3 us
    pallas_call x1, Pallas kernels, grads_call(): pl.pallas_call(grads_kernel, name='grads', out_shape=(jax.ShapeDtypeStruc...  9.22 us
    ppermute x9, starting transfers between devices, swapped(): return lax.ppermute(shard, axis, [(i, i ^ bit) for i in range(length)])  8.85 us
    pallas_call x1, Pallas kernels, attend_call(): pl.pallas_call(attend_kernel, name='attend', out_shape=(jax.ShapeDtypeStr...  5.74 us
    ppermute x6, starting transfers between devices, ringed(): return lax.ppermute(shard, ('ctx', 'head'), pairs)  5.34 us
    ppermute x2, starting transfers between devices, passed_along(): return lax.ppermute(shard, axis, pairs)  5.23 us
  transfers between devices with their start and end apart: 17, of which 8 were waited for; matrix products, arithmetic and copies ran while one was open for 0% of the time, Pallas kernels for 23%

profile of v3, /device:TPU:0, one launch (start us, length us, event | category | flops | bytes accessed | tf_op | source)
XLA Modules:
  0.0 86.6 jit_solution(2957836832875661441)
XLA Ops:
  0.6 3.0 %collective-permute-start.7 = (bf16[384,512]{1,0:T(8,128)(2,1)}, bf16[384,512]{1,0:T(8,128)(2,1)S(1)}, u32[]{:S(2)}, u32[]{:S(2)}) collective-permute-start(bf16[384,512]{1,0:T(8,128)(2,1)} %c0.1), channel_id=1, source_target_pairs={{0,2},{1,3},{2,0},{3,1},{4,6},{5,7},{6,4},{7,5},{8,10},{9,11},{10,... | collective-permute-start | bytes 1179656 | tf_op jit(solution)/shard_map/ppermute | solution.py:36
  3.7 1.1 %payload.5 = (bf16[384,512]{1,0:T(8,128)(2,1)S(1)}, bf16[384,512]{1,0:T(8,128)(2,1)S(1)}) custom-call(s32[1]{0:T(128)} %bitcast.odd_ref, s32[1]{0:T(128)} %bitcast.1.me_ref, bf16[384,512]{1,0:T(8,128)(2,1)} %k0.3, bf16[384,512]{1,0:T(8,128)(2,1)} %q0.1), custom_call_target="tpu_custom_call" | custom-call | bytes 1572864 | tf_op jit(solution)/shard_map/payload/pallas_call | solution.py:110
  4.8 1.6 %collective-permute-start.1 = (bf16[384,512]{1,0:T(8,128)(2,1)S(1)}, bf16[384,512]{1,0:T(8,128)(2,1)S(1)}, u32[]{:S(2)}, u32[]{:S(2)}) collective-permute-start(bf16[384,512]{1,0:T(8,128)(2,1)S(1)} %get-tuple-element.23.refs_0_), channel_id=1, source_target_pairs={{0,8},{1,0},{2,10},{3,2},{4,12},{5,4},{6,14},{7,6},{8,16},{9,1},{1... | collective-permute-start | bytes 1179656 | tf_op jit(solution)/shard_map/ppermute | solution.py:466
  6.4 3.9 %collective-permute-start.4 = (bf16[384,512]{1,0:T(8,128)(2,1)}, bf16[384,512]{1,0:T(8,128)(2,1)S(1)}, u32[]{:S(2)}, u32[]{:S(2)}) collective-permute-start(bf16[384,512]{1,0:T(8,128)(2,1)} %v0.3), channel_id=1, source_target_pairs={{0,8},{4,12},{8,16},{12,20},{16,24},{20,28},{1,9},{5,13},{9,17},{1... | collective-permute-start | bytes 1179656 | tf_op jit(solution)/shard_map/ppermute | solution.py:31
  10.3 0.1 collective-permute-start.6
  10.4 2.6 %collective-permute-done.7.c2 = bf16[384,512]{1,0:T(8,128)(2,1)S(1)} collective-permute-done((bf16[384,512]{1,0:T(8,128)(2,1)}, bf16[384,512]{1,0:T(8,128)(2,1)S(1)}, u32[]{:S(2)}, u32[]{:S(2)}) %collective-permute-start.7) | collective-permute-done | bytes 393248 | tf_op jit(solution)/shard_map/ppermute | solution.py:36
  13.0 0.2 payload.6
  13.2 2.7 %collective-permute-done.1.refs_1_.refs_0_.up = bf16[384,512]{1,0:T(8,128)(2,1)S(1)} collective-permute-done((bf16[384,512]{1,0:T(8,128)(2,1)S(1)}, bf16[384,512]{1,0:T(8,128)(2,1)S(1)}, u32[]{:S(2)}, u32[]{:S(2)}) %collective-permute-start.1) | collective-permute-done | bytes 393248 | tf_op jit(solution)/shard_map/ppermute | solution.py:466
  15.9 1.5 %collective-permute-start = (bf16[384,512]{1,0:T(8,128)(2,1)S(1)}, bf16[384,512]{1,0:T(8,128)(2,1)}, u32[]{:S(2)}, u32[]{:S(2)}) collective-permute-start(bf16[384,512]{1,0:T(8,128)(2,1)S(1)} %payload.6), channel_id=1, source_target_pairs={{0,4},{4,0},{8,12},{12,8},{16,20},{20,16},{24,28},{28,24},{1,5},{5... | collective-permute-start | bytes 1179656 | tf_op jit(solution)/shard_map/ppermute | solution.py:36
  17.4 5.8 %collective-permute-done.4.refs_2_.v2 = bf16[384,512]{1,0:T(8,128)(2,1)S(1)} collective-permute-done((bf16[384,512]{1,0:T(8,128)(2,1)}, bf16[384,512]{1,0:T(8,128)(2,1)S(1)}, u32[]{:S(2)}, u32[]{:S(2)}) %collective-permute-start.4) | collective-permute-done | bytes 393248 | tf_op jit(solution)/shard_map/ppermute | solution.py:31
  23.2 0.2 payload.8
  23.4 1.6 %collective-permute-start.5 = (bf16[384,512]{1,0:T(8,128)(2,1)S(1)}, bf16[384,512]{1,0:T(8,128)(2,1)}, u32[]{:S(2)}, u32[]{:S(2)}) collective-permute-start(bf16[384,512]{1,0:T(8,128)(2,1)S(1)} %payload.8), channel_id=1, source_target_pairs={{0,4},{4,0},{8,12},{12,8},{16,20},{20,16},{24,28},{28,24},{1,5},{5... | collective-permute-start | bytes 1179656 | tf_op jit(solution)/shard_map/ppermute | solution.py:36
  25.0 1.0 %payload.7 = bf16[384,512]{1,0:T(8,128)(2,1)S(1)} custom-call(s32[1]{0:T(128)} %bitcast.odd_ref, s32[1]{0:T(128)} %bitcast.1.me_ref, bf16[384,512]{1,0:T(8,128)(2,1)} %v0.3, bf16[384,512]{1,0:T(8,128)(2,1)S(1)} %collective-permute-done.1.refs_1_.refs_0_.up, bf16[384,512]{1,0:T(8,128)(2,1)S(1)} %collective-permute-done.2.refs_2_.refs_1_.down), custom_call_target="tpu_custom_call" | custom-call | bytes 786432 | tf_op jit(solution)/shard_map/payload/pallas_call | solution.py:110
  26.1 0.1 pad_add_fusion.base_ref
  26.1 1.0 %windows.1 = (s32[384,128]{1,0:T(8,128)S(1)}, s32[3,384]{1,0:T(4,128)S(1)}) custom-call(s32[2]{0:T(128)S(1)} %pad_add_fusion.base_ref, s32[136]{0:T(256)S(1)} %copy-done.1), custom_call_target="tpu_custom_call" | custom-call | flops 1048576 | bytes 262144 | tf_op jit(solution)/shard_map/windows/pallas_call | solution.py:66
  27.1 4.2 %near.1 = (bf16[4,384,768]{2,1,0:T(8,128)(2,1)S(1)}, f32[384,512]{1,0:T(8,128)S(1)}, f32[384,512]{1,0:T(8,128)S(1)}, f32[384,512]{1,0:T(8,128)S(1)}) custom-call(s32[1]{0:T(128)} %bitcast.1.me_ref, s32[384,128]{1,0:T(8,128)S(1)} %get-tuple-element.22.lo_ref, bf16[384,512]{1,0:T(8,128)(2,1)} %q0.1, bf16[384,512]{1,0:T(8,128)(2,1)} %k0.3, ...), custom_call_target="tpu_custom_call" | custom-call | flops 1207959552 | bytes 10485760 | tf_op jit(solution)/shard_map/near/pallas_call | solution.py:213
  31.4 2.7 %grad_out.1.g.refs_1_.g0 = bf16[384,512]{1,0:T(8,128)(2,1)S(1)} custom-call(s32[1]{0:T(128)} %bitcast.1.me_ref, bf16[384,512]{1,0:T(8,128)(2,1)} %c0.1, bf16[384,512]{1,0:T(8,128)(2,1)S(1)} %collective-permute-done.6.c1, bf16[384,512]{1,0:T(8,128)(2,1)S(1)} %collective-permute-done.7.c2, bf16[384,512]{1,0:T(8,128)(2,1)S(1)} %collective-permute-done.8.c3, ...), custom_call_target="tpu_custom_call" | custom-call | flops 805306368 | bytes 6291456 | tf_op jit(solution)/shard_map/grad_out/pallas_call | solution.py:137
  34.2 1.4 %collective-permute-done.5.r3 = bf16[384,512]{1,0:T(8,128)(2,1)} collective-permute-done((bf16[384,512]{1,0:T(8,128)(2,1)S(1)}, bf16[384,512]{1,0:T(8,128)(2,1)}, u32[]{:S(2)}, u32[]{:S(2)}) %collective-permute-start.5) | collective-permute-done | bytes 393248 | tf_op jit(solution)/shard_map/ppermute | solution.py:36
  35.6 6.3 %collective-permute-done.3.r2 = bf16[384,512]{1,0:T(8,128)(2,1)} collective-permute-done((bf16[384,512]{1,0:T(8,128)(2,1)S(1)}, bf16[384,512]{1,0:T(8,128)(2,1)}, u32[]{:S(2)}, u32[]{:S(2)}) %collective-permute-start.3) | collective-permute-done | bytes 393248 | tf_op jit(solution)/shard_map/ppermute | solution.py:36
  41.9 5.7 %attend.1 = (bf16[384,512]{1,0:T(8,128)(2,1)S(1)}, bf16[4,384,384]{2,1,0:T(8,128)(2,1)S(1)}, f32[384,512]{1,0:T(8,128)S(1)}, f32[4,2,384]{2,1,0:T(2,128)S(1)}, b...) custom-call(s32[1]{0:T(128)} %bitcast.odd_ref, s32[1]{0:T(128)} %bitcast.1.me_ref, ...), custom_call_target="tpu_custom_call" | custom-call | flops 603979776 | bytes 12582912 | tf_op jit(solution)/shard_map/attend/pallas_call | solution.py:292
  47.7 1.3 %collective-permute-start.11 = (bf16[384,512]{1,0:T(8,128)(2,1)S(1)}, bf16[384,512]{1,0:T(8,128)(2,1)S(1)}, u32[]{:S(2)}, u32[]{:S(2)}) collective-permute-start(bf16[384,512]{1,0:T(8,128)(2,1)S(1)} %grad_out.1.g.refs_1_.g0), channel_id=1, source_target_pairs={{8,0},{12,4},{16,8},{20,12},{24,16},{28,20},{9,1},{13,5},{17,9},{2... | collective-permute-start | bytes 1179656 | tf_op jit(solution)/shard_map/ppermute | solution.py:31
  49.0 12.8 %collective-permute-done.11.refs_0_.g2 = bf16[384,512]{1,0:T(8,128)(2,1)S(1)} collective-permute-done((bf16[384,512]{1,0:T(8,128)(2,1)S(1)}, bf16[384,512]{1,0:T(8,128)(2,1)S(1)}, u32[]{:S(2)}, u32[]{:S(2)}) %collective-permute-start.11) | collective-permute-done | bytes 393248 | tf_op jit(solution)/shard_map/ppermute | solution.py:31
  61.9 0.2 payload.9
  62.1 1.6 %collective-permute-start.12 = (bf16[384,512]{1,0:T(8,128)(2,1)S(1)}, bf16[384,512]{1,0:T(8,128)(2,1)S(1)}, u32[]{:S(2)}, u32[]{:S(2)}) collective-permute-start(bf16[384,512]{1,0:T(8,128)(2,1)S(1)} %payload.9), channel_id=1, source_target_pairs={{0,4},{4,0},{8,12},{12,8},{16,20},{20,16},{24,28},{28,24},{1,5},{5... | collective-permute-start | bytes 1179656 | tf_op jit(solution)/shard_map/ppermute | solution.py:36
  63.6 0.1 add_convert_fusion.1
  63.8 0.9 %collective-permute-start.10 = (bf16[384,512]{1,0:T(8,128)(2,1)S(1)}, bf16[384,512]{1,0:T(8,128)(2,1)S(1)}, u32[]{:S(2)}, u32[]{:S(2)}) collective-permute-start(bf16[384,512]{1,0:T(8,128)(2,1)S(1)} %add_convert_fusion.1), channel_id=1, source_target_pairs={{0,2},{1,3},{2,0},{3,1},{4,6},{5,7},{6,4},{7,5},{8,10},{9,11},{10,... | collective-permute-start | bytes 1179656 | tf_op jit(solution)/shard_map/ppermute | solution.py:36
  64.7 2.0 %collective-permute-start.14 = (f32[4,2,384]{2,1,0:T(2,128)S(1)}, f32[4,2,384]{2,1,0:T(2,128)S(1)}, u32[]{:S(2)}, u32[]{:S(2)}) collective-permute-start(f32[4,2,384]{2,1,0:T(2,128)S(1)} %get-tuple-element.36.s0), channel_id=1, source_target_pairs={{0,4},{1,0},{2,6},{3,2},{4,8},{5,1},{6,10},{7,3},{8,12},{9,5},{10,... | collective-permute-start | bytes 36872 | tf_op jit(solution)/shard_map/ppermute | solution.py:466
  66.7 6.6 %collective-permute-done.13.s10 = f32[4,2,384]{2,1,0:T(2,128)S(1)} collective-permute-done((f32[4,2,384]{2,1,0:T(2,128)S(1)}, f32[4,2,384]{2,1,0:T(2,128)S(1)}, u32[]{:S(2)}, u32[]{:S(2)}) %collective-permute-start.13) | collective-permute-done | bytes 12320 | tf_op jit(solution)/shard_map/ppermute | solution.py:466
  73.3 1.7 %collective-permute-start.16 = (f32[4,2,384]{2,1,0:T(2,128)S(1)}, f32[4,2,384]{2,1,0:T(2,128)S(1)}, u32[]{:S(2)}, u32[]{:S(2)}) collective-permute-start(f32[4,2,384]{2,1,0:T(2,128)S(1)} %get-tuple-element.36.s0), channel_id=1, source_target_pairs={{0,8},{1,0},{2,10},{3,2},{4,12},{5,4},{6,14},{7,6},{8,16},{9,1},{1... | collective-permute-start | bytes 36872 | tf_op jit(solution)/shard_map/ppermute | solution.py:466
  75.1 1.4 %collective-permute-done.16.s21 = f32[4,2,384]{2,1,0:T(2,128)S(1)} collective-permute-done((f32[4,2,384]{2,1,0:T(2,128)S(1)}, f32[4,2,384]{2,1,0:T(2,128)S(1)}, u32[]{:S(2)}, u32[]{:S(2)}) %collective-permute-start.16) | collective-permute-done | bytes 12320 | tf_op jit(solution)/shard_map/ppermute | solution.py:466
  76.5 9.2 %grads.1 = (bf16[384,512]{1,0:T(8,128)(2,1)}, bf16[384,512]{1,0:T(8,128)(2,1)}, bf16[384,512]{1,0:T(8,128)(2,1)}) custom-call(s32[1]{0:T(128)} %bitcast.odd_ref, s32[1]{0:T(128)} %bitcast.1.me_ref, s32[3,384]{1,0:T(4,128)S(1)} %get-tuple-element.31.lo_ref, bf16[4,384,768]{2,1,0:T(8,128)(2,1)S(1)} %get-tuple-element.32.near_ref, ...), custom_call_target="tpu_custom_call" | custom-call | flops 2717908992 | bytes 10485760 | tf_op jit(solution)/shard_map/grads/pallas_call | solution.py:414
  85.7 1.0 %add_convert_fusion = bf16[384,512]{1,0:T(8,128)(2,1)} fusion(bf16[384,512]{1,0:T(8,128)(2,1)S(1)} %collective-permute-done.10, f32[384,512]{1,0:T(8,128)S(1)} %get-tuple-element.28, bf16[384,1024]{1,0:T(8,128)(2,1)S(1)} %collective-permute-done.9), kind=kLoop, calls=%fused_computation | loop fusion | flops 983040 | bytes 1966080 | tf_op jit(solution)/shard_map/convert_element_type | solution.py:503
  (19 shorter events, 0.2 us)
Async XLA Ops:
  0.6 12.4 %collective-permute-start.7 = (bf16[384,512]{1,0:T(8,128)(2,1)}, bf16[384,512]{1,0:T(8,128)(2,1)S(1)}, u32[]{:S(2)}, u32[]{:S(2)}) collective-permute-start(bf16[384,512]{1,0:T(8,128)(2,1)} %c0.1), channel_id=1, source_target_pairs={{0,2},{1,3},{2,0},{3,1},{4,6},{5,7},{6,4},{7,5},{8,10},{9,11},{10,... | collective-permute-start | bytes 1179656 | tf_op jit(solution)/shard_map/ppermute | solution.py:36
  4.8 11.1 %collective-permute-start.1 = (bf16[384,512]{1,0:T(8,128)(2,1)S(1)}, bf16[384,512]{1,0:T(8,128)(2,1)S(1)}, u32[]{:S(2)}, u32[]{:S(2)}) collective-permute-start(bf16[384,512]{1,0:T(8,128)(2,1)S(1)} %get-tuple-element.23.refs_0_), channel_id=1, source_target_pairs={{0,8},{1,0},{2,10},{3,2},{4,12},{5,4},{6,14},{7,6},{8,16},{9,1},{1... | collective-permute-start | bytes 1179656 | tf_op jit(solution)/shard_map/ppermute | solution.py:466
  6.4 19.8 %copy-start.1 = (s32[136]{0:T(256)S(1)}, s32[136]{0:T(256)}, u32[]{:S(2)}) copy-start(s32[136]{0:T(256)} %offsets_ref.1) | copy-start | bytes 1636
  6.4 11.0 %collective-permute-start.2 = (bf16[384,512]{1,0:T(8,128)(2,1)S(1)}, bf16[384,512]{1,0:T(8,128)(2,1)S(1)}, u32[]{:S(2)}, u32[]{:S(2)}) collective-permute-start(bf16[384,512]{1,0:T(8,128)(2,1)S(1)} %get-tuple-element.24.refs_1_), channel_id=1, source_target_pairs={{0,1},{1,9},{2,3},{3,11},{4,5},{5,13},{6,7},{7,15},{8,0},{9,17},{1... | collective-permute-start | bytes 1179656 | tf_op jit(solution)/shard_map/ppermute | solution.py:466
  6.4 16.8 %collective-permute-start.4 = (bf16[384,512]{1,0:T(8,128)(2,1)}, bf16[384,512]{1,0:T(8,128)(2,1)S(1)}, u32[]{:S(2)}, u32[]{:S(2)}) collective-permute-start(bf16[384,512]{1,0:T(8,128)(2,1)} %v0.3), channel_id=1, source_target_pairs={{0,8},{4,12},{8,16},{12,20},{16,24},{20,28},{1,9},{5,13},{9,17},{1... | collective-permute-start | bytes 1179656 | tf_op jit(solution)/shard_map/ppermute | solution.py:31
  10.3 21.1 %collective-permute-start.6 = (bf16[384,512]{1,0:T(8,128)(2,1)}, bf16[384,512]{1,0:T(8,128)(2,1)S(1)}, u32[]{:S(2)}, u32[]{:S(2)}) collective-permute-start(bf16[384,512]{1,0:T(8,128)(2,1)} %c0.1), channel_id=1, source_target_pairs={{0,1},{1,0},{2,3},{3,2},{4,5},{5,4},{6,7},{7,6},{8,9},{9,8},{10,11... | collective-permute-start | bytes 1179656 | tf_op jit(solution)/shard_map/ppermute | solution.py:36
  13.0 18.4 %collective-permute-start.8 = (bf16[384,512]{1,0:T(8,128)(2,1)S(1)}, bf16[384,512]{1,0:T(8,128)(2,1)S(1)}, u32[]{:S(2)}, u32[]{:S(2)}) collective-permute-start(bf16[384,512]{1,0:T(8,128)(2,1)S(1)} %collective-permute-done.7.c2), channel_id=1, source_target_pairs={{0,1},{1,0},{2,3},{3,2},{4,5},{5,4},{6,7},{7,6},{8,9},{9,8},{10,11... | collective-permute-start | bytes 1179656 | tf_op jit(solution)/shard_map/ppermute | solution.py:36
  15.9 18.3 %collective-permute-start = (bf16[384,512]{1,0:T(8,128)(2,1)S(1)}, bf16[384,512]{1,0:T(8,128)(2,1)}, u32[]{:S(2)}, u32[]{:S(2)}) collective-permute-start(bf16[384,512]{1,0:T(8,128)(2,1)S(1)} %payload.6), channel_id=1, source_target_pairs={{0,4},{4,0},{8,12},{12,8},{16,20},{20,16},{24,28},{28,24},{1,5},{5... | collective-permute-start | bytes 1179656 | tf_op jit(solution)/shard_map/ppermute | solution.py:36
  23.4 12.2 %collective-permute-start.5 = (bf16[384,512]{1,0:T(8,128)(2,1)S(1)}, bf16[384,512]{1,0:T(8,128)(2,1)}, u32[]{:S(2)}, u32[]{:S(2)}) collective-permute-start(bf16[384,512]{1,0:T(8,128)(2,1)S(1)} %payload.8), channel_id=1, source_target_pairs={{0,4},{4,0},{8,12},{12,8},{16,20},{20,16},{24,28},{28,24},{1,5},{5... | collective-permute-start | bytes 1179656 | tf_op jit(solution)/shard_map/ppermute | solution.py:36
  26.0 15.9 %collective-permute-start.3 = (bf16[384,512]{1,0:T(8,128)(2,1)S(1)}, bf16[384,512]{1,0:T(8,128)(2,1)}, u32[]{:S(2)}, u32[]{:S(2)}) collective-permute-start(bf16[384,512]{1,0:T(8,128)(2,1)S(1)} %payload.7), channel_id=1, source_target_pairs={{0,4},{4,0},{8,12},{12,8},{16,20},{20,16},{24,28},{28,24},{1,5},{5... | collective-permute-start | bytes 1179656 | tf_op jit(solution)/shard_map/ppermute | solution.py:36
  31.4 10.5 %copy-start = (bf16[512,2048]{1,0:T(8,128)(2,1)S(1)}, bf16[512,2048]{1,0:T(8,128)(2,1)}, u32[]{:S(2)}) copy-start(bf16[512,2048]{1,0:T(8,128)(2,1)} %w_ref.3) | copy-start | bytes 6291460
  47.6 16.0 %collective-permute-start.9 = (bf16[384,1024]{1,0:T(8,128)(2,1)S(1)}, bf16[384,1024]{1,0:T(8,128)(2,1)S(1)}, u32[]{:S(2)}, u32[]{:S(2)}) collective-permute-start(bf16[384,1024]{1,0:T(8,128)(2,1)S(1)} %get-tuple-element.29), channel_id=1, source_target_pairs={{0,1},{1,0},{2,3},{3,2},{4,5},{5,4},{6,7},{7,6},{8,9},{9,8},{10,11... | collective-permute-start | bytes 2359304 | tf_op jit(solution)/shard_map/ppermute | solution.py:36
  47.7 14.1 %collective-permute-start.11 = (bf16[384,512]{1,0:T(8,128)(2,1)S(1)}, bf16[384,512]{1,0:T(8,128)(2,1)S(1)}, u32[]{:S(2)}, u32[]{:S(2)}) collective-permute-start(bf16[384,512]{1,0:T(8,128)(2,1)S(1)} %grad_out.1.g.refs_1_.g0), channel_id=1, source_target_pairs={{8,0},{12,4},{16,8},{20,12},{24,16},{28,20},{9,1},{13,5},{17,9},{2... | collective-permute-start | bytes 1179656 | tf_op jit(solution)/shard_map/ppermute | solution.py:31
  62.1 14.4 %collective-permute-start.12 = (bf16[384,512]{1,0:T(8,128)(2,1)S(1)}, bf16[384,512]{1,0:T(8,128)(2,1)S(1)}, u32[]{:S(2)}, u32[]{:S(2)}) collective-permute-start(bf16[384,512]{1,0:T(8,128)(2,1)S(1)} %payload.9), channel_id=1, source_target_pairs={{0,4},{4,0},{8,12},{12,8},{16,20},{20,16},{24,28},{28,24},{1,5},{5... | collective-permute-start | bytes 1179656 | tf_op jit(solution)/shard_map/ppermute | solution.py:36
  63.8 21.9 %collective-permute-start.10 = (bf16[384,512]{1,0:T(8,128)(2,1)S(1)}, bf16[384,512]{1,0:T(8,128)(2,1)S(1)}, u32[]{:S(2)}, u32[]{:S(2)}) collective-permute-start(bf16[384,512]{1,0:T(8,128)(2,1)S(1)} %add_convert_fusion.1), channel_id=1, source_target_pairs={{0,2},{1,3},{2,0},{3,1},{4,6},{5,7},{6,4},{7,5},{8,10},{9,11},{10,... | collective-permute-start | bytes 1179656 | tf_op jit(solution)/shard_map/ppermute | solution.py:36
  64.7 8.6 %collective-permute-start.13 = (f32[4,2,384]{2,1,0:T(2,128)S(1)}, f32[4,2,384]{2,1,0:T(2,128)S(1)}, u32[]{:S(2)}, u32[]{:S(2)}) collective-permute-start(f32[4,2,384]{2,1,0:T(2,128)S(1)} %get-tuple-element.36.s0), channel_id=1, source_target_pairs={{0,1},{1,5},{2,3},{3,7},{4,0},{5,9},{6,2},{7,11},{8,4},{9,13},{10,... | collective-permute-start | bytes 36872 | tf_op jit(solution)/shard_map/ppermute | solution.py:466
  64.7 10.3 %collective-permute-start.14 = (f32[4,2,384]{2,1,0:T(2,128)S(1)}, f32[4,2,384]{2,1,0:T(2,128)S(1)}, u32[]{:S(2)}, u32[]{:S(2)}) collective-permute-start(f32[4,2,384]{2,1,0:T(2,128)S(1)} %get-tuple-element.36.s0), channel_id=1, source_target_pairs={{0,4},{1,0},{2,6},{3,2},{4,8},{5,1},{6,10},{7,3},{8,12},{9,5},{10,... | collective-permute-start | bytes 36872 | tf_op jit(solution)/shard_map/ppermute | solution.py:466
  66.7 8.3 %collective-permute-start.15 = (f32[4,2,384]{2,1,0:T(2,128)S(1)}, f32[4,2,384]{2,1,0:T(2,128)S(1)}, u32[]{:S(2)}, u32[]{:S(2)}) collective-permute-start(f32[4,2,384]{2,1,0:T(2,128)S(1)} %get-tuple-element.36.s0), channel_id=1, source_target_pairs={{0,1},{1,9},{2,3},{3,11},{4,5},{5,13},{6,7},{7,15},{8,0},{9,17},{1... | collective-permute-start | bytes 36872 | tf_op jit(solution)/shard_map/ppermute | solution.py:466
  73.3 3.1 %collective-permute-start.16 = (f32[4,2,384]{2,1,0:T(2,128)S(1)}, f32[4,2,384]{2,1,0:T(2,128)S(1)}, u32[]{:S(2)}, u32[]{:S(2)}) collective-permute-start(f32[4,2,384]{2,1,0:T(2,128)S(1)} %get-tuple-element.36.s0), channel_id=1, source_target_pairs={{0,8},{1,0},{2,10},{3,2},{4,12},{5,4},{6,14},{7,6},{8,16},{9,1},{1... | collective-permute-start | bytes 36872 | tf_op jit(solution)/shard_map/ppermute | solution.py:466

commit v4 on v3

--- a/solution.py
+++ b/solution.py
@@ -165,24 +165,29 @@
 
 
 def near_kernel(
-    me_ref, lo_ref, q, k0, up, down, v0, v2, prob_ref, top_ref, total_ref, sum_ref, k2
+    odd_ref, me_ref, lo_ref, q, k0, up, down, r1, r2, v0, v2,
+    prob_ref, top_ref, total_ref, sum_ref, k1, k2,
 ):
     rows = q.shape[0]
     blocks = range(0, rows, ROWS)
     cols = head_cols()
     head = pl.program_id(0)
-    up, down, v2 = up.at[:, cols], down.at[:, cols], v2.at[:, cols]
+    up, down, r1, r2, v2 = (x.at[:, cols] for x in (up, down, r1, r2, v2))
     top_ref, total_ref, sum_ref = (x.at[:, cols] for x in (top_ref, total_ref, sum_ref))
     prob_ref = prob_ref.at[head]
     pick(me_ref[0] & 1, up, down, k2)
+    pick(odd_ref[0], r2, r1, k1)
     own = [mm(q[c:rows, :], k0[c : c + ROWS, :], NT) for c in blocks]
     far = [mm(q[0 : c + ROWS, :], k2[c : c + ROWS, :], NT) for c in blocks]
+    last = mm(q[...], k1[...], NT)
     for b in blocks:
         mine = slice(b, b + ROWS)
         lo = lo_ref[mine, :]
         scores = []
         for c in blocks:
             lane = lax.broadcasted_iota(jnp.int32, (ROWS, HD), 1)
+            ok = lane + (c - rows) >= lo
+            scores.append((2 * rows + c, jnp.where(ok, last[mine, c : c + HD], NEG_FILL)))
             if c <= b:
                 ok = lane + c >= lo
                 if c == b:
@@ -206,67 +211,52 @@
         total_ref[mine, :] = spread(total)
 
 
-def near_call(me, lo, q, k0, up, down, v0, v2):
+def near_call(odd, me, lo, q, k0, up, down, r1, r2, v0, v2):
     rows, cols = q.shape
     heads = cols // HD
-    tile = pl.BlockSpec((rows, HD), lambda h, me: (0, h))
+    tile = pl.BlockSpec((rows, HD), lambda h, odd, me: (0, h))
     return pl.pallas_call(
         near_kernel,
         name="near",
-        out_shape=(jax.ShapeDtypeStruct((heads, rows, 2 * rows), BF16),)
+        out_shape=(jax.ShapeDtypeStruct((heads, rows, (REACH + 1) * rows), BF16),)
         + (jax.ShapeDtypeStruct((rows, cols), F32),) * 3,
         grid_spec=pltpu.PrefetchScalarGridSpec(
-            num_scalar_prefetch=1,
+            num_scalar_prefetch=2,
             grid=(heads,),
-            in_specs=[RESIDENT, tile, tile, RESIDENT, RESIDENT, tile, RESIDENT],
+            in_specs=[RESIDENT, tile, tile] + [RESIDENT] * 4 + [tile, RESIDENT],
             out_specs=(RESIDENT,) * 4,
-            scratch_shapes=[pltpu.VMEM((rows, HD), BF16)],
+            scratch_shapes=[pltpu.VMEM((rows, HD), BF16)] * 2,
         ),
         compiler_params=pltpu.CompilerParams(vmem_limit_bytes=VMEM_BYTES),
         cost_estimate=pl.CostEstimate(
-            flops=16 * heads * rows * rows * HD, bytes_accessed=10 << 20,
-            transcendentals=2 * heads * rows * rows,
-        ),
-    )(me, *in_vmem(lo), *in_hbm(q, k0), *in_vmem(up, down), *in_hbm(v0), *in_vmem(v2))
+            flops=24 * heads * rows * rows * HD, bytes_accessed=10 << 20,
+            transcendentals=3 * heads * rows * rows,
+        ),
+    )(odd, me, *in_vmem(lo), *in_hbm(q, k0), *in_vmem(up, down, r1, r2), *in_hbm(v0), *in_vmem(v2))
 
 
 def attend_kernel(
-    odd_ref, me_ref, lo_ref, q, r1, r2, r3, g, near_top, near_total, near_sum, w_ref,
-    att_ref, prob_ref, factor_ref, stat_ref, sent_ref, mine_ref, far_ref, k1, v1,
+    odd_ref, me_ref, r2, r3, g, prob_ref, top_ref, total_ref, sum_ref, w_ref,
+    att_ref, factor_ref, stat_ref, sent_ref, mine_ref, far_ref, v1,
 ):
-    rows = q.shape[0]
+    rows = g.shape[0]
     head = pl.program_id(0)
     cols = head_cols()
-    r1, r2, r3, g, near_top, near_total, near_sum, factor_ref = (
-        x.at[:, cols] for x in (r1, r2, r3, g, near_top, near_total, near_sum, factor_ref)
+    r2, r3, g, top_ref, total_ref, sum_ref, factor_ref = (
+        x.at[:, cols] for x in (r2, r3, g, top_ref, total_ref, sum_ref, factor_ref)
     )
     prob_ref, stat_ref = prob_ref.at[head], stat_ref.at[head]
-    pick(odd_ref[0], r2, r1, k1)
     pick(odd_ref[0], r3, r2, v1)
-    raw = mm(q[...], k1[...], NT)
+    last = mm(prob_ref[:, 2 * rows :], v1[...], NN)
     for b in range(0, rows, ROWS):
         mine = slice(b, b + ROWS)
-        lo = lo_ref[mine, :]
-        scores = []
-        for c in range(0, rows, ROWS):
-            lane = lax.broadcasted_iota(jnp.int32, (ROWS, HD), 1)
-            scores.append(jnp.where(lane + (c - rows) >= lo, raw[mine, c : c + HD], NEG_FILL))
-        top = jnp.max(functools.reduce(jnp.maximum, scores), axis=1, keepdims=True)
-        shift = jnp.maximum(spread(top * (SCALE * LOG2E)), near_top[mine, :])
-        exps = [jnp.exp2(s * (SCALE * LOG2E) - shift) for s in scores]
-        rescale = jnp.exp2(near_top[mine, :] - shift)
-        total = rescale * near_total[mine, :] + spread(
-            jnp.sum(functools.reduce(jnp.add, exps), axis=1, keepdims=True)
-        )
-        inverse = 1.0 / total
-        factor = rescale * inverse
-        for n, e in enumerate(exps):
-            prob_ref[mine, n * HD : (n + 1) * HD] = (e * inverse).astype(BF16)
-        attended = (near_sum[mine, :] * factor + mm(prob_ref[mine, :], v1[...], NN)).astype(BF16)
+        total = total_ref[mine, :]
+        factor = 1.0 / total
+        attended = ((sum_ref[mine, :] + last[mine, :]) * factor).astype(BF16)
         att_ref[mine, cols] = attended
         factor_ref[mine, :] = factor
         delta = jnp.sum(attended.astype(F32) * g[mine, :].astype(F32), axis=1, keepdims=True)
-        log_total = shift + jnp.log2(total)
+        log_total = top_ref[mine, :] + jnp.log2(total)
         lane = lax.broadcasted_iota(jnp.int32, (ROWS, ROWS), 1)
         stats = jnp.where(lane == 0, log_total, delta).T
         stat_ref[:, mine] = stats[0:2, :]
@@ -285,16 +275,14 @@
         mine_ref[...] = project(0)
 
 
-def attend_call(odd, me, lo, q, r1, r2, r3, g, near, weight):
-    rows, cols = q.shape
+def attend_call(odd, me, r2, r3, g, scored, weight):
+    rows, cols = g.shape
     heads = cols // HD
-    tile = pl.BlockSpec((rows, HD), lambda h, odd, me: (0, h))
     return pl.pallas_call(
         attend_kernel,
         name="attend",
         out_shape=(
             jax.ShapeDtypeStruct((rows, cols), BF16),
-            jax.ShapeDtypeStruct((heads, rows, rows), BF16),
             jax.ShapeDtypeStruct((rows, cols), F32),
             jax.ShapeDtypeStruct((heads, 2, rows), F32),
             jax.ShapeDtypeStruct((rows, 2 * cols), BF16),
@@ -304,20 +292,20 @@
         grid_spec=pltpu.PrefetchScalarGridSpec(
             num_scalar_prefetch=2,
             grid=(heads,),
-            in_specs=[RESIDENT, tile] + [RESIDENT] * 8,
-            out_specs=(RESIDENT,) * 7,
-            scratch_shapes=[pltpu.VMEM((rows, HD), BF16)] * 2,
+            in_specs=[RESIDENT] * 8,
+            out_specs=(RESIDENT,) * 6,
+            scratch_shapes=[pltpu.VMEM((rows, HD), BF16)],
         ),
         compiler_params=pltpu.CompilerParams(vmem_limit_bytes=VMEM_BYTES),
         cost_estimate=pl.CostEstimate(
             flops=8 * heads * rows * rows * HD, bytes_accessed=12 << 20,
             transcendentals=heads * rows * rows,
         ),
-    )(odd, me, *in_vmem(lo), *in_hbm(q), *in_vmem(r1, r2, r3, g, *near, weight))
+    )(odd, me, *in_vmem(r2, r3, g, *scored, weight))
 
 
 def grads_kernel(
-    odd_ref, me_ref, lo_ref, near_ref, prob_ref, factor_ref, att, k0, up, v0, v2, q0, down, r1, r2, r3, g0, g1, g2,
+    odd_ref, me_ref, lo_ref, prob_ref, factor_ref, att, k0, up, v0, v2, q0, down, r1, r2, r3, g0, g1, g2,
     s0, s10, s11, s20, s21, dq_ref, dk_ref, dv_ref,
     kc, qc, gc, v1, s1, s2, probs, grad_s, grad_q,
 ):
@@ -328,8 +316,8 @@
     factor_ref, att, up, v2, down, r1, r2, r3, g0, g1, g2 = (
         x.at[:, cols] for x in (factor_ref, att, up, v2, down, r1, r2, r3, g0, g1, g2)
     )
-    near_ref, prob_ref, s0, s10, s11, s20, s21 = (
-        x.at[head] for x in (near_ref, prob_ref, s0, s10, s11, s20, s21)
+    prob_ref, s0, s10, s11, s20, s21 = (
+        x.at[head] for x in (prob_ref, s0, s10, s11, s20, s21)
     )
 
     @pl.when(pl.program_id(0) == 0)
@@ -363,8 +351,8 @@
         for c in blocks:
             first, last = {0: (0, c + ROWS), 1: (0, rows), 2: (c, rows)}[t]
             at = t * rows + c
-            asked = qc[at : at + ROWS, :]
-            grad = gc[at : at + ROWS, :]
+            asked = q0[c : c + ROWS, :] if t == 0 else qc[at : at + ROWS, :]
+            grad = (g0, g1, g2)[t][c : c + ROWS, :]
             raw = mm(k0[first:last, :], asked, NT)
             grad_prob = mm(values[0][first:last, :], grad, NT)
             lo = lo_ref[t : t + 1, c : c + ROWS]
@@ -392,19 +380,14 @@
             first, last = {0: (c, rows), 1: (0, rows), 2: (0, c + ROWS)}[t]
             grad_prob = mm(g0[first:last, :], values[t][c : c + ROWS, :], NT)
             into = {0: 0, 2: rows, 1: 2 * rows}[t] + c
-            if t == 1:
-                prob = prob_ref[first:last, c : c + ROWS].astype(F32)
-            else:
-                prob = near_ref[first:last, into : into + ROWS].astype(F32)
+            prob = prob_ref[first:last, into : into + ROWS].astype(F32)
             grad_q[first:last, into : into + ROWS] = (
                 prob * (grad_prob - delta[first:last, :])
             ).astype(BF16)
-    near = mm(grad_q[:, 0 : 2 * rows], kc[0 : 2 * rows, :], NN)
-    last = mm(grad_q[:, 2 * rows :], kc[2 * rows :, :], NN)
-    dq_ref[...] = ((near * factor_ref[...] + last) * SCALE).astype(BF16)
-
-
-def grads_call(odd, me, lo, near, prob, factor, att, k, v, q, received, grads, stats):
+    dq_ref[...] = (mm(grad_q[...], kc[...], NN) * (factor_ref[...] * SCALE)).astype(BF16)
+
+
+def grads_call(odd, me, lo, prob, factor, att, k, v, q, received, grads, stats):
     rows, cols = q[0].shape
     heads = cols // HD
     tile = pl.BlockSpec((rows, HD), lambda h, odd, me: (0, h))
@@ -418,7 +401,7 @@
         grid_spec=pltpu.PrefetchScalarGridSpec(
             num_scalar_prefetch=2,
             grid=(heads,),
-            in_specs=[RESIDENT] * 5
+            in_specs=[RESIDENT] * 4
             + [tile, RESIDENT, tile, RESIDENT, tile, RESIDENT]
             + [RESIDENT] * 11,
             out_specs=(tile,) * 3,
@@ -433,7 +416,7 @@
             transcendentals=heads * rows * span,
         ),
     )(
-        odd, me, *in_vmem(lo, near, prob, factor, att),
+        odd, me, *in_vmem(lo, prob, factor, att),
         hbm[0], vmem[0], hbm[1], vmem[1], hbm[2], vmem[2], *vmem[3:], *in_vmem(*stats),
     )
 
@@ -486,18 +469,18 @@
     r3 = exchanged(*payload_call(odd, me, ((1, 0, 2, 2),), *in_vmem(up, down, v2)))
     g1 = exchanged(*payload_call(odd, me, ((0, 0, 1, 1),), *in_vmem(g2, g)))
 
-    near, *near_rows = near_call(
-        me, lo_col, queries, key_rows, up, down, value_rows, v2
-    )
-    attended, prob, factor, stat, sent, kept, kept_far = attend_call(
-        odd, me, lo_col, queries, r1, r2, r3, g, near_rows, out_weight
+    scored = near_call(
+        odd, me, lo_col, queries, key_rows, up, down, r1, r2, value_rows, v2
+    )
+    attended, factor, stat, sent, kept, kept_far = attend_call(
+        odd, me, r2, r3, g, scored, out_weight
     )
     stats = [stat] + [ringed(stat, n, bit) for n in (1, 2) for bit in (0, 1)]
     came = across(sent, 1)
     far = across((kept_far + came[:, cols:].astype(F32)).astype(BF16), 2)
 
     grad_queries, grad_keys, grad_values = grads_call(
-        odd, me, lo_row, near, prob, factor, attended, (key_rows, up), (value_rows, v2), (queries, down),
+        odd, me, lo_row, scored[0], factor, attended, (key_rows, up), (value_rows, v2), (queries, down),
         (r1, r2, r3), (g, g1, g2), stats,
     )
     mixed = (kept + came[:, :cols].astype(F32) + far.astype(F32)).astype(BF16)

time: 87.1 us -> 90.4 us (1.038)
  Pallas kernels: 25.6 us -> 36.5 us
  waiting for transfers between devices: 39.6 us -> 32.9 us
    pallas_call x5, Pallas kernels: 2.73 us -> 15.3 us  [payload_call(): pl.pallas_call(functools.partial(payload_kernel, table, len(arrays)), nam...]
    ppermute x2, waiting for transfers between devices: 18.6 us -> 12.6 us  [passed_along(): return lax.ppermute(shard, axis, pairs)]
    pallas_call x1, Pallas kernels: 5.74 us -> 2.64 us  [attend_call(): pl.pallas_call(attend_kernel, name='attend', out_shape=(jax.ShapeDtypeStr...]
    ppermute x9, waiting for transfers between devices: 10.3 us -> 8.46 us  [swapped(): return lax.ppermute(shard, axis, [(i, i ^ bit) for i in range(length)])]
    ppermute x6, waiting for transfers between devices: 10.7 us -> 11.8 us  [ringed(): return lax.ppermute(shard, ('ctx', 'head'), pairs)]
  transfers between devices with their start and end apart: 17 -> 17, of which waited for: 8 -> 7; matrix products, arithmetic and copies ran while one was open for 0% -> 0% of each run, Pallas kernels for 23% -> 38%
where the time goes in v4:
time: 90.4 us; the launch traced here: 90.1 us
  Pallas kernels  36.5 us (40%)
  waiting for transfers between devices  32.9 us (36%)
  starting transfers between devices  18.8 us (21%)
  other arithmetic  1.15 us (1%)
    pallas_call x5, Pallas kernels, payload_call(): pl.pallas_call(functools.partial(payload_kernel, table, len(arrays)), nam...  15.3 us
    ppermute x2, waiting for transfers between devices, passed_along(): return lax.ppermute(shard, axis, pairs)  12.6 us
    ppermute x6, waiting for transfers between devices, ringed(): return lax.ppermute(shard, ('ctx', 'head'), pairs)  11.8 us
    pallas_call x1, Pallas kernels, grads_call(): pl.pallas_call(grads_kernel, name='grads', out_shape=(jax.ShapeDtypeStruc...  9.88 us
    ppermute x9, waiting for transfers between devices, swapped(): return lax.ppermute(shard, axis, [(i, i ^ bit) for i in range(length)])  8.46 us
    ppermute x9, starting transfers between devices, swapped(): return lax.ppermute(shard, axis, [(i, i ^ bit) for i in range(length)])  8.2 us
    ppermute x6, starting transfers between devices, ringed(): return lax.ppermute(shard, ('ctx', 'head'), pairs)  5.34 us
    ppermute x2, starting transfers between devices, passed_along(): return lax.ppermute(shard, axis, pairs)  5.23 us
  transfers between devices with their start and end apart: 17, of which 7 were waited for; matrix products, arithmetic and copies ran while one was open for 0% of the time, Pallas kernels for 38%

profile of v4, /device:TPU:0, one launch (start us, length us, event | category | flops | bytes accessed | tf_op | source)
XLA Modules:
  0.0 90.1 jit_solution(10864636787485431908)
XLA Ops:
  0.6 3.0 %collective-permute-start.6 = (bf16[384,512]{1,0:T(8,128)(2,1)}, bf16[384,512]{1,0:T(8,128)(2,1)S(1)}, u32[]{:S(2)}, u32[]{:S(2)}) collective-permute-start(bf16[384,512]{1,0:T(8,128)(2,1)} %c0.1), channel_id=1, source_target_pairs={{0,2},{1,3},{2,0},{3,1},{4,6},{5,7},{6,4},{7,5},{8,10},{9,11},{10,... | collective-permute-start | bytes 1179656 | tf_op jit(solution)/shard_map/ppermute | solution.py:36
  3.7 1.1 %payload.5 = (bf16[384,512]{1,0:T(8,128)(2,1)S(1)}, bf16[384,512]{1,0:T(8,128)(2,1)S(1)}) custom-call(s32[1]{0:T(128)} %bitcast.odd_ref, s32[1]{0:T(128)} %bitcast.1.me_ref, bf16[384,512]{1,0:T(8,128)(2,1)} %k0.3, bf16[384,512]{1,0:T(8,128)(2,1)} %q0.1), custom_call_target="tpu_custom_call" | custom-call | bytes 1572864 | tf_op jit(solution)/shard_map/payload/pallas_call | solution.py:110
  4.8 1.6 %collective-permute-start = (bf16[384,512]{1,0:T(8,128)(2,1)S(1)}, bf16[384,512]{1,0:T(8,128)(2,1)S(1)}, u32[]{:S(2)}, u32[]{:S(2)}) collective-permute-start(bf16[384,512]{1,0:T(8,128)(2,1)S(1)} %get-tuple-element.21.refs_0_), channel_id=1, source_target_pairs={{0,8},{1,0},{2,10},{3,2},{4,12},{5,4},{6,14},{7,6},{8,16},{9,1},{1... | collective-permute-start | bytes 1179656 | tf_op jit(solution)/shard_map/ppermute | solution.py:449
  6.4 3.9 %collective-permute-start.3 = (bf16[384,512]{1,0:T(8,128)(2,1)}, bf16[384,512]{1,0:T(8,128)(2,1)S(1)}, u32[]{:S(2)}, u32[]{:S(2)}) collective-permute-start(bf16[384,512]{1,0:T(8,128)(2,1)} %v0.3), channel_id=1, source_target_pairs={{0,8},{4,12},{8,16},{12,20},{16,24},{20,28},{1,9},{5,13},{9,17},{1... | collective-permute-start | bytes 1179656 | tf_op jit(solution)/shard_map/ppermute | solution.py:31
  10.4 0.1 collective-permute-start.5
  10.4 2.6 %collective-permute-done.6.c2 = bf16[384,512]{1,0:T(8,128)(2,1)S(1)} collective-permute-done((bf16[384,512]{1,0:T(8,128)(2,1)}, bf16[384,512]{1,0:T(8,128)(2,1)S(1)}, u32[]{:S(2)}, u32[]{:S(2)}) %collective-permute-start.6) | collective-permute-done | bytes 393248 | tf_op jit(solution)/shard_map/ppermute | solution.py:36
  13.0 0.2 payload.8
  13.2 2.7 %collective-permute-done.refs_1_.refs_0_.up = bf16[384,512]{1,0:T(8,128)(2,1)S(1)} collective-permute-done((bf16[384,512]{1,0:T(8,128)(2,1)S(1)}, bf16[384,512]{1,0:T(8,128)(2,1)S(1)}, u32[]{:S(2)}, u32[]{:S(2)}) %collective-permute-start) | collective-permute-done | bytes 393248 | tf_op jit(solution)/shard_map/ppermute | solution.py:449
  15.9 1.5 %collective-permute-start.8 = (bf16[384,512]{1,0:T(8,128)(2,1)S(1)}, bf16[384,512]{1,0:T(8,128)(2,1)}, u32[]{:S(2)}, u32[]{:S(2)}) collective-permute-start(bf16[384,512]{1,0:T(8,128)(2,1)S(1)} %payload.8), channel_id=1, source_target_pairs={{0,4},{4,0},{8,12},{12,8},{16,20},{20,16},{24,28},{28,24},{1,5},{5... | collective-permute-start | bytes 1179656 | tf_op jit(solution)/shard_map/ppermute | solution.py:36
  17.4 13.0 %payload.6 = bf16[384,512]{1,0:T(8,128)(2,1)} custom-call(s32[1]{0:T(128)} %bitcast.odd_ref, s32[1]{0:T(128)} %bitcast.1.me_ref, bf16[384,512]{1,0:T(8,128)(2,1)} %v0.3, bf16[384,512]{1,0:T(8,128)(2,1)S(1)} %collective-permute-done.refs_1_.refs_0_.up, bf16[384,512]{1,0:T(8,128)(2,1)S(1)} %collective-permute-done.1.refs_2_.refs_1_.down), custom_call_target="tpu_custom_call" | custom-call | bytes 786432 | tf_op jit(solution)/shard_map/payload/pallas_call | solution.py:110
  30.5 0.8 payload.7
  31.3 2.1 %collective-permute-start.4 = (bf16[384,512]{1,0:T(8,128)(2,1)}, bf16[384,512]{1,0:T(8,128)(2,1)S(1)}, u32[]{:S(2)}, u32[]{:S(2)}) collective-permute-start(bf16[384,512]{1,0:T(8,128)(2,1)} %payload.7), channel_id=1, source_target_pairs={{0,4},{4,0},{8,12},{12,8},{16,20},{20,16},{24,28},{28,24},{1,5},{5... | collective-permute-start | bytes 1179656 | tf_op jit(solution)/shard_map/ppermute | solution.py:36
  33.4 0.1 pad_add_fusion.base_ref
  33.5 1.0 %windows.1 = (s32[384,128]{1,0:T(8,128)S(1)}, s32[3,384]{1,0:T(4,128)S(1)}) custom-call(s32[2]{0:T(128)S(1)} %pad_add_fusion.base_ref, s32[136]{0:T(256)S(1)} %copy-done.1), custom_call_target="tpu_custom_call" | custom-call | flops 1048576 | bytes 262144 | tf_op jit(solution)/shard_map/windows/pallas_call | solution.py:66
  34.5 2.6 %grad_out.1.g.refs_1_.g0 = bf16[384,512]{1,0:T(8,128)(2,1)S(1)} custom-call(s32[1]{0:T(128)} %bitcast.1.me_ref, bf16[384,512]{1,0:T(8,128)(2,1)} %c0.1, bf16[384,512]{1,0:T(8,128)(2,1)S(1)} %collective-permute-done.5.c1, bf16[384,512]{1,0:T(8,128)(2,1)S(1)} %collective-permute-done.6.c2, bf16[384,512]{1,0:T(8,128)(2,1)S(1)} %collective-permute-done.7.c3, ...), custom_call_target="tpu_custom_call" | custom-call | flops 805306368 | bytes 6291456 | tf_op jit(solution)/shard_map/grad_out/pallas_call | solution.py:137
  37.1 5.6 %collective-permute-done.2.r2 = bf16[384,512]{1,0:T(8,128)(2,1)S(1)} collective-permute-done((bf16[384,512]{1,0:T(8,128)(2,1)}, bf16[384,512]{1,0:T(8,128)(2,1)S(1)}, u32[]{:S(2)}, u32[]{:S(2)}) %collective-permute-start.2) | collective-permute-done | bytes 393248 | tf_op jit(solution)/shard_map/ppermute | solution.py:36
  42.7 5.0 %near.1 = (bf16[4,384,1152]{2,1,0:T(8,128)(2,1)S(1)}, f32[384,512]{1,0:T(8,128)S(1)}, f32[384,512]{1,0:T(8,128)S(1)}, f32[384,512]{1,0:T(8,128)S(1)}) custom-call(s32[1]{0:T(128)} %bitcast.odd_ref, s32[1]{0:T(128)} %bitcast.1.me_ref, s32[384,128]{1,0:T(8,128)S(1)} %get-tuple-element.23.lo_ref, bf16[384,512]{1,0:T(8,128)(2,1)} %q0.1, bf16[384,512]{1,0:T(8,128)(2,1)} %k0.3, ...), custom_call_target="tpu_custom_call" | custom-call | flops 1811939328 | bytes 10485760 | tf_op jit(solution)/shard_map/near/pallas_call | solution.py:218
  47.8 0.3 collective-permute-done.4.r3
  48.0 2.6 %attend.1 = (bf16[384,512]{1,0:T(8,128)(2,1)S(1)}, f32[384,512]{1,0:T(8,128)S(1)}, f32[4,2,384]{2,1,0:T(2,128)S(1)}, bf16[384,1024]{1,0:T(8,128)(2,1)S(1)}, f32[...) custom-call(s32[1]{0:T(128)} %bitcast.odd_ref, s32[1]{0:T(128)} %bitcast.1.me_ref, ...), custom_call_target="tpu_custom_call" | custom-call | flops 603979776 | bytes 12582912 | tf_op jit(solution)/shard_map/attend/pallas_call | solution.py:281
  50.7 0.1 collective-permute-start.9
  50.8 1.3 %collective-permute-start.11 = (bf16[384,512]{1,0:T(8,128)(2,1)S(1)}, bf16[384,512]{1,0:T(8,128)(2,1)S(1)}, u32[]{:S(2)}, u32[]{:S(2)}) collective-permute-start(bf16[384,512]{1,0:T(8,128)(2,1)S(1)} %grad_out.1.g.refs_1_.g0), channel_id=1, source_target_pairs={{8,0},{12,4},{16,8},{20,12},{24,16},{28,20},{9,1},{13,5},{17,9},{2... | collective-permute-start | bytes 1179656 | tf_op jit(solution)/shard_map/ppermute | solution.py:31
  52.1 12.6 %collective-permute-done.11.refs_0_.g2 = bf16[384,512]{1,0:T(8,128)(2,1)S(1)} collective-permute-done((bf16[384,512]{1,0:T(8,128)(2,1)S(1)}, bf16[384,512]{1,0:T(8,128)(2,1)S(1)}, u32[]{:S(2)}, u32[]{:S(2)}) %collective-permute-start.11) | collective-permute-done | bytes 393248 | tf_op jit(solution)/shard_map/ppermute | solution.py:31
  64.7 0.2 payload.9
  64.9 0.1 collective-permute-start.12
  65.0 0.1 add_convert_fusion.1
  65.1 1.3 %collective-permute-start.10 = (bf16[384,512]{1,0:T(8,128)(2,1)S(1)}, bf16[384,512]{1,0:T(8,128)(2,1)S(1)}, u32[]{:S(2)}, u32[]{:S(2)}) collective-permute-start(bf16[384,512]{1,0:T(8,128)(2,1)S(1)} %add_convert_fusion.1), channel_id=1, source_target_pairs={{0,2},{1,3},{2,0},{3,1},{4,6},{5,7},{6,4},{7,5},{8,10},{9,11},{10,... | collective-permute-start | bytes 1179656 | tf_op jit(solution)/shard_map/ppermute | solution.py:36
  66.4 2.0 %collective-permute-start.14 = (f32[4,2,384]{2,1,0:T(2,128)S(1)}, f32[4,2,384]{2,1,0:T(2,128)S(1)}, u32[]{:S(2)}, u32[]{:S(2)}) collective-permute-start(f32[4,2,384]{2,1,0:T(2,128)S(1)} %get-tuple-element.34.s0), channel_id=1, source_target_pairs={{0,4},{1,0},{2,6},{3,2},{4,8},{5,1},{6,10},{7,3},{8,12},{9,5},{10,... | collective-permute-start | bytes 36872 | tf_op jit(solution)/shard_map/ppermute | solution.py:449
  68.4 7.7 %collective-permute-done.13.s10 = f32[4,2,384]{2,1,0:T(2,128)S(1)} collective-permute-done((f32[4,2,384]{2,1,0:T(2,128)S(1)}, f32[4,2,384]{2,1,0:T(2,128)S(1)}, u32[]{:S(2)}, u32[]{:S(2)}) %collective-permute-start.13) | collective-permute-done | bytes 12320 | tf_op jit(solution)/shard_map/ppermute | solution.py:449
  76.1 1.7 %collective-permute-start.16 = (f32[4,2,384]{2,1,0:T(2,128)S(1)}, f32[4,2,384]{2,1,0:T(2,128)S(1)}, u32[]{:S(2)}, u32[]{:S(2)}) collective-permute-start(f32[4,2,384]{2,1,0:T(2,128)S(1)} %get-tuple-element.34.s0), channel_id=1, source_target_pairs={{0,8},{1,0},{2,10},{3,2},{4,12},{5,4},{6,14},{7,6},{8,16},{9,1},{1... | collective-permute-start | bytes 36872 | tf_op jit(solution)/shard_map/ppermute | solution.py:449
  77.9 1.4 %collective-permute-done.16.s21 = f32[4,2,384]{2,1,0:T(2,128)S(1)} collective-permute-done((f32[4,2,384]{2,1,0:T(2,128)S(1)}, f32[4,2,384]{2,1,0:T(2,128)S(1)}, u32[]{:S(2)}, u32[]{:S(2)}) %collective-permute-start.16) | collective-permute-done | bytes 12320 | tf_op jit(solution)/shard_map/ppermute | solution.py:449
  79.3 9.9 %grads.1 = (bf16[384,512]{1,0:T(8,128)(2,1)}, bf16[384,512]{1,0:T(8,128)(2,1)}, bf16[384,512]{1,0:T(8,128)(2,1)}) custom-call(s32[1]{0:T(128)} %bitcast.odd_ref, s32[1]{0:T(128)} %bitcast.1.me_ref, s32[3,384]{1,0:T(4,128)S(1)} %get-tuple-element.31.lo_ref, bf16[4,384,1152]{2,1,0:T(8,128)(2,1)S(1)} %get-tuple-element.24.prob_ref, ...), custom_call_target="tpu_custom_call" | custom-call | flops 2717908992 | bytes 10485760 | tf_op jit(solution)/shard_map/grads/pallas_call | solution.py:397
  89.2 1.0 %add_convert_fusion = bf16[384,512]{1,0:T(8,128)(2,1)} fusion(bf16[384,512]{1,0:T(8,128)(2,1)S(1)} %collective-permute-done.10, f32[384,512]{1,0:T(8,128)S(1)} %get-tuple-element.28, bf16[384,1024]{1,0:T(8,128)(2,1)S(1)} %collective-permute-done.9), kind=kLoop, calls=%fused_computation | loop fusion | flops 983040 | bytes 1966080 | tf_op jit(solution)/shard_map/convert_element_type | solution.py:486
  (19 shorter events, 0.1 us)
Async XLA Ops:
  0.6 32.8 %copy-start.1 = (s32[136]{0:T(256)S(1)}, s32[136]{0:T(256)}, u32[]{:S(2)}) copy-start(s32[136]{0:T(256)} %offsets_ref.1) | copy-start | bytes 1636
  0.6 12.4 %collective-permute-start.6 = (bf16[384,512]{1,0:T(8,128)(2,1)}, bf16[384,512]{1,0:T(8,128)(2,1)S(1)}, u32[]{:S(2)}, u32[]{:S(2)}) collective-permute-start(bf16[384,512]{1,0:T(8,128)(2,1)} %c0.1), channel_id=1, source_target_pairs={{0,2},{1,3},{2,0},{3,1},{4,6},{5,7},{6,4},{7,5},{8,10},{9,11},{10,... | collective-permute-start | bytes 1179656 | tf_op jit(solution)/shard_map/ppermute | solution.py:36
  4.8 11.1 %collective-permute-start = (bf16[384,512]{1,0:T(8,128)(2,1)S(1)}, bf16[384,512]{1,0:T(8,128)(2,1)S(1)}, u32[]{:S(2)}, u32[]{:S(2)}) collective-permute-start(bf16[384,512]{1,0:T(8,128)(2,1)S(1)} %get-tuple-element.21.refs_0_), channel_id=1, source_target_pairs={{0,8},{1,0},{2,10},{3,2},{4,12},{5,4},{6,14},{7,6},{8,16},{9,1},{1... | collective-permute-start | bytes 1179656 | tf_op jit(solution)/shard_map/ppermute | solution.py:449
  6.4 11.0 %collective-permute-start.1 = (bf16[384,512]{1,0:T(8,128)(2,1)S(1)}, bf16[384,512]{1,0:T(8,128)(2,1)S(1)}, u32[]{:S(2)}, u32[]{:S(2)}) collective-permute-start(bf16[384,512]{1,0:T(8,128)(2,1)S(1)} %get-tuple-element.22.refs_1_), channel_id=1, source_target_pairs={{0,1},{1,9},{2,3},{3,11},{4,5},{5,13},{6,7},{7,15},{8,0},{9,17},{1... | collective-permute-start | bytes 1179656 | tf_op jit(solution)/shard_map/ppermute | solution.py:449
  6.4 24.1 %collective-permute-start.3 = (bf16[384,512]{1,0:T(8,128)(2,1)}, bf16[384,512]{1,0:T(8,128)(2,1)S(1)}, u32[]{:S(2)}, u32[]{:S(2)}) collective-permute-start(bf16[384,512]{1,0:T(8,128)(2,1)} %v0.3), channel_id=1, source_target_pairs={{0,8},{4,12},{8,16},{12,20},{16,24},{20,28},{1,9},{5,13},{9,17},{1... | collective-permute-start | bytes 1179656 | tf_op jit(solution)/shard_map/ppermute | solution.py:31
  10.4 24.1 %collective-permute-start.5 = (bf16[384,512]{1,0:T(8,128)(2,1)}, bf16[384,512]{1,0:T(8,128)(2,1)S(1)}, u32[]{:S(2)}, u32[]{:S(2)}) collective-permute-start(bf16[384,512]{1,0:T(8,128)(2,1)} %c0.1), channel_id=1, source_target_pairs={{0,1},{1,0},{2,3},{3,2},{4,5},{5,4},{6,7},{7,6},{8,9},{9,8},{10,11... | collective-permute-start | bytes 1179656 | tf_op jit(solution)/shard_map/ppermute | solution.py:36
  13.0 21.5 %collective-permute-start.7 = (bf16[384,512]{1,0:T(8,128)(2,1)S(1)}, bf16[384,512]{1,0:T(8,128)(2,1)S(1)}, u32[]{:S(2)}, u32[]{:S(2)}) collective-permute-start(bf16[384,512]{1,0:T(8,128)(2,1)S(1)} %collective-permute-done.6.c2), channel_id=1, source_target_pairs={{0,1},{1,0},{2,3},{3,2},{4,5},{5,4},{6,7},{7,6},{8,9},{9,8},{10,11... | collective-permute-start | bytes 1179656 | tf_op jit(solution)/shard_map/ppermute | solution.py:36
  15.9 21.2 %collective-permute-start.8 = (bf16[384,512]{1,0:T(8,128)(2,1)S(1)}, bf16[384,512]{1,0:T(8,128)(2,1)}, u32[]{:S(2)}, u32[]{:S(2)}) collective-permute-start(bf16[384,512]{1,0:T(8,128)(2,1)S(1)} %payload.8), channel_id=1, source_target_pairs={{0,4},{4,0},{8,12},{12,8},{16,20},{20,16},{24,28},{28,24},{1,5},{5... | collective-permute-start | bytes 1179656 | tf_op jit(solution)/shard_map/ppermute | solution.py:36
  30.5 12.3 %collective-permute-start.2 = (bf16[384,512]{1,0:T(8,128)(2,1)}, bf16[384,512]{1,0:T(8,128)(2,1)S(1)}, u32[]{:S(2)}, u32[]{:S(2)}) collective-permute-start(bf16[384,512]{1,0:T(8,128)(2,1)} %payload.6), channel_id=1, source_target_pairs={{0,4},{4,0},{8,12},{12,8},{16,20},{20,16},{24,28},{28,24},{1,5},{5... | collective-permute-start | bytes 1179656 | tf_op jit(solution)/shard_map/ppermute | solution.py:36
  31.3 16.7 %collective-permute-start.4 = (bf16[384,512]{1,0:T(8,128)(2,1)}, bf16[384,512]{1,0:T(8,128)(2,1)S(1)}, u32[]{:S(2)}, u32[]{:S(2)}) collective-permute-start(bf16[384,512]{1,0:T(8,128)(2,1)} %payload.7), channel_id=1, source_target_pairs={{0,4},{4,0},{8,12},{12,8},{16,20},{20,16},{24,28},{28,24},{1,5},{5... | collective-permute-start | bytes 1179656 | tf_op jit(solution)/shard_map/ppermute | solution.py:36
  37.1 11.0 %copy-start = (bf16[512,2048]{1,0:T(8,128)(2,1)S(1)}, bf16[512,2048]{1,0:T(8,128)(2,1)}, u32[]{:S(2)}) copy-start(bf16[512,2048]{1,0:T(8,128)(2,1)} %w_ref.3) | copy-start | bytes 6291460
  50.7 14.3 %collective-permute-start.9 = (bf16[384,1024]{1,0:T(8,128)(2,1)S(1)}, bf16[384,1024]{1,0:T(8,128)(2,1)S(1)}, u32[]{:S(2)}, u32[]{:S(2)}) collective-permute-start(bf16[384,1024]{1,0:T(8,128)(2,1)S(1)} %get-tuple-element.29), channel_id=1, source_target_pairs={{0,1},{1,0},{2,3},{3,2},{4,5},{5,4},{6,7},{7,6},{8,9},{9,8},{10,11... | collective-permute-start | bytes 2359304 | tf_op jit(solution)/shard_map/ppermute | solution.py:36
  50.8 13.9 %collective-permute-start.11 = (bf16[384,512]{1,0:T(8,128)(2,1)S(1)}, bf16[384,512]{1,0:T(8,128)(2,1)S(1)}, u32[]{:S(2)}, u32[]{:S(2)}) collective-permute-start(bf16[384,512]{1,0:T(8,128)(2,1)S(1)} %grad_out.1.g.refs_1_.g0), channel_id=1, source_target_pairs={{8,0},{12,4},{16,8},{20,12},{24,16},{28,20},{9,1},{13,5},{17,9},{2... | collective-permute-start | bytes 1179656 | tf_op jit(solution)/shard_map/ppermute | solution.py:31
  64.9 14.4 %collective-permute-start.12 = (bf16[384,512]{1,0:T(8,128)(2,1)S(1)}, bf16[384,512]{1,0:T(8,128)(2,1)S(1)}, u32[]{:S(2)}, u32[]{:S(2)}) collective-permute-start(bf16[384,512]{1,0:T(8,128)(2,1)S(1)} %payload.9), channel_id=1, source_target_pairs={{0,4},{4,0},{8,12},{12,8},{16,20},{20,16},{24,28},{28,24},{1,5},{5... | collective-permute-start | bytes 1179656 | tf_op jit(solution)/shard_map/ppermute | solution.py:36
  65.1 24.1 %collective-permute-start.10 = (bf16[384,512]{1,0:T(8,128)(2,1)S(1)}, bf16[384,512]{1,0:T(8,128)(2,1)S(1)}, u32[]{:S(2)}, u32[]{:S(2)}) collective-permute-start(bf16[384,512]{1,0:T(8,128)(2,1)S(1)} %add_convert_fusion.1), channel_id=1, source_target_pairs={{0,2},{1,3},{2,0},{3,1},{4,6},{5,7},{6,4},{7,5},{8,10},{9,11},{10,... | collective-permute-start | bytes 1179656 | tf_op jit(solution)/shard_map/ppermute | solution.py:36
  66.4 9.7 %collective-permute-start.13 = (f32[4,2,384]{2,1,0:T(2,128)S(1)}, f32[4,2,384]{2,1,0:T(2,128)S(1)}, u32[]{:S(2)}, u32[]{:S(2)}) collective-permute-start(f32[4,2,384]{2,1,0:T(2,128)S(1)} %get-tuple-element.34.s0), channel_id=1, source_target_pairs={{0,1},{1,5},{2,3},{3,7},{4,0},{5,9},{6,2},{7,11},{8,4},{9,13},{10,... | collective-permute-start | bytes 36872 | tf_op jit(solution)/shard_map/ppermute | solution.py:449
  66.4 11.5 %collective-permute-start.14 = (f32[4,2,384]{2,1,0:T(2,128)S(1)}, f32[4,2,384]{2,1,0:T(2,128)S(1)}, u32[]{:S(2)}, u32[]{:S(2)}) collective-permute-start(f32[4,2,384]{2,1,0:T(2,128)S(1)} %get-tuple-element.34.s0), channel_id=1, source_target_pairs={{0,4},{1,0},{2,6},{3,2},{4,8},{5,1},{6,10},{7,3},{8,12},{9,5},{10,... | collective-permute-start | bytes 36872 | tf_op jit(solution)/shard_map/ppermute | solution.py:449
  68.4 9.4 %collective-permute-start.15 = (f32[4,2,384]{2,1,0:T(2,128)S(1)}, f32[4,2,384]{2,1,0:T(2,128)S(1)}, u32[]{:S(2)}, u32[]{:S(2)}) collective-permute-start(f32[4,2,384]{2,1,0:T(2,128)S(1)} %get-tuple-element.34.s0), channel_id=1, source_target_pairs={{0,1},{1,9},{2,3},{3,11},{4,5},{5,13},{6,7},{7,15},{8,0},{9,17},{1... | collective-permute-start | bytes 36872 | tf_op jit(solution)/shard_map/ppermute | solution.py:449
  76.1 3.1 %collective-permute-start.16 = (f32[4,2,384]{2,1,0:T(2,128)S(1)}, f32[4,2,384]{2,1,0:T(2,128)S(1)}, u32[]{:S(2)}, u32[]{:S(2)}) collective-permute-start(f32[4,2,384]{2,1,0:T(2,128)S(1)} %get-tuple-element.34.s0), channel_id=1, source_target_pairs={{0,8},{1,0},{2,10},{3,2},{4,12},{5,4},{6,14},{7,6},{8,16},{9,1},{1... | collective-permute-start | bytes 36872 | tf_op jit(solution)/shard_map/ppermute | solution.py:449

commit v5 on v4

--- a/solution.py
+++ b/solution.py
@@ -121,35 +121,36 @@
     )(odd, me, *arrays)
 
 
-def grad_out_kernel(me_ref, c0, c1, c2, c3, w_ref, out_ref):
-    cols = c0.shape[1]
-    total = None
-    for s, c in enumerate((c0, c1, c2, c3)):
-        start = pl.multiple_of((me_ref[0] ^ s) * cols, cols)
-        part = mm(c[...], w_ref[:, pl.ds(start, cols)], NT)
+def grad_out_kernel(groups, me_ref, w_ref, *refs):
+    shards, base, out_ref = refs[: len(groups)], refs[len(groups) : -1], refs[-1]
+    cols = shards[0].shape[1]
+    width = 2 * HD
+    step = pl.ds(pl.multiple_of(pl.program_id(0) * width, width), width)
+    total = base[0][:, step] if base else None
+    for group, shard in zip(groups, shards):
+        start = pl.multiple_of((me_ref[0] ^ group) * cols, cols)
+        part = mm(shard[...], w_ref[step, pl.ds(start, cols)], NT)
         total = part if total is None else total + part
-    out_ref[...] = total.astype(BF16)
-
-
-def grad_out_call(me, shards, weight):
+    out_ref[:, step] = total.astype(out_ref.dtype)
+
+
+def grad_out_call(me, weight, groups, shards, base, dtype):
     rows, cols = shards[0].shape
-    whole = pl.BlockSpec((rows, cols), lambda h, me: (0, 0))
-    return pl.pallas_call(
-        grad_out_kernel,
-        name="grad_out",
-        out_shape=jax.ShapeDtypeStruct((rows, cols), BF16),
+    operands = in_vmem(weight, *shards, *base)
+    return pl.pallas_call(
+        functools.partial(grad_out_kernel, groups),
+        out_shape=jax.ShapeDtypeStruct((rows, cols), dtype),
         grid_spec=pltpu.PrefetchScalarGridSpec(
             num_scalar_prefetch=1,
             grid=(cols // (2 * HD),),
-            in_specs=[whole] + [RESIDENT] * 3
-            + [pl.BlockSpec((2 * HD, weight.shape[1]), lambda h, me: (h, 0))],
-            out_specs=pl.BlockSpec((rows, 2 * HD), lambda h, me: (0, h)),
+            in_specs=[RESIDENT] * len(operands),
+            out_specs=RESIDENT,
         ),
         compiler_params=pltpu.CompilerParams(vmem_limit_bytes=VMEM_BYTES),
         cost_estimate=pl.CostEstimate(
-            flops=2 * rows * cols * weight.shape[1], bytes_accessed=6 << 20, transcendentals=0
-        ),
-    )(me, *in_hbm(shards[0]), *in_vmem(*shards[1:]), *in_hbm(weight))
+            flops=2 * len(groups) * rows * cols * cols, bytes_accessed=3 << 20, transcendentals=0
+        ),
+    )(me, *operands)
 
 
 def pick(odd, even_ref, odd_ref, into):
@@ -304,121 +305,164 @@
     )(odd, me, *in_vmem(r2, r3, g, *scored, weight))
 
 
-def grads_kernel(
-    odd_ref, me_ref, lo_ref, prob_ref, factor_ref, att, k0, up, v0, v2, q0, down, r1, r2, r3, g0, g1, g2,
-    s0, s10, s11, s20, s21, dq_ref, dk_ref, dv_ref,
-    kc, qc, gc, v1, s1, s2, probs, grad_s, grad_q,
+def weigh(raw, grad_prob, first, c, same, lo, stat, probs, grad_s, at):
+    log_total, delta = stat[0:1, c : c + ROWS], stat[1:2, c : c + ROWS]
+    for r in range(first, first + raw.shape[0], ROWS):
+        here = slice(r - first, r - first + ROWS)
+        part = raw[here, :]
+        pos = r + lax.broadcasted_iota(jnp.int32, part.shape, 0)
+        ok = pos >= lo
+        if same and r == c:
+            ok &= pos <= c + lax.broadcasted_iota(jnp.int32, part.shape, 1)
+        prob = jnp.where(ok, jnp.exp2(part * (SCALE * LOG2E) - log_total), 0.0)
+        probs[r : r + ROWS, at : at + ROWS] = prob.astype(BF16)
+        grad_s[r : r + ROWS, at : at + ROWS] = (prob * (grad_prob[here, :] - delta)).astype(BF16)
+
+
+def grads_own_kernel(
+    odd_ref, me_ref, lo_ref, prob_ref, factor_ref, att, stat, up, down, v2, r1, r2, r3, g0,
+    k0, v0, q0, dq_ref, dk_ref, dv_ref, kc, v1, probs, grad_s, grad_q,
 ):
     rows = g0.shape[0]
     blocks = range(0, rows, ROWS)
     cols = head_cols()
     head = pl.program_id(0)
-    factor_ref, att, up, v2, down, r1, r2, r3, g0, g1, g2 = (
-        x.at[:, cols] for x in (factor_ref, att, up, v2, down, r1, r2, r3, g0, g1, g2)
-    )
-    prob_ref, s0, s10, s11, s20, s21 = (
-        x.at[head] for x in (prob_ref, s0, s10, s11, s20, s21)
-    )
-
-    @pl.when(pl.program_id(0) == 0)
+    factor_ref, att, up, down, v2, r1, r2, r3, g0, dk_ref, dv_ref = (
+        x.at[:, cols] for x in (factor_ref, att, up, down, v2, r1, r2, r3, g0, dk_ref, dv_ref)
+    )
+    prob_ref, stat = prob_ref.at[head], stat.at[head]
+
+    @pl.when(head == 0)
     def _():
         nothing = jnp.zeros((ROWS, ROWS), BF16)
         for early in blocks:
             for late in range(early + ROWS, rows, ROWS):
-                far = 2 * rows
                 for into in (probs, grad_s):
                     into[late : late + ROWS, early : early + ROWS] = nothing
-                    into[early : early + ROWS, far + late : far + late + ROWS] = nothing
                 grad_q[early : early + ROWS, late : late + ROWS] = nothing
                 grad_q[late : late + ROWS, rows + early : rows + early + ROWS] = nothing
 
-    odd, group = odd_ref[0], me_ref[0] & 1
-    tiles = [slice(t * rows, (t + 1) * rows) for t in range(REACH + 1)]
-    pick(odd, r2, r1, kc.at[tiles[2], :])
-    pick(odd, r3, r2, v1)
-    pick(odd, r1, r3, qc.at[tiles[1], :])
-    pick(group, s10, s11, s1)
-    pick(group, s20, s21, s2)
-    pick(group, up, down, kc.at[tiles[1], :])
-    pick(group, down, up, qc.at[tiles[2], :])
-    for into, t, ref in (
-        (kc, 0, k0), (qc, 0, q0), (gc, 0, g0), (gc, 1, g1), (gc, 2, g2)
-    ):
-        into[tiles[t], :] = ref[...]
-    values, stats = (v0, v1, v2), (s0, s1, s2)
-
-    for t in (0, 2, 1):
-        for c in blocks:
-            first, last = {0: (0, c + ROWS), 1: (0, rows), 2: (c, rows)}[t]
-            at = t * rows + c
-            asked = q0[c : c + ROWS, :] if t == 0 else qc[at : at + ROWS, :]
-            grad = (g0, g1, g2)[t][c : c + ROWS, :]
-            raw = mm(k0[first:last, :], asked, NT)
-            grad_prob = mm(values[0][first:last, :], grad, NT)
-            lo = lo_ref[t : t + 1, c : c + ROWS]
-            log_total = stats[t][0:1, c : c + ROWS]
-            delta = stats[t][1:2, c : c + ROWS]
-            for r in range(first, last, ROWS):
-                here = slice(r - first, r - first + ROWS)
-                part = raw[here, :]
-                pos = r + lax.broadcasted_iota(jnp.int32, part.shape, 0)
-                ok = pos >= lo
-                if t == 0 and r == c:
-                    ok &= pos <= c + lax.broadcasted_iota(jnp.int32, part.shape, 1)
-                prob = jnp.where(ok, jnp.exp2(part * (SCALE * LOG2E) - log_total), 0.0)
-                probs[r : r + ROWS, at : at + ROWS] = prob.astype(BF16)
-                grad_s[r : r + ROWS, at : at + ROWS] = (
-                    prob * (grad_prob[here, :] - delta)
-                ).astype(BF16)
-    dk_ref[...] = (mm(grad_s[...], qc[...], NN) * SCALE).astype(BF16)
-    dv_ref[...] = mm(probs[...], gc[...], NN).astype(BF16)
+    kc[0:rows, :] = k0[...]
+    pick(me_ref[0] & 1, up, down, kc.at[rows : 2 * rows, :])
+    pick(odd_ref[0], r2, r1, kc.at[2 * rows : 3 * rows, :])
+    pick(odd_ref[0], r3, r2, v1)
 
     product = att[...].astype(F32) * g0[...].astype(F32)
-    delta = jnp.broadcast_to(jnp.sum(product, axis=1, keepdims=True), (rows, HD))
-    for t in (0, 2, 1):
+    delta = spread(jnp.sum(product, axis=1, keepdims=True))
+    for t, values in ((0, v0), (2, v2), (1, v1)):
         for c in blocks:
             first, last = {0: (c, rows), 1: (0, rows), 2: (0, c + ROWS)}[t]
-            grad_prob = mm(g0[first:last, :], values[t][c : c + ROWS, :], NT)
+            grad_prob = mm(g0[first:last, :], values[c : c + ROWS, :], NT)
             into = {0: 0, 2: rows, 1: 2 * rows}[t] + c
             prob = prob_ref[first:last, into : into + ROWS].astype(F32)
             grad_q[first:last, into : into + ROWS] = (
                 prob * (grad_prob - delta[first:last, :])
             ).astype(BF16)
+
+    for c in blocks:
+        raw = mm(k0[0 : c + ROWS, :], q0[c : c + ROWS, :], NT)
+        grad_prob = mm(v0[0 : c + ROWS, :], g0[c : c + ROWS, :], NT)
+        weigh(raw, grad_prob, 0, c, True, lo_ref[0:1, c : c + ROWS], stat, probs, grad_s, c)
     dq_ref[...] = (mm(grad_q[...], kc[...], NN) * (factor_ref[...] * SCALE)).astype(BF16)
-
-
-def grads_call(odd, me, lo, prob, factor, att, k, v, q, received, grads, stats):
-    rows, cols = q[0].shape
+    dk_ref[...] = mm(grad_s[...], q0[...], NN)
+    dv_ref[...] = mm(probs[...], g0[...], NN)
+
+
+def grads_own_call(odd, me, lo, prob, factor, att, stat, up, down, v2, received, g, k, v, q):
+    rows, cols = q.shape
     heads = cols // HD
     tile = pl.BlockSpec((rows, HD), lambda h, odd, me: (0, h))
     span = (REACH + 1) * rows
-    hbm = in_hbm(k[0], v[0], q[0])
-    vmem = in_vmem(k[1], v[1], q[1], *received, *grads)
-    return pl.pallas_call(
-        grads_kernel,
-        name="grads",
-        out_shape=(jax.ShapeDtypeStruct((rows, cols), BF16),) * 3,
+    vmem = in_vmem(lo, prob, factor, att, stat, up, down, v2, *received, g)
+    return pl.pallas_call(
+        grads_own_kernel,
+        name="grads_own",
+        out_shape=(jax.ShapeDtypeStruct((rows, cols), BF16),)
+        + (jax.ShapeDtypeStruct((rows, cols), F32),) * 2,
         grid_spec=pltpu.PrefetchScalarGridSpec(
             num_scalar_prefetch=2,
             grid=(heads,),
-            in_specs=[RESIDENT] * 4
-            + [tile, RESIDENT, tile, RESIDENT, tile, RESIDENT]
-            + [RESIDENT] * 11,
-            out_specs=(tile,) * 3,
-            scratch_shapes=[pltpu.VMEM((span, HD), BF16)] * 3
-            + [pltpu.VMEM((rows, HD), BF16)]
-            + [pltpu.VMEM((2, rows), F32)] * 2
-            + [pltpu.VMEM((rows, span), BF16)] * 3,
+            in_specs=[RESIDENT] * len(vmem) + [tile] * 3,
+            out_specs=(tile, RESIDENT, RESIDENT),
+            scratch_shapes=[
+                pltpu.VMEM((span, HD), BF16), pltpu.VMEM((rows, HD), BF16),
+                pltpu.VMEM((rows, rows), BF16), pltpu.VMEM((rows, rows), BF16),
+                pltpu.VMEM((rows, span), BF16),
+            ],
         ),
         compiler_params=pltpu.CompilerParams(vmem_limit_bytes=VMEM_BYTES),
         cost_estimate=pl.CostEstimate(
-            flops=12 * heads * rows * span * HD, bytes_accessed=10 << 20,
+            flops=8 * heads * rows * span * HD, bytes_accessed=10 << 20,
+            transcendentals=heads * rows * rows,
+        ),
+    )(odd, me, *vmem, *in_hbm(k, v, q))
+
+
+def grads_far_kernel(
+    odd_ref, me_ref, lo_ref, up, down, r1, r3, g1, g2, s10, s11, s20, s21, dk0, dv0,
+    k0, v0, dk_ref, dv_ref, qc, gc, s1, s2, probs, grad_s,
+):
+    rows = k0.shape[0]
+    blocks = range(0, rows, ROWS)
+    cols = head_cols()
+    head = pl.program_id(0)
+    up, down, r1, r3, g1, g2, dk0, dv0 = (
+        x.at[:, cols] for x in (up, down, r1, r3, g1, g2, dk0, dv0)
+    )
+    s10, s11, s20, s21 = (x.at[head] for x in (s10, s11, s20, s21))
+
+    @pl.when(head == 0)
+    def _():
+        nothing = jnp.zeros((ROWS, ROWS), BF16)
+        for early in blocks:
+            for late in range(early + ROWS, rows, ROWS):
+                for into in (probs, grad_s):
+                    into[early : early + ROWS, rows + late : rows + late + ROWS] = nothing
+
+    group = me_ref[0] & 1
+    pick(group, s20, s21, s2)
+    pick(group, down, up, qc.at[rows : 2 * rows, :])
+    gc[rows : 2 * rows, :] = g2[...]
+    pick(group, s10, s11, s1)
+    pick(odd_ref[0], r1, r3, qc.at[0:rows, :])
+    gc[0:rows, :] = g1[...]
+    for t, stat in ((2, s2), (1, s1)):
+        for c in blocks:
+            first = c if t == 2 else 0
+            at = (t - 1) * rows + c
+            raw = mm(k0[first:rows, :], qc[at : at + ROWS, :], NT)
+            grad_prob = mm(v0[first:rows, :], gc[at : at + ROWS, :], NT)
+            lo = lo_ref[t : t + 1, c : c + ROWS]
+            weigh(raw, grad_prob, first, c, False, lo, stat, probs, grad_s, at)
+    dk_ref[...] = ((dk0[...] + mm(grad_s[...], qc[...], NN)) * SCALE).astype(BF16)
+    dv_ref[...] = (dv0[...] + mm(probs[...], gc[...], NN)).astype(BF16)
+
+
+def grads_far_call(odd, me, lo, up, down, r1, r3, g1, g2, stats, dk0, dv0, k, v):
+    rows, cols = k.shape
+    heads = cols // HD
+    tile = pl.BlockSpec((rows, HD), lambda h, odd, me: (0, h))
+    span = REACH * rows
+    vmem = in_vmem(lo, up, down, r1, r3, g1, g2, *stats, dk0, dv0)
+    return pl.pallas_call(
+        grads_far_kernel,
+        name="grads_far",
+        out_shape=(jax.ShapeDtypeStruct((rows, cols), BF16),) * 2,
+        grid_spec=pltpu.PrefetchScalarGridSpec(
+            num_scalar_prefetch=2,
+            grid=(heads,),
+            in_specs=[RESIDENT] * len(vmem) + [tile] * 2,
+            out_specs=(tile, tile),
+            scratch_shapes=[pltpu.VMEM((span, HD), BF16)] * 2
+            + [pltpu.VMEM((2, rows), F32)] * 2
+            + [pltpu.VMEM((rows, span), BF16)] * 2,
+        ),
+        compiler_params=pltpu.CompilerParams(vmem_limit_bytes=VMEM_BYTES),
+        cost_estimate=pl.CostEstimate(
+            flops=8 * heads * rows * span * HD, bytes_accessed=8 << 20,
             transcendentals=heads * rows * span,
         ),
-    )(
-        odd, me, *in_vmem(lo, prob, factor, att),
-        hbm[0], vmem[0], hbm[1], vmem[1], hbm[2], vmem[2], *vmem[3:], *in_vmem(*stats),
-    )
+    )(odd, me, *vmem, *in_hbm(k, v))
 
 
 def layer(queries, key_rows, value_rows, out_weight, cotangent, offsets):
@@ -458,11 +502,12 @@
     down = ringed(down, 2, 0)
     r1 = exchanged(side)
     v2 = along(value_rows, 2)
+    g_near = grad_out_call(me, out_weight, (0, 1), (cotangent, cot_near), (), F32)
     cot_both = across(cot_far, 1)
     values = in_hbm(value_rows)
     r2 = exchanged(*payload_call(odd, me, ((0, 0, 1, 2),), *values, *in_vmem(up, down)))
 
-    g = grad_out_call(me, (cotangent, cot_near, cot_far, cot_both), out_weight)
+    g = grad_out_call(me, out_weight, (2, 3), (cot_far, cot_both), (g_near,), BF16)
     g2 = along(g, -2)
     bounds = jnp.stack([base, count * rows]).astype(jnp.int32)
     lo_col, lo_row = windows_call(bounds, offsets, rows)
@@ -475,13 +520,17 @@
     attended, factor, stat, sent, kept, kept_far = attend_call(
         odd, me, r2, r3, g, scored, out_weight
     )
-    stats = [stat] + [ringed(stat, n, bit) for n in (1, 2) for bit in (0, 1)]
+    stats = [ringed(stat, n, bit) for n in (1, 2) for bit in (0, 1)]
     came = across(sent, 1)
     far = across((kept_far + came[:, cols:].astype(F32)).astype(BF16), 2)
 
-    grad_queries, grad_keys, grad_values = grads_call(
-        odd, me, lo_row, scored[0], factor, attended, (key_rows, up), (value_rows, v2), (queries, down),
-        (r1, r2, r3), (g, g1, g2), stats,
+    grad_queries, own_keys, own_values = grads_own_call(
+        odd, me, lo_row, scored[0], factor, attended, stat, up, down, v2, (r1, r2, r3), g,
+        key_rows, value_rows, queries,
+    )
+    grad_keys, grad_values = grads_far_call(
+        odd, me, lo_row, up, down, r1, r3, g1, g2, stats, own_keys, own_values,
+        key_rows, value_rows,
     )
     mixed = (kept + came[:, :cols].astype(F32) + far.astype(F32)).astype(BF16)
     return (mixed, grad_queries, grad_keys, grad_values)

time: 90.4 us -> 92.4 us (1.022)
  waiting for transfers between devices: 32.9 us -> 27.4 us
  Pallas kernels: 36.5 us -> 41.2 us
  local copies, waits for them, and re-layouts: 0.01 us -> 1.79 us
    pallas_call x2 -> x4, Pallas kernels: 12.5 us -> 15.6 us  [the longest x1 6.05 us: grads_own_call(): pl.pallas_call(grads_own_kernel, name='grads_own', out_shape=(jax.ShapeDt...]
    ppermute x6, waiting for transfers between devices: 11.8 us -> 9.12 us  [ringed(): return lax.ppermute(shard, ('ctx', 'head'), pairs)]
    ppermute x9, waiting for transfers between devices: 8.46 us -> 6.13 us  [swapped(): return lax.ppermute(shard, axis, [(i, i ^ bit) for i in range(length)])]
    unnamed x4 -> x10, local copies, waits for them, and re-layouts: 0.01 us -> 1.79 us
    pallas_call x1, Pallas kernels: 2.64 us -> 3.63 us  [attend_call(): pl.pallas_call(attend_kernel, name='attend', out_shape=(jax.ShapeDtypeStr...]
  transfers between devices with their start and end apart: 17 -> 17, of which waited for: 7 -> 6; matrix products, arithmetic and copies ran while one was open for 0% -> 0% of each run, Pallas kernels for 38% -> 41%
where the time goes in v5:
time: 92.4 us; the launch traced here: 91.8 us
  Pallas kernels  41.2 us (45%)
  waiting for transfers between devices  27.4 us (30%)
  starting transfers between devices  19.3 us (21%)
  local copies, waits for them, and re-layouts  1.79 us (2%)
  other arithmetic  1.17 us (1%)
    pallas_call x5, Pallas kernels, payload_call(): pl.pallas_call(functools.partial(payload_kernel, table, len(arrays)), nam...  15.9 us
    ppermute x2, waiting for transfers between devices, passed_along(): return lax.ppermute(shard, axis, pairs)  12.2 us
    ppermute x6, waiting for transfers between devices, ringed(): return lax.ppermute(shard, ('ctx', 'head'), pairs)  9.12 us
    ppermute x9, starting transfers between devices, swapped(): return lax.ppermute(shard, axis, [(i, i ^ bit) for i in range(length)])  8.58 us
    ppermute x9, waiting for transfers between devices, swapped(): return lax.ppermute(shard, axis, [(i, i ^ bit) for i in range(length)])  6.13 us
    pallas_call x1, Pallas kernels, grads_own_call(): pl.pallas_call(grads_own_kernel, name='grads_own', out_shape=(jax.ShapeDt...  6.05 us
    pallas_call x1, Pallas kernels, grads_far_call(): pl.pallas_call(grads_far_kernel, name='grads_far', out_shape=(jax.ShapeDt...  5.73 us
    ppermute x6, starting transfers between devices, ringed(): return lax.ppermute(shard, ('ctx', 'head'), pairs)  5.52 us
  transfers between devices with their start and end apart: 17, of which 6 were waited for; matrix products, arithmetic and copies ran while one was open for 0% of the time, Pallas kernels for 41%

profile of v5, /device:TPU:0, one launch (start us, length us, event | category | flops | bytes accessed | tf_op | source)
XLA Modules:
  0.0 91.8 jit_solution(12777778882788568422)
XLA Ops:
  0.7 3.0 %collective-permute-start.5 = (bf16[384,512]{1,0:T(8,128)(2,1)}, bf16[384,512]{1,0:T(8,128)(2,1)}, u32[]{:S(2)}, u32[]{:S(2)}) collective-permute-start(bf16[384,512]{1,0:T(8,128)(2,1)} %refs_0_.5), channel_id=1, source_target_pairs={{0,2},{1,3},{2,0},{3,1},{4,6},{5,7},{6,4},{7,5},{8,10},{9,11},{10,... | collective-permute-start | bytes 1179656 | tf_op jit(solution)/shard_map/ppermute | solution.py:36
  3.7 1.1 %payload.5 = (bf16[384,512]{1,0:T(8,128)(2,1)S(1)}, bf16[384,512]{1,0:T(8,128)(2,1)S(1)}) custom-call(s32[1]{0:T(128)} %bitcast.odd_ref, s32[1]{0:T(128)} %bitcast.1.me_ref, bf16[384,512]{1,0:T(8,128)(2,1)} %k0.5, bf16[384,512]{1,0:T(8,128)(2,1)} %q0.1), custom_call_target="tpu_custom_call" | custom-call | bytes 1572864 | tf_op jit(solution)/shard_map/payload/pallas_call | solution.py:110
  4.8 1.6 %collective-permute-start = (bf16[384,512]{1,0:T(8,128)(2,1)S(1)}, bf16[384,512]{1,0:T(8,128)(2,1)S(1)}, u32[]{:S(2)}, u32[]{:S(2)}) collective-permute-start(bf16[384,512]{1,0:T(8,128)(2,1)S(1)} %get-tuple-element.23.refs_0_), channel_id=1, source_target_pairs={{0,8},{1,0},{2,10},{3,2},{4,12},{5,4},{6,14},{7,6},{8,16},{9,1},{1... | collective-permute-start | bytes 1179656 | tf_op jit(solution)/shard_map/ppermute | solution.py:493
  6.4 3.9 %collective-permute-start.3 = (bf16[384,512]{1,0:T(8,128)(2,1)}, bf16[384,512]{1,0:T(8,128)(2,1)S(1)}, u32[]{:S(2)}, u32[]{:S(2)}) collective-permute-start(bf16[384,512]{1,0:T(8,128)(2,1)} %v0.5), channel_id=1, source_target_pairs={{0,8},{4,12},{8,16},{12,20},{16,24},{20,28},{1,9},{5,13},{9,17},{1... | collective-permute-start | bytes 1179656 | tf_op jit(solution)/shard_map/ppermute | solution.py:31
  10.4 2.7 %collective-permute-done.5.refs_0_ = bf16[384,512]{1,0:T(8,128)(2,1)} collective-permute-done((bf16[384,512]{1,0:T(8,128)(2,1)}, bf16[384,512]{1,0:T(8,128)(2,1)}, u32[]{:S(2)}, u32[]{:S(2)}) %collective-permute-start.5) | collective-permute-done | bytes 393248 | tf_op jit(solution)/shard_map/ppermute | solution.py:36
  13.1 0.8 payload.8
  13.9 2.0 %collective-permute-done.refs_1_.refs_0_.up = bf16[384,512]{1,0:T(8,128)(2,1)S(1)} collective-permute-done((bf16[384,512]{1,0:T(8,128)(2,1)S(1)}, bf16[384,512]{1,0:T(8,128)(2,1)S(1)}, u32[]{:S(2)}, u32[]{:S(2)}) %collective-permute-start) | collective-permute-done | bytes 393248 | tf_op jit(solution)/shard_map/ppermute | solution.py:493
  15.9 1.5 %collective-permute-start.8 = (bf16[384,512]{1,0:T(8,128)(2,1)}, bf16[384,512]{1,0:T(8,128)(2,1)}, u32[]{:S(2)}, u32[]{:S(2)}) collective-permute-start(bf16[384,512]{1,0:T(8,128)(2,1)} %payload.8), channel_id=1, source_target_pairs={{0,4},{4,0},{8,12},{12,8},{16,20},{20,16},{24,28},{28,24},{1,5},{5... | collective-permute-start | bytes 1179656 | tf_op jit(solution)/shard_map/ppermute | solution.py:36
  17.4 13.0 %payload.6 = bf16[384,512]{1,0:T(8,128)(2,1)} custom-call(s32[1]{0:T(128)} %bitcast.odd_ref, s32[1]{0:T(128)} %bitcast.1.me_ref, bf16[384,512]{1,0:T(8,128)(2,1)} %v0.5, bf16[384,512]{1,0:T(8,128)(2,1)S(1)} %collective-permute-done.refs_1_.refs_0_.up, bf16[384,512]{1,0:T(8,128)(2,1)S(1)} %collective-permute-done.1.refs_2_.refs_1_.down), custom_call_target="tpu_custom_call" | custom-call | bytes 786432 | tf_op jit(solution)/shard_map/payload/pallas_call | solution.py:110
  30.6 0.8 payload.7
  31.3 0.7 copy-done.1
  32.1 2.0 %collective-permute-start.4 = (bf16[384,512]{1,0:T(8,128)(2,1)}, bf16[384,512]{1,0:T(8,128)(2,1)S(1)}, u32[]{:S(2)}, u32[]{:S(2)}) collective-permute-start(bf16[384,512]{1,0:T(8,128)(2,1)} %payload.7), channel_id=1, source_target_pairs={{0,4},{4,0},{8,12},{12,8},{16,20},{20,16},{24,28},{28,24},{1,5},{5... | collective-permute-start | bytes 1179656 | tf_op jit(solution)/shard_map/ppermute | solution.py:36
  34.2 1.0 %windows.1 = (s32[384,128]{1,0:T(8,128)S(1)}, s32[3,384]{1,0:T(4,128)S(1)}) custom-call(s32[2]{0:T(128)S(1)} %pad_add_fusion.base_ref, s32[136]{0:T(256)S(1)} %copy-done.4), custom_call_target="tpu_custom_call" | custom-call | flops 1048576 | bytes 262144 | tf_op jit(solution)/shard_map/windows/pallas_call | solution.py:66
  35.2 1.0 %copy-done.3 = bf16[384,512]{1,0:T(8,128)(2,1)S(1)} copy-done((bf16[384,512]{1,0:T(8,128)(2,1)S(1)}, bf16[384,512]{1,0:T(8,128)(2,1)}, u32[]{:S(2)}) %copy-start.3) | copy-done | bytes 393240
  36.2 1.8 %shard_map.93.refs_2_ = f32[384,512]{1,0:T(8,128)S(1)} custom-call(s32[1]{0:T(128)} %bitcast.1.me_ref, bf16[512,2048]{1,0:T(8,128)(2,1)S(1)} %copy-done, bf16[384,512]{1,0:T(8,128)(2,1)S(1)} %copy-done.3, bf16[384,512]{1,0:T(8,128)(2,1)} %collective-permute-done.7.refs_1_), custom_call_target="tpu_custom_call" | custom-call | flops 402653184 | bytes 3145728 | tf_op jit(solution)/shard_map/pallas_call | solution.py:140
  38.1 2.0 %shard_map.94.g.g0.refs_1_ = bf16[384,512]{1,0:T(8,128)(2,1)S(1)} custom-call(s32[1]{0:T(128)} %bitcast.1.me_ref, bf16[512,2048]{1,0:T(8,128)(2,1)S(1)} %copy-done, bf16[384,512]{1,0:T(8,128)(2,1)} %collective-permute-done.5.refs_0_, bf16[384,512]{1,0:T(8,128)(2,1)} %collective-permute-done.6.refs_1_, f32[384,512]{1,0:T(8,128)S(1)} %shard_map.93.refs_2_), custom_call_target="tpu_custom_call" | custom-call | flops 402653184 | bytes 3145728 | tf_op jit(solution)/shard_map/pallas_call | solution.py:140
  40.1 2.8 %collective-permute-done.2.r2 = bf16[384,512]{1,0:T(8,128)(2,1)} collective-permute-done((bf16[384,512]{1,0:T(8,128)(2,1)}, bf16[384,512]{1,0:T(8,128)(2,1)}, u32[]{:S(2)}, u32[]{:S(2)}) %collective-permute-start.2) | collective-permute-done | bytes 393248 | tf_op jit(solution)/shard_map/ppermute | solution.py:36
  42.8 5.2 %near.1 = (bf16[4,384,1152]{2,1,0:T(8,128)(2,1)S(1)}, f32[384,512]{1,0:T(8,128)S(1)}, f32[384,512]{1,0:T(8,128)S(1)}, f32[384,512]{1,0:T(8,128)S(1)}) custom-call(s32[1]{0:T(128)} %bitcast.odd_ref, s32[1]{0:T(128)} %bitcast.1.me_ref, s32[384,128]{1,0:T(8,128)S(1)} %get-tuple-element.25.lo_ref, bf16[384,512]{1,0:T(8,128)(2,1)} %q0.1, bf16[384,512]{1,0:T(8,128)(2,1)} %k0.5, ...), custom_call_target="tpu_custom_call" | custom-call | flops 1811939328 | bytes 10485760 | tf_op jit(solution)/shard_map/near/pallas_call | solution.py:219
  48.0 0.7 collective-permute-done.4.r3
  48.7 3.6 %attend.1 = (bf16[384,512]{1,0:T(8,128)(2,1)S(1)}, f32[384,512]{1,0:T(8,128)S(1)}, f32[4,2,384]{2,1,0:T(2,128)S(1)}, bf16[384,1024]{1,0:T(8,128)(2,1)S(1)}, f32[...) custom-call(s32[1]{0:T(128)} %bitcast.odd_ref, s32[1]{0:T(128)} %bitcast.1.me_ref, ...), custom_call_target="tpu_custom_call" | custom-call | flops 603979776 | bytes 12582912 | tf_op jit(solution)/shard_map/attend/pallas_call | solution.py:282
  52.4 1.3 %collective-permute-start.11 = (bf16[384,512]{1,0:T(8,128)(2,1)S(1)}, bf16[384,512]{1,0:T(8,128)(2,1)S(1)}, u32[]{:S(2)}, u32[]{:S(2)}) collective-permute-start(bf16[384,512]{1,0:T(8,128)(2,1)S(1)} %shard_map.94.g.g0.refs_1_), channel_id=1, source_target_pairs={{8,0},{12,4},{16,8},{20,12},{24,16},{28,20},{9,1},{13,5},{17,9},{2... | collective-permute-start | bytes 1179656 | tf_op jit(solution)/shard_map/ppermute | solution.py:31
  53.7 12.2 %collective-permute-done.11.refs_0_.g2 = bf16[384,512]{1,0:T(8,128)(2,1)S(1)} collective-permute-done((bf16[384,512]{1,0:T(8,128)(2,1)S(1)}, bf16[384,512]{1,0:T(8,128)(2,1)S(1)}, u32[]{:S(2)}, u32[]{:S(2)}) %collective-permute-start.11) | collective-permute-done | bytes 393248 | tf_op jit(solution)/shard_map/ppermute | solution.py:31
  65.9 0.2 payload.9
  66.1 0.3 collective-permute-start.12
  66.4 0.2 add_convert_fusion.1
  66.5 1.6 %collective-permute-start.10 = (bf16[384,512]{1,0:T(8,128)(2,1)S(1)}, bf16[384,512]{1,0:T(8,128)(2,1)S(1)}, u32[]{:S(2)}, u32[]{:S(2)}) collective-permute-start(bf16[384,512]{1,0:T(8,128)(2,1)S(1)} %add_convert_fusion.1), channel_id=1, source_target_pairs={{0,2},{1,3},{2,0},{3,1},{4,6},{5,7},{6,4},{7,5},{8,10},{9,11},{10,... | collective-permute-start | bytes 1179656 | tf_op jit(solution)/shard_map/ppermute | solution.py:36
  68.1 2.0 %collective-permute-start.14 = (f32[4,2,384]{2,1,0:T(2,128)S(1)}, f32[4,2,384]{2,1,0:T(2,128)S(1)}, u32[]{:S(2)}, u32[]{:S(2)}) collective-permute-start(f32[4,2,384]{2,1,0:T(2,128)S(1)} %get-tuple-element.36.stat), channel_id=1, source_target_pairs={{0,4},{1,0},{2,6},{3,2},{4,8},{5,1},{6,10},{7,3},{8,12},{9,5},{10,... | collective-permute-start | bytes 36872 | tf_op jit(solution)/shard_map/ppermute | solution.py:493
  70.1 7.1 %collective-permute-done.13.s10 = f32[4,2,384]{2,1,0:T(2,128)S(1)} collective-permute-done((f32[4,2,384]{2,1,0:T(2,128)S(1)}, f32[4,2,384]{2,1,0:T(2,128)S(1)}, u32[]{:S(2)}, u32[]{:S(2)}) %collective-permute-start.13) | collective-permute-done | bytes 12320 | tf_op jit(solution)/shard_map/ppermute | solution.py:493
  77.2 1.9 %collective-permute-start.16 = (f32[4,2,384]{2,1,0:T(2,128)S(1)}, f32[4,2,384]{2,1,0:T(2,128)S(1)}, u32[]{:S(2)}, u32[]{:S(2)}) collective-permute-start(f32[4,2,384]{2,1,0:T(2,128)S(1)} %get-tuple-element.36.stat), channel_id=1, source_target_pairs={{0,8},{1,0},{2,10},{3,2},{4,12},{5,4},{6,14},{7,6},{8,16},{9,1},{1... | collective-permute-start | bytes 36872 | tf_op jit(solution)/shard_map/ppermute | solution.py:493
  79.1 6.0 %grads_own.1 = (bf16[384,512]{1,0:T(8,128)(2,1)}, f32[384,512]{1,0:T(8,128)S(1)}, f32[384,512]{1,0:T(8,128)S(1)}) custom-call(s32[1]{0:T(128)} %bitcast.odd_ref, s32[1]{0:T(128)} %bitcast.1.me_ref, s32[3,384]{1,0:T(4,128)S(1)} %get-tuple-element.33.lo_ref, bf16[4,384,1152]{2,1,0:T(8,128)(2,1)S(1)} %get-tuple-element.26.prob_ref, ...), custom_call_target="tpu_custom_call" | custom-call | flops 1811939328 | bytes 10485760 | tf_op jit(solution)/shard_map/grads_own/pallas_call | solution.py:377
  85.2 5.7 %grads_far.1 = (bf16[384,512]{1,0:T(8,128)(2,1)}, bf16[384,512]{1,0:T(8,128)(2,1)}) custom-call(s32[1]{0:T(128)} %bitcast.odd_ref, s32[1]{0:T(128)} %bitcast.1.me_ref, s32[3,384]{1,0:T(4,128)S(1)} %get-tuple-element.33.lo_ref, bf16[384,512]{1,0:T(8,128)(2,1)S(1)} %collective-permute-done.refs_1_.refs_0_.up, ...), custom_call_target="tpu_custom_call" | custom-call | flops 1207959552 | bytes 8388608 | tf_op jit(solution)/shard_map/grads_far/pallas_call | solution.py:447
  90.9 0.9 %add_convert_fusion = bf16[384,512]{1,0:T(8,128)(2,1)} fusion(bf16[384,512]{1,0:T(8,128)(2,1)S(1)} %collective-permute-done.10, f32[384,512]{1,0:T(8,128)S(1)} %get-tuple-element.30, bf16[384,1024]{1,0:T(8,128)(2,1)S(1)} %collective-permute-done.9), kind=kLoop, calls=%fused_computation | loop fusion | flops 983040 | bytes 1966080 | tf_op jit(solution)/shard_map/convert_element_type | solution.py:535
  (27 shorter events, 0.4 us)
Async XLA Ops:
  0.6 33.5 %copy-start.4 = (s32[136]{0:T(256)S(1)}, s32[136]{0:T(256)}, u32[]{:S(2)}) copy-start(s32[136]{0:T(256)} %offsets_ref.1) | copy-start | bytes 1636
  0.6 34.5 %copy-start = (bf16[512,2048]{1,0:T(8,128)(2,1)S(1)}, bf16[512,2048]{1,0:T(8,128)(2,1)}, u32[]{:S(2)}) copy-start(bf16[512,2048]{1,0:T(8,128)(2,1)} %w_ref.5) | copy-start | bytes 6291460
  0.7 12.5 %collective-permute-start.5 = (bf16[384,512]{1,0:T(8,128)(2,1)}, bf16[384,512]{1,0:T(8,128)(2,1)}, u32[]{:S(2)}, u32[]{:S(2)}) collective-permute-start(bf16[384,512]{1,0:T(8,128)(2,1)} %refs_0_.5), channel_id=1, source_target_pairs={{0,2},{1,3},{2,0},{3,1},{4,6},{5,7},{6,4},{7,5},{8,10},{9,11},{10,... | collective-permute-start | bytes 1179656 | tf_op jit(solution)/shard_map/ppermute | solution.py:36
  4.8 11.1 %collective-permute-start = (bf16[384,512]{1,0:T(8,128)(2,1)S(1)}, bf16[384,512]{1,0:T(8,128)(2,1)S(1)}, u32[]{:S(2)}, u32[]{:S(2)}) collective-permute-start(bf16[384,512]{1,0:T(8,128)(2,1)S(1)} %get-tuple-element.23.refs_0_), channel_id=1, source_target_pairs={{0,8},{1,0},{2,10},{3,2},{4,12},{5,4},{6,14},{7,6},{8,16},{9,1},{1... | collective-permute-start | bytes 1179656 | tf_op jit(solution)/shard_map/ppermute | solution.py:493
  6.4 11.0 %collective-permute-start.1 = (bf16[384,512]{1,0:T(8,128)(2,1)S(1)}, bf16[384,512]{1,0:T(8,128)(2,1)S(1)}, u32[]{:S(2)}, u32[]{:S(2)}) collective-permute-start(bf16[384,512]{1,0:T(8,128)(2,1)S(1)} %get-tuple-element.24.refs_1_), channel_id=1, source_target_pairs={{0,1},{1,9},{2,3},{3,11},{4,5},{5,13},{6,7},{7,15},{8,0},{9,17},{1... | collective-permute-start | bytes 1179656 | tf_op jit(solution)/shard_map/ppermute | solution.py:493
  6.4 24.1 %collective-permute-start.3 = (bf16[384,512]{1,0:T(8,128)(2,1)}, bf16[384,512]{1,0:T(8,128)(2,1)S(1)}, u32[]{:S(2)}, u32[]{:S(2)}) collective-permute-start(bf16[384,512]{1,0:T(8,128)(2,1)} %v0.5), channel_id=1, source_target_pairs={{0,8},{4,12},{8,16},{12,20},{16,24},{20,28},{1,9},{5,13},{9,17},{1... | collective-permute-start | bytes 1179656 | tf_op jit(solution)/shard_map/ppermute | solution.py:31
  10.4 24.8 %collective-permute-start.7 = (bf16[384,512]{1,0:T(8,128)(2,1)}, bf16[384,512]{1,0:T(8,128)(2,1)}, u32[]{:S(2)}, u32[]{:S(2)}) collective-permute-start(bf16[384,512]{1,0:T(8,128)(2,1)} %refs_0_.5), channel_id=1, source_target_pairs={{0,1},{1,0},{2,3},{3,2},{4,5},{5,4},{6,7},{7,6},{8,9},{9,8},{10,11... | collective-permute-start | bytes 1179656 | tf_op jit(solution)/shard_map/ppermute | solution.py:36
  13.1 25.0 %collective-permute-start.6 = (bf16[384,512]{1,0:T(8,128)(2,1)}, bf16[384,512]{1,0:T(8,128)(2,1)}, u32[]{:S(2)}, u32[]{:S(2)}) collective-permute-start(bf16[384,512]{1,0:T(8,128)(2,1)} %collective-permute-done.5.refs_0_), channel_id=1, source_target_pairs={{0,1},{1,0},{2,3},{3,2},{4,5},{5,4},{6,7},{7,6},{8,9},{9,8},{10,11... | collective-permute-start | bytes 1179656 | tf_op jit(solution)/shard_map/ppermute | solution.py:36
  15.9 24.2 %collective-permute-start.8 = (bf16[384,512]{1,0:T(8,128)(2,1)}, bf16[384,512]{1,0:T(8,128)(2,1)}, u32[]{:S(2)}, u32[]{:S(2)}) collective-permute-start(bf16[384,512]{1,0:T(8,128)(2,1)} %payload.8), channel_id=1, source_target_pairs={{0,4},{4,0},{8,12},{12,8},{16,20},{20,16},{24,28},{28,24},{1,5},{5... | collective-permute-start | bytes 1179656 | tf_op jit(solution)/shard_map/ppermute | solution.py:36
  30.5 12.4 %collective-permute-start.2 = (bf16[384,512]{1,0:T(8,128)(2,1)}, bf16[384,512]{1,0:T(8,128)(2,1)}, u32[]{:S(2)}, u32[]{:S(2)}) collective-permute-start(bf16[384,512]{1,0:T(8,128)(2,1)} %payload.6), channel_id=1, source_target_pairs={{0,4},{4,0},{8,12},{12,8},{16,20},{20,16},{24,28},{28,24},{1,5},{5... | collective-permute-start | bytes 1179656 | tf_op jit(solution)/shard_map/ppermute | solution.py:36
  31.3 0.7 copy-start.1
  32.1 16.6 %collective-permute-start.4 = (bf16[384,512]{1,0:T(8,128)(2,1)}, bf16[384,512]{1,0:T(8,128)(2,1)S(1)}, u32[]{:S(2)}, u32[]{:S(2)}) collective-permute-start(bf16[384,512]{1,0:T(8,128)(2,1)} %payload.7), channel_id=1, source_target_pairs={{0,4},{4,0},{8,12},{12,8},{16,20},{20,16},{24,28},{28,24},{1,5},{5... | collective-permute-start | bytes 1179656 | tf_op jit(solution)/shard_map/ppermute | solution.py:36
  35.1 7.7 %copy-start.2 = (bf16[384,512]{1,0:T(8,128)(2,1)S(1)}, bf16[384,512]{1,0:T(8,128)(2,1)}, u32[]{:S(2)}) copy-start(bf16[384,512]{1,0:T(8,128)(2,1)} %copy-done.1) | copy-start | bytes 1179652
  35.2 1.0 %copy-start.3 = (bf16[384,512]{1,0:T(8,128)(2,1)S(1)}, bf16[384,512]{1,0:T(8,128)(2,1)}, u32[]{:S(2)}) copy-start(bf16[384,512]{1,0:T(8,128)(2,1)} %refs_0_.5) | copy-start | bytes 1179652
  52.3 14.0 %collective-permute-start.9 = (bf16[384,1024]{1,0:T(8,128)(2,1)S(1)}, bf16[384,1024]{1,0:T(8,128)(2,1)S(1)}, u32[]{:S(2)}, u32[]{:S(2)}) collective-permute-start(bf16[384,1024]{1,0:T(8,128)(2,1)S(1)} %get-tuple-element.31), channel_id=1, source_target_pairs={{0,1},{1,0},{2,3},{3,2},{4,5},{5,4},{6,7},{7,6},{8,9},{9,8},{10,11... | collective-permute-start | bytes 2359304 | tf_op jit(solution)/shard_map/ppermute | solution.py:36
  52.4 13.5 %collective-permute-start.11 = (bf16[384,512]{1,0:T(8,128)(2,1)S(1)}, bf16[384,512]{1,0:T(8,128)(2,1)S(1)}, u32[]{:S(2)}, u32[]{:S(2)}) collective-permute-start(bf16[384,512]{1,0:T(8,128)(2,1)S(1)} %shard_map.94.g.g0.refs_1_), channel_id=1, source_target_pairs={{8,0},{12,4},{16,8},{20,12},{24,16},{28,20},{9,1},{13,5},{17,9},{2... | collective-permute-start | bytes 1179656 | tf_op jit(solution)/shard_map/ppermute | solution.py:31
  66.1 19.0 %collective-permute-start.12 = (bf16[384,512]{1,0:T(8,128)(2,1)S(1)}, bf16[384,512]{1,0:T(8,128)(2,1)S(1)}, u32[]{:S(2)}, u32[]{:S(2)}) collective-permute-start(bf16[384,512]{1,0:T(8,128)(2,1)S(1)} %payload.9), channel_id=1, source_target_pairs={{0,4},{4,0},{8,12},{12,8},{16,20},{20,16},{24,28},{28,24},{1,5},{5... | collective-permute-start | bytes 1179656 | tf_op jit(solution)/shard_map/ppermute | solution.py:36
  66.5 24.4 %collective-permute-start.10 = (bf16[384,512]{1,0:T(8,128)(2,1)S(1)}, bf16[384,512]{1,0:T(8,128)(2,1)S(1)}, u32[]{:S(2)}, u32[]{:S(2)}) collective-permute-start(bf16[384,512]{1,0:T(8,128)(2,1)S(1)} %add_convert_fusion.1), channel_id=1, source_target_pairs={{0,2},{1,3},{2,0},{3,1},{4,6},{5,7},{6,4},{7,5},{8,10},{9,11},{10,... | collective-permute-start | bytes 1179656 | tf_op jit(solution)/shard_map/ppermute | solution.py:36
  68.1 9.1 %collective-permute-start.13 = (f32[4,2,384]{2,1,0:T(2,128)S(1)}, f32[4,2,384]{2,1,0:T(2,128)S(1)}, u32[]{:S(2)}, u32[]{:S(2)}) collective-permute-start(f32[4,2,384]{2,1,0:T(2,128)S(1)} %get-tuple-element.36.stat), channel_id=1, source_target_pairs={{0,1},{1,5},{2,3},{3,7},{4,0},{5,9},{6,2},{7,11},{8,4},{9,13},{10,... | collective-permute-start | bytes 36872 | tf_op jit(solution)/shard_map/ppermute | solution.py:493
  68.1 17.1 %collective-permute-start.14 = (f32[4,2,384]{2,1,0:T(2,128)S(1)}, f32[4,2,384]{2,1,0:T(2,128)S(1)}, u32[]{:S(2)}, u32[]{:S(2)}) collective-permute-start(f32[4,2,384]{2,1,0:T(2,128)S(1)} %get-tuple-element.36.stat), channel_id=1, source_target_pairs={{0,4},{1,0},{2,6},{3,2},{4,8},{5,1},{6,10},{7,3},{8,12},{9,5},{10,... | collective-permute-start | bytes 36872 | tf_op jit(solution)/shard_map/ppermute | solution.py:493
  70.1 15.0 %collective-permute-start.15 = (f32[4,2,384]{2,1,0:T(2,128)S(1)}, f32[4,2,384]{2,1,0:T(2,128)S(1)}, u32[]{:S(2)}, u32[]{:S(2)}) collective-permute-start(f32[4,2,384]{2,1,0:T(2,128)S(1)} %get-tuple-element.36.stat), channel_id=1, source_target_pairs={{0,1},{1,9},{2,3},{3,11},{4,5},{5,13},{6,7},{7,15},{8,0},{9,17},{1... | collective-permute-start | bytes 36872 | tf_op jit(solution)/shard_map/ppermute | solution.py:493
  77.2 8.0 %collective-permute-start.16 = (f32[4,2,384]{2,1,0:T(2,128)S(1)}, f32[4,2,384]{2,1,0:T(2,128)S(1)}, u32[]{:S(2)}, u32[]{:S(2)}) collective-permute-start(f32[4,2,384]{2,1,0:T(2,128)S(1)} %get-tuple-element.36.stat), channel_id=1, source_target_pairs={{0,8},{1,0},{2,10},{3,2},{4,12},{5,4},{6,14},{7,6},{8,16},{9,1},{1... | collective-permute-start | bytes 36872 | tf_op jit(solution)/shard_map/ppermute | solution.py:493
